TPU v7x, 32 devices: a whole 2x2x4 slice. The times are simulated.
32 devices in a mesh: section: 2 (over core), dp: 4 (over z), tensor: 4 (over y, x).
Axes of the slice: x: 2, y: 2, z: 4, core: 2. Of those that a mesh axis runs over, the one named last changes fastest.
Arguments:
- boundary: bfloat16 [2, 8, 1024, 1024], P('section', 'dp', 'tensor'), may hold values from -6 to 6
- seg_ids: int32 [8, 1024], P('dp'), may hold values from 0 to 3, never falling along the last dimension, each value on 1 to 512 neighbouring positions
- ln1_gain: bfloat16 [2, 1024], P('section'), may hold values from 0.5 to 1.5
- ln1_bias: bfloat16 [2, 1024], P('section'), may hold values from -3 to 3
- w_qkv: bfloat16 [2, 1024, 16, 192], P('section', None, 'tensor'), may hold values from -0.1875 to 0.1875
- b_qkv: bfloat16 [2, 16, 192], P('section', 'tensor'), may hold values from -4 to 4
- w_out: bfloat16 [2, 16, 64, 1024], P('section', 'tensor'), may hold values from -1.5 to 1.5
- b_out: bfloat16 [2, 1024], P('section'), may hold values from -4 to 4
- ln2_gain: bfloat16 [2, 1024], P('section'), may hold values from 0.5 to 1.5
- ln2_bias: bfloat16 [2, 1024], P('section'), may hold values from -3 to 3
- w_up: bfloat16 [2, 1024, 4096], P('section', None, 'tensor'), may hold values from -0.1875 to 0.1875
- b_up: bfloat16 [2, 4096], P('section', 'tensor'), may hold values from -4 to 4
- w_down: bfloat16 [2, 4096, 1024], P('section', 'tensor'), may hold values from -0.09375 to 0.09375
- b_down: bfloat16 [2, 1024], P('section'), may hold values from -4 to 4
- prefix_embed: bfloat16 [10, 1024], replicated, may hold values from -6 to 6
- reparam_w1: bfloat16 [1024, 512], replicated, may hold values from -0.1875 to 0.1875
- reparam_b1: bfloat16 [512], replicated, may hold values from -4 to 4
- reparam_w2: bfloat16 [512, 2, 16, 128], P(None, 'section', 'tensor'), may hold values from -0.375 to 0.375
- reparam_b2: bfloat16 [2, 16, 128], P('section', 'tensor'), may hold values from -4 to 4
Outputs:
- boundary_out: bfloat16 [2, 8, 1024, 1024], P('section', 'dp', 'tensor')
- embed_grad: float32 [10, 1024], replicated
- w1_grad: float32 [1024, 512], replicated
- b1_grad: float32 [512], replicated
- w2_grad: float32 [512, 2, 16, 128], P(None, 'section', 'tensor')
- b2_grad: float32 [2, 16, 128], P('section', 'tensor')
All inputs are finite; a program needn't handle non-finite values.
Results may differ from a plain program's by a relative error of at most 0.02.
Values may be sent and summed in bfloat16 or wider, within the bound.
No kernel may reach another device: no remote copies, remote signals or barrier semaphores. Data moves between devices by JAX's collectives and lax.ppermute only.
A program may use at most 192 MiB of HBM per device.

v0:
```python
import jax
import jax.numpy as jnp
from jax import lax
from jax.sharding import PartitionSpec as P

epsilon = 1e-05
masked_value = -1e30


def passed_along(value, axis, steps):
    count = lax.axis_size(axis)
    leading, last = (max(0, -steps), min(count, count - steps))
    return lax.ppermute(value, axis, [(source, source + steps) for source in range(leading, last)])


def layer_norm(values, ln_gain, ln_bias):
    row_mean = jnp.mean(values, axis=-1, keepdims=True)
    centered = values - row_mean
    row_var = jnp.mean(centered * centered, axis=-1, keepdims=True)
    return centered * lax.rsqrt(row_var + epsilon) * ln_gain + ln_bias


def norm_back(values, ln_gain, ln_bias, grad_normed):
    pullback = jax.vjp(lambda inner_values: layer_norm(inner_values, ln_gain, ln_bias), values)[1]
    return pullback(grad_normed)[0]


def gelu_tanh(values):
    return jax.nn.gelu(values, approximate=True)


def gelu_back(values, grad_values):
    return jax.vjp(gelu_tanh, values)[1](grad_values)[0]


def row_mask(seg_row, start_row, block_rows):
    seg_query = seg_row[start_row : start_row + block_rows]
    query_pos = start_row + jnp.arange(block_rows)
    key_pos = jnp.arange(seg_row.shape[0])
    return (seg_query[:, None] == seg_row[None, :]) & (key_pos[None, :] <= query_pos[:, None])


def block_scores(query_block, key_rows, prefix_keys, allowed, scaling):
    main_scores = (
        jnp.einsum("bhd,khd->hbk", query_block, key_rows, preferred_element_type=jnp.float32)
        * scaling
    )
    main_scores = jnp.where(allowed[None], main_scores, masked_value)
    prefix_scores = (
        jnp.einsum("bhd,phd->hbp", query_block, prefix_keys, preferred_element_type=jnp.float32)
        * scaling
    )
    return (main_scores, prefix_scores)


def attention_forward(queries, key_rows, value_rows, prefix_keys, prefix_values, seg_row):
    seq_len = queries.shape[0]
    block_rows = min(512, seq_len)
    scaling = queries.shape[-1] ** (-0.5)
    contexts = []
    log_sums = []
    for start_row in range(0, seq_len, block_rows):
        query_block = queries[start_row : start_row + block_rows]
        allowed = row_mask(seg_row, start_row, block_rows)
        main_scores, prefix_scores = block_scores(
            query_block, key_rows, prefix_keys, allowed, scaling
        )
        row_max = jnp.maximum(jnp.max(main_scores, axis=-1), jnp.max(prefix_scores, axis=-1))
        main_exp = jnp.exp(main_scores - row_max[..., None])
        prefix_exp = jnp.exp(prefix_scores - row_max[..., None])
        row_sum = jnp.sum(main_exp, axis=-1) + jnp.sum(prefix_exp, axis=-1)
        main_prob = (main_exp / row_sum[..., None]).astype(jnp.bfloat16)
        prefix_prob = (prefix_exp / row_sum[..., None]).astype(jnp.bfloat16)
        context = jnp.einsum(
            "hbk,khd->bhd", main_prob, value_rows, preferred_element_type=jnp.float32
        )
        context = context + jnp.einsum(
            "hbp,phd->bhd", prefix_prob, prefix_values, preferred_element_type=jnp.float32
        )
        contexts.append(context)
        log_sums.append(row_max + jnp.log(row_sum))
    return (jnp.concatenate(contexts, axis=0), jnp.concatenate(log_sums, axis=1))


def attention_backward(
    queries, key_rows, value_rows, prefix_keys, prefix_values, seg_row, log_sums, grad_context
):
    seq_len = queries.shape[0]
    block_rows = min(512, seq_len)
    scaling = queries.shape[-1] ** (-0.5)
    grad_keys = jnp.zeros(key_rows.shape, jnp.float32)
    grad_values = jnp.zeros(value_rows.shape, jnp.float32)
    grad_prefix_keys = jnp.zeros(prefix_keys.shape, jnp.float32)
    grad_prefix_values = jnp.zeros(prefix_values.shape, jnp.float32)
    grad_queries = []
    for start_row in range(0, seq_len, block_rows):
        query_block = queries[start_row : start_row + block_rows]
        grad_block = grad_context[start_row : start_row + block_rows]
        block_lse = log_sums[:, start_row : start_row + block_rows]
        allowed = row_mask(seg_row, start_row, block_rows)
        main_scores, prefix_scores = block_scores(
            query_block, key_rows, prefix_keys, allowed, scaling
        )
        main_prob = jnp.exp(main_scores - block_lse[..., None])
        prefix_prob = jnp.exp(prefix_scores - block_lse[..., None])
        main_dp = jnp.einsum(
            "bhd,khd->hbk", grad_block, value_rows, preferred_element_type=jnp.float32
        )
        prefix_dp = jnp.einsum(
            "bhd,phd->hbp", grad_block, prefix_values, preferred_element_type=jnp.float32
        )
        row_delta = jnp.sum(main_prob * main_dp, axis=-1) + jnp.sum(
            prefix_prob * prefix_dp, axis=-1
        )
        main_ds = (main_prob * (main_dp - row_delta[..., None])).astype(jnp.bfloat16)
        prefix_ds = (prefix_prob * (prefix_dp - row_delta[..., None])).astype(jnp.bfloat16)
        grad_query = jnp.einsum(
            "hbk,khd->bhd", main_ds, key_rows, preferred_element_type=jnp.float32
        )
        grad_query = grad_query + jnp.einsum(
            "hbp,phd->bhd", prefix_ds, prefix_keys, preferred_element_type=jnp.float32
        )
        grad_queries.append(grad_query * scaling)
        grad_keys = (
            grad_keys
            + jnp.einsum("hbk,bhd->khd", main_ds, query_block, preferred_element_type=jnp.float32)
            * scaling
        )
        grad_values = grad_values + jnp.einsum(
            "hbk,bhd->khd",
            main_prob.astype(jnp.bfloat16),
            grad_block,
            preferred_element_type=jnp.float32,
        )
        grad_prefix_keys = (
            grad_prefix_keys
            + jnp.einsum("hbp,bhd->phd", prefix_ds, query_block, preferred_element_type=jnp.float32)
            * scaling
        )
        grad_prefix_values = grad_prefix_values + jnp.einsum(
            "hbp,bhd->phd",
            prefix_prob.astype(jnp.bfloat16),
            grad_block,
            preferred_element_type=jnp.float32,
        )
    return (
        jnp.concatenate(grad_queries, axis=0),
        grad_keys,
        grad_values,
        grad_prefix_keys,
        grad_prefix_values,
    )


def layer_forward(inputs, seg_row, params, prefix_keys, prefix_values):
    (
        ln1_gain,
        ln1_bias,
        qkv_weight,
        qkv_bias,
        out_weight,
        out_bias,
        ln2_gain,
        ln2_bias,
        up_weight,
        up_bias,
        down_weight,
        down_bias,
    ) = params
    heads_local = prefix_keys.shape[1]
    head_dim = prefix_keys.shape[2]
    normed = layer_norm(inputs, ln1_gain, ln1_bias).astype(jnp.bfloat16)
    packed = (
        jnp.dot(
            lax.all_gather(normed, "tensor", axis=0, tiled=True),
            qkv_weight,
            preferred_element_type=jnp.float32,
        )
        + qkv_bias
    ).astype(jnp.bfloat16)
    seq_len = packed.shape[0]
    split_heads = packed.reshape(seq_len, heads_local, 3, head_dim)
    context, log_sums = attention_forward(
        split_heads[:, :, 0],
        split_heads[:, :, 1],
        split_heads[:, :, 2],
        prefix_keys,
        prefix_values,
        seg_row,
    )
    context_flat = context.astype(jnp.bfloat16).reshape(seq_len, heads_local * head_dim)
    attn_sum = lax.psum_scatter(
        jnp.dot(context_flat, out_weight, preferred_element_type=jnp.float32).astype(jnp.bfloat16),
        "tensor",
        scatter_dimension=0,
        tiled=True,
    ).astype(jnp.float32)
    middle = inputs + (attn_sum + out_bias)
    normed_two = layer_norm(middle, ln2_gain, ln2_bias).astype(jnp.bfloat16)
    hidden_pre = (
        jnp.dot(
            lax.all_gather(normed_two, "tensor", axis=0, tiled=True),
            up_weight,
            preferred_element_type=jnp.float32,
        )
        + up_bias
    )
    hidden = gelu_tanh(hidden_pre).astype(jnp.bfloat16)
    ffn_sum = lax.psum_scatter(
        jnp.dot(hidden, down_weight, preferred_element_type=jnp.float32).astype(jnp.bfloat16),
        "tensor",
        scatter_dimension=0,
        tiled=True,
    ).astype(jnp.float32)
    output = middle + (ffn_sum + down_bias)
    return (output, (inputs, middle, packed, log_sums, hidden_pre))


def layer_backward(seg_row, params, prefix_keys, prefix_values, kept_state, grad_out):
    (
        ln1_gain,
        ln1_bias,
        qkv_weight,
        qkv_bias,
        out_weight,
        out_bias,
        ln2_gain,
        ln2_bias,
        up_weight,
        up_bias,
        down_weight,
        down_bias,
    ) = params
    inputs, middle, packed, log_sums, hidden_pre = kept_state
    tok_rows = inputs.shape[0]
    heads_local = prefix_keys.shape[1]
    head_dim = prefix_keys.shape[2]
    grad_branch = grad_out.astype(jnp.bfloat16)
    grad_hidden = jnp.einsum(
        "td,fd->tf",
        lax.all_gather(grad_branch, "tensor", axis=0, tiled=True),
        down_weight,
        preferred_element_type=jnp.float32,
    )
    grad_hidden_pre = gelu_back(hidden_pre, grad_hidden).astype(jnp.bfloat16)
    grad_normed_two = lax.psum_scatter(
        jnp.einsum(
            "tf,df->td",
            lax.slice_in_dim(grad_hidden_pre, 0, tok_rows * lax.axis_size("tensor"), axis=0),
            up_weight,
            preferred_element_type=jnp.float32,
        ).astype(jnp.bfloat16),
        "tensor",
        scatter_dimension=0,
        tiled=True,
    ).astype(jnp.float32)
    grad_middle = grad_out + norm_back(middle, ln2_gain, ln2_bias, grad_normed_two)
    grad_attn = grad_middle.astype(jnp.bfloat16)
    grad_context = jnp.einsum(
        "td,jd->tj",
        lax.all_gather(grad_attn, "tensor", axis=0, tiled=True),
        out_weight,
        preferred_element_type=jnp.float32,
    ).astype(jnp.bfloat16)
    seq_len = packed.shape[0]
    grad_context = grad_context.reshape(seq_len, heads_local, head_dim)
    split_heads = packed.reshape(seq_len, heads_local, 3, head_dim)
    grad_queries, grad_keys, grad_values, grad_prefix_keys, grad_prefix_values = attention_backward(
        split_heads[:, :, 0],
        split_heads[:, :, 1],
        split_heads[:, :, 2],
        prefix_keys,
        prefix_values,
        seg_row,
        log_sums,
        grad_context,
    )
    grad_packed = (
        jnp.stack([grad_queries, grad_keys, grad_values], axis=2)
        .astype(jnp.bfloat16)
        .reshape(seq_len, heads_local * 3 * head_dim)
    )
    grad_normed = lax.psum_scatter(
        jnp.einsum(
            "tj,dj->td",
            lax.slice_in_dim(grad_packed, 0, tok_rows * lax.axis_size("tensor"), axis=0),
            qkv_weight,
            preferred_element_type=jnp.float32,
        ).astype(jnp.bfloat16),
        "tensor",
        scatter_dimension=0,
        tiled=True,
    ).astype(jnp.float32)
    grad_in = grad_middle + norm_back(inputs, ln1_gain, ln1_bias, grad_normed)
    return (grad_in, jnp.stack([grad_prefix_keys, grad_prefix_values], axis=2))


def local(
    boundary,
    seg_ids,
    ln1_gain,
    ln1_bias,
    w_qkv,
    b_qkv,
    w_out,
    b_out,
    ln2_gain,
    ln2_bias,
    w_up,
    b_up,
    w_down,
    b_down,
    prefix_embed,
    reparam_w1,
    reparam_b1,
    reparam_w2,
    reparam_b2,
):
    section_index = lax.axis_index("section")
    row_total = boundary.shape[1]
    tok_rows = boundary.shape[2]
    width = boundary.shape[3]
    heads_local = w_qkv.shape[2]
    head_dim = w_qkv.shape[3] // 3
    prefix_len = prefix_embed.shape[0]
    params = (
        ln1_gain[0].astype(jnp.float32),
        ln1_bias[0].astype(jnp.float32),
        w_qkv[0].reshape(width, heads_local * 3 * head_dim),
        b_qkv[0].reshape(heads_local * 3 * head_dim).astype(jnp.float32),
        w_out[0].reshape(heads_local * head_dim, width),
        b_out[0].astype(jnp.float32),
        ln2_gain[0].astype(jnp.float32),
        ln2_bias[0].astype(jnp.float32),
        w_up[0],
        b_up[0].astype(jnp.float32),
        w_down[0],
        b_down[0].astype(jnp.float32),
    )
    prefix_pre = jnp.dot(
        prefix_embed, reparam_w1, preferred_element_type=jnp.float32
    ) + reparam_b1.astype(jnp.float32)
    prefix_hidden = jnp.tanh(prefix_pre)
    hidden_low = prefix_hidden.astype(jnp.bfloat16)
    w2_flat = reparam_w2.reshape(reparam_w2.shape[0], heads_local * 2 * head_dim)
    prefix_flat = jnp.dot(
        hidden_low, w2_flat, preferred_element_type=jnp.float32
    ) + reparam_b2.reshape(heads_local * 2 * head_dim).astype(jnp.float32)
    prefix_split = prefix_flat.astype(jnp.bfloat16).reshape(prefix_len, heads_local, 2, head_dim)
    prefix_keys = prefix_split[:, :, 0]
    prefix_values = prefix_split[:, :, 1]
    own_rows = boundary[0]

    def forward_step(sent_rows, counter):
        received = passed_along(sent_rows, "section", 1)
        row_index = jnp.clip(counter - section_index, 0, row_total - 1)
        own_row = lax.dynamic_index_in_dim(own_rows, jnp.minimum(counter, row_total - 1), 0, False)
        inputs = jnp.where(section_index == 0, own_row, received).astype(jnp.float32)
        seg_row = lax.dynamic_index_in_dim(seg_ids, row_index, 0, False)
        output, kept_state = layer_forward(inputs, seg_row, params, prefix_keys, prefix_values)
        output_low = output.astype(jnp.bfloat16)
        return (output_low, (output_low, kept_state))

    first_sent = jnp.zeros((tok_rows, width), jnp.bfloat16)
    final_sent, (outputs_all, kept_all) = lax.scan(
        forward_step, first_sent, jnp.arange(row_total + 1)
    )

    def backward_step(carry_value, counter):
        sent_rows, grad_prefix = carry_value
        received = passed_along(sent_rows, "section", -1)
        row_index = counter - 1 + section_index
        is_valid = (row_index >= 0) & (row_index < row_total)
        safe_row = jnp.clip(row_index, 0, row_total - 1)
        own_row = lax.dynamic_index_in_dim(own_rows, jnp.minimum(counter, row_total - 1), 0, False)
        grad_out = jnp.where(section_index == 1, own_row, received).astype(jnp.float32)
        kept_index = safe_row + section_index
        kept_state = jax.tree.map(
            lambda stacked: lax.dynamic_index_in_dim(stacked, kept_index, 0, False), kept_all
        )
        seg_row = lax.dynamic_index_in_dim(seg_ids, safe_row, 0, False)
        grad_in, grad_pairs = layer_backward(
            seg_row, params, prefix_keys, prefix_values, kept_state, grad_out
        )
        grad_prefix = grad_prefix + jnp.where(is_valid, grad_pairs, 0.0)
        grad_low = grad_in.astype(jnp.bfloat16)
        return ((grad_low, grad_prefix), grad_low)

    first_grads = (
        jnp.zeros((tok_rows, width), jnp.bfloat16),
        jnp.zeros((prefix_len, heads_local, 2, head_dim), jnp.float32),
    )
    (final_grad, grad_prefix), grads_all = lax.scan(
        backward_step, first_grads, jnp.arange(row_total + 1)
    )
    boundary_result = jnp.where(section_index == 0, grads_all[1:], outputs_all[1:])[None]
    grad_prefix_total = lax.psum(grad_prefix, "dp")
    grad_flat = grad_prefix_total.reshape(prefix_len, heads_local * 2 * head_dim).astype(
        jnp.bfloat16
    )
    w2_grad = jnp.einsum(
        "pr,pc->rc", hidden_low, grad_flat, preferred_element_type=jnp.float32
    ).reshape(reparam_w2.shape)
    b2_grad = jnp.sum(grad_flat.astype(jnp.float32), axis=0).reshape(reparam_b2.shape)
    hidden_part = jnp.einsum("pc,rc->pr", grad_flat, w2_flat, preferred_element_type=jnp.float32)
    hidden_grad = lax.psum(hidden_part, ("section", "tensor"))
    pre_grad = jax.vjp(jnp.tanh, prefix_pre)[1](hidden_grad)[0].astype(jnp.bfloat16)
    w1_grad = jnp.einsum("pd,pr->dr", prefix_embed, pre_grad, preferred_element_type=jnp.float32)
    b1_grad = jnp.sum(pre_grad.astype(jnp.float32), axis=0)
    embed_grad = jnp.einsum("pr,dr->pd", pre_grad, reparam_w1, preferred_element_type=jnp.float32)
    return (boundary_result, embed_grad, w1_grad, b1_grad, w2_grad, b2_grad)


def solution(mesh):
    return jax.shard_map(
        local,
        mesh=mesh,
        in_specs=(
            P("section", "dp", "tensor", None),
            P("dp", None),
            P("section", None),
            P("section", None),
            P("section", None, "tensor", None),
            P("section", "tensor", None),
            P("section", "tensor", None, None),
            P("section", None),
            P("section", None),
            P("section", None),
            P("section", None, "tensor"),
            P("section", "tensor"),
            P("section", "tensor", None),
            P("section", None),
            P(),
            P(),
            P(),
            P(None, "section", "tensor", None),
            P("section", "tensor", None),
        ),
        out_specs=(
            P("section", "dp", "tensor", None),
            P(),
            P(),
            P(),
            P(None, "section", "tensor", None),
            P("section", "tensor", None),
        ),
        check_vma=False,
    )
```

profile of v0, /device:TPU:1, one launch (start us, length us, event | category | flops | bytes accessed | tf_op | source)
XLA Modules:
  0.0 1305.9 jit_solution(1190346601542746473)
XLA Ops:
  15.7 570.0 %while.41 = (s32[]{:T(128)}, bf16[256,1024]{1,0:T(8,128)(2,1)}, bf16[3,256,1024]{2,1,0:T(8,128)(2,1)}, f32[3,256,1024]{2,1,0:T(8,128)}, f32[3,256,1024]{2,1,0:T(...) while((s32[]{:T(128)}, bf16[256,1024]{1,0:T(8,128)(2,1)}, ...), condition=%wide.region_15.16_spmd.clone, body=%wide.region_0.15_spmd.clone.sunk | while | flops 7609803776 | bytes 152481968 | solution.py:365
  25.4 35.0 %all-gather.5.cloned.1.call-done = bf16[1024,1024]{1,0:T(8,128)(2,1)} async-done(((bf16[256,1024]{1,0:T(8,128)(2,1)}), bf16[1024,1024]{1,0:T(8,128)(2,1)}) %all-gather.5.cloned.1.call-update) | async-done | bytes 2097168 | tf_op jit(solution)/shard_map/while/body/eval_jaxpr/all_gather | solution.py:175
  82.3 35.3 %reduce-scatter.5.cloned.1.call-done = bf16[256,1024]{1,0:T(8,128)(2,1)} async-done(((bf16[1024,1024]{1,0:T(8,128)(2,1)}), bf16[256,1024]{1,0:T(8,128)(2,1)}) %reduce-scatter.5.cloned.1.call-update) | async-done | bytes 524304 | tf_op jit(solution)/shard_map/while/body/eval_jaxpr/reduce_scatter | solution.py:192
  122.5 35.4 %all-gather.7.cloned.1.call-done = bf16[1024,1024]{1,0:T(8,128)(2,1)} async-done(((bf16[256,1024]{1,0:T(8,128)(2,1)}), bf16[1024,1024]{1,0:T(8,128)(2,1)}) %all-gather.7.cloned.1.call-update) | async-done | bytes 2097168 | tf_op jit(solution)/shard_map/while/body/eval_jaxpr/all_gather | solution.py:202
  170.5 33.6 %reduce-scatter.7.cloned.1.call-done = bf16[256,1024]{1,0:T(8,128)(2,1)} async-done(((bf16[1024,1024]{1,0:T(8,128)(2,1)}), bf16[256,1024]{1,0:T(8,128)(2,1)}) %reduce-scatter.7.cloned.1.call-update) | async-done | bytes 524304 | tf_op jit(solution)/shard_map/while/body/eval_jaxpr/reduce_scatter | solution.py:209
  217.1 33.0 %all-gather.5.cloned.1.call-done = bf16[1024,1024]{1,0:T(8,128)(2,1)} async-done(((bf16[256,1024]{1,0:T(8,128)(2,1)}), bf16[1024,1024]{1,0:T(8,128)(2,1)}) %all-gather.5.cloned.1.call-update) | async-done | bytes 2097168 | tf_op jit(solution)/shard_map/while/body/eval_jaxpr/all_gather | solution.py:175
  271.9 35.3 %reduce-scatter.5.cloned.1.call-done = bf16[256,1024]{1,0:T(8,128)(2,1)} async-done(((bf16[1024,1024]{1,0:T(8,128)(2,1)}), bf16[256,1024]{1,0:T(8,128)(2,1)}) %reduce-scatter.5.cloned.1.call-update) | async-done | bytes 524304 | tf_op jit(solution)/shard_map/while/body/eval_jaxpr/reduce_scatter | solution.py:192
  312.1 35.4 %all-gather.7.cloned.1.call-done = bf16[1024,1024]{1,0:T(8,128)(2,1)} async-done(((bf16[256,1024]{1,0:T(8,128)(2,1)}), bf16[1024,1024]{1,0:T(8,128)(2,1)}) %all-gather.7.cloned.1.call-update) | async-done | bytes 2097168 | tf_op jit(solution)/shard_map/while/body/eval_jaxpr/all_gather | solution.py:202
  360.1 33.5 %reduce-scatter.7.cloned.1.call-done = bf16[256,1024]{1,0:T(8,128)(2,1)} async-done(((bf16[1024,1024]{1,0:T(8,128)(2,1)}), bf16[256,1024]{1,0:T(8,128)(2,1)}) %reduce-scatter.7.cloned.1.call-update) | async-done | bytes 524304 | tf_op jit(solution)/shard_map/while/body/eval_jaxpr/reduce_scatter | solution.py:209
  406.7 33.0 %all-gather.5.cloned.1.call-done = bf16[1024,1024]{1,0:T(8,128)(2,1)} async-done(((bf16[256,1024]{1,0:T(8,128)(2,1)}), bf16[1024,1024]{1,0:T(8,128)(2,1)}) %all-gather.5.cloned.1.call-update) | async-done | bytes 2097168 | tf_op jit(solution)/shard_map/while/body/eval_jaxpr/all_gather | solution.py:175
  461.6 35.3 %reduce-scatter.5.cloned.1.call-done = bf16[256,1024]{1,0:T(8,128)(2,1)} async-done(((bf16[1024,1024]{1,0:T(8,128)(2,1)}), bf16[256,1024]{1,0:T(8,128)(2,1)}) %reduce-scatter.5.cloned.1.call-update) | async-done | bytes 524304 | tf_op jit(solution)/shard_map/while/body/eval_jaxpr/reduce_scatter | solution.py:192
  501.8 35.4 %all-gather.7.cloned.1.call-done = bf16[1024,1024]{1,0:T(8,128)(2,1)} async-done(((bf16[256,1024]{1,0:T(8,128)(2,1)}), bf16[1024,1024]{1,0:T(8,128)(2,1)}) %all-gather.7.cloned.1.call-update) | async-done | bytes 2097168 | tf_op jit(solution)/shard_map/while/body/eval_jaxpr/all_gather | solution.py:202
  549.8 33.6 %reduce-scatter.7.cloned.1.call-done = bf16[256,1024]{1,0:T(8,128)(2,1)} async-done(((bf16[1024,1024]{1,0:T(8,128)(2,1)}), bf16[256,1024]{1,0:T(8,128)(2,1)}) %reduce-scatter.7.cloned.1.call-update) | async-done | bytes 524304 | tf_op jit(solution)/shard_map/while/body/eval_jaxpr/reduce_scatter | solution.py:209
  587.7 651.4 %while.42 = (s32[]{:T(128)}, bf16[256,1024]{1,0:T(8,128)(2,1)S(1)}, f32[10,4,2,64]{3,0,1,2:T(8,128)}, bf16[3,256,1024]{2,1,0:T(8,128)(2,1)}, pred[]{:T(512)}, /*...) while((s32[]{:T(128)}, bf16[256,1024]{1,0:T(8,128)(2,1)S(1)}, ...), condition=%wide.region_31.32_spmd.clone, body=%wide.region_16.31_spmd.clone.sunk | while | flops 9260854272 | bytes 304395840 | solution.py:393
  612.5 34.2 %all-gather.9.cloned.1.call-done = bf16[1024,1024]{1,0:T(8,128)(2,1)} async-done(((bf16[256,1024]{1,0:T(8,128)(2,1)}), bf16[1024,1024]{1,0:T(8,128)(2,1)}) %all-gather.9.cloned.1.call-update) | async-done | bytes 2097168 | tf_op jit(solution)/shard_map/while/body/eval_jaxpr/all_gather | solution.py:241
  659.1 33.9 %reduce-scatter.9.cloned.1.call-done = bf16[256,1024]{1,0:T(8,128)(2,1)} async-done(((bf16[1024,1024]{1,0:T(8,128)(2,1)}), bf16[256,1024]{1,0:T(8,128)(2,1)}) %reduce-scatter.9.cloned.1.call-update) | async-done | bytes 524304 | tf_op jit(solution)/shard_map/while/body/eval_jaxpr/reduce_scatter | solution.py:246
  780.5 29.3 %reduce-scatter.11.cloned.1.call-done = bf16[256,1024]{1,0:T(8,128)(2,1)} async-done(((bf16[1024,1024]{1,0:T(8,128)(2,1)}), bf16[256,1024]{1,0:T(8,128)(2,1)}) %reduce-scatter.11.cloned.1.call-update) | async-done | bytes 524304 | tf_op jit(solution)/shard_map/while/body/eval_jaxpr/reduce_scatter | solution.py:283
  823.7 34.2 %all-gather.9.cloned.1.call-done = bf16[1024,1024]{1,0:T(8,128)(2,1)} async-done(((bf16[256,1024]{1,0:T(8,128)(2,1)}), bf16[1024,1024]{1,0:T(8,128)(2,1)}) %all-gather.9.cloned.1.call-update) | async-done | bytes 2097168 | tf_op jit(solution)/shard_map/while/body/eval_jaxpr/all_gather | solution.py:241
  870.3 33.9 %reduce-scatter.9.cloned.1.call-done = bf16[256,1024]{1,0:T(8,128)(2,1)} async-done(((bf16[1024,1024]{1,0:T(8,128)(2,1)}), bf16[256,1024]{1,0:T(8,128)(2,1)}) %reduce-scatter.9.cloned.1.call-update) | async-done | bytes 524304 | tf_op jit(solution)/shard_map/while/body/eval_jaxpr/reduce_scatter | solution.py:246
  992.5 28.5 %reduce-scatter.11.cloned.1.call-done = bf16[256,1024]{1,0:T(8,128)(2,1)} async-done(((bf16[1024,1024]{1,0:T(8,128)(2,1)}), bf16[256,1024]{1,0:T(8,128)(2,1)}) %reduce-scatter.11.cloned.1.call-update) | async-done | bytes 524304 | tf_op jit(solution)/shard_map/while/body/eval_jaxpr/reduce_scatter | solution.py:283
  1035.0 34.2 %all-gather.9.cloned.1.call-done = bf16[1024,1024]{1,0:T(8,128)(2,1)} async-done(((bf16[256,1024]{1,0:T(8,128)(2,1)}), bf16[1024,1024]{1,0:T(8,128)(2,1)}) %all-gather.9.cloned.1.call-update) | async-done | bytes 2097168 | tf_op jit(solution)/shard_map/while/body/eval_jaxpr/all_gather | solution.py:241
  1081.6 33.9 %reduce-scatter.9.cloned.1.call-done = bf16[256,1024]{1,0:T(8,128)(2,1)} async-done(((bf16[1024,1024]{1,0:T(8,128)(2,1)}), bf16[256,1024]{1,0:T(8,128)(2,1)}) %reduce-scatter.9.cloned.1.call-update) | async-done | bytes 524304 | tf_op jit(solution)/shard_map/while/body/eval_jaxpr/reduce_scatter | solution.py:246
  1203.8 28.5 %reduce-scatter.11.cloned.1.call-done = bf16[256,1024]{1,0:T(8,128)(2,1)} async-done(((bf16[1024,1024]{1,0:T(8,128)(2,1)}), bf16[256,1024]{1,0:T(8,128)(2,1)}) %reduce-scatter.11.cloned.1.call-update) | async-done | bytes 524304 | tf_op jit(solution)/shard_map/while/body/eval_jaxpr/reduce_scatter | solution.py:283
  1256.9 31.1 %psum.15 = f32[10,512]{1,0:T(8,128)S(1)} all-reduce(f32[10,512]{1,0:T(8,128)S(1)} %fusion.137), channel_id=1, replica_groups=mesh['section'=2,'dp'=4,'tensor'=4] {'section','tensor'}, use_global_device_ids=true, to_apply=%region_33.34 | all-reduce | flops 5120 | bytes 40960 | tf_op jit(solution)/shard_map/psum | solution.py:406
  (628 shorter events, 527.6 us)
Async XLA Ops:
  15.7 44.7 %all-gather.5.cloned.1.call-start = ((), (), s32[]{:S(2)}) async-start(), calls=%async_computation.4 | async-start | bytes 2621440 | tf_op jit(solution)/shard_map/while/body/eval_jaxpr/all_gather | solution.py:175
  23.4 94.2 %reduce-scatter.5.cloned.1.call-start = ((), (), s32[]{:S(2)}) async-start(), calls=%async_computation.5 | async-start | bytes 2621440 | tf_op jit(solution)/shard_map/while/body/eval_jaxpr/reduce_scatter | solution.py:192
  82.2 75.7 %all-gather.7.cloned.1.call-start = ((), (), s32[]{:S(2)}) async-start(), calls=%async_computation.6 | async-start | bytes 2621440 | tf_op jit(solution)/shard_map/while/body/eval_jaxpr/all_gather | solution.py:202
  122.4 81.7 %reduce-scatter.7.cloned.1.call-start = ((), (), s32[]{:S(2)}) async-start(), calls=%async_computation.7 | async-start | bytes 2621440 | tf_op jit(solution)/shard_map/while/body/eval_jaxpr/reduce_scatter | solution.py:209
  206.4 43.6 %all-gather.5.cloned.1.call-start = ((), (), s32[]{:S(2)}) async-start(), calls=%async_computation.4 | async-start | bytes 2621440 | tf_op jit(solution)/shard_map/while/body/eval_jaxpr/all_gather | solution.py:175
  215.1 92.1 %reduce-scatter.5.cloned.1.call-start = ((), (), s32[]{:S(2)}) async-start(), calls=%async_computation.5 | async-start | bytes 2621440 | tf_op jit(solution)/shard_map/while/body/eval_jaxpr/reduce_scatter | solution.py:192
  271.8 75.7 %all-gather.7.cloned.1.call-start = ((), (), s32[]{:S(2)}) async-start(), calls=%async_computation.6 | async-start | bytes 2621440 | tf_op jit(solution)/shard_map/while/body/eval_jaxpr/all_gather | solution.py:202
  312.0 81.7 %reduce-scatter.7.cloned.1.call-start = ((), (), s32[]{:S(2)}) async-start(), calls=%async_computation.7 | async-start | bytes 2621440 | tf_op jit(solution)/shard_map/while/body/eval_jaxpr/reduce_scatter | solution.py:209
  396.1 43.6 %all-gather.5.cloned.1.call-start = ((), (), s32[]{:S(2)}) async-start(), calls=%async_computation.4 | async-start | bytes 2621440 | tf_op jit(solution)/shard_map/while/body/eval_jaxpr/all_gather | solution.py:175
  404.7 92.2 %reduce-scatter.5.cloned.1.call-start = ((), (), s32[]{:S(2)}) async-start(), calls=%async_computation.5 | async-start | bytes 2621440 | tf_op jit(solution)/shard_map/while/body/eval_jaxpr/reduce_scatter | solution.py:192
  461.5 75.7 %all-gather.7.cloned.1.call-start = ((), (), s32[]{:S(2)}) async-start(), calls=%async_computation.6 | async-start | bytes 2621440 | tf_op jit(solution)/shard_map/while/body/eval_jaxpr/all_gather | solution.py:202
  501.7 81.7 %reduce-scatter.7.cloned.1.call-start = ((), (), s32[]{:S(2)}) async-start(), calls=%async_computation.7 | async-start | bytes 2621440 | tf_op jit(solution)/shard_map/while/body/eval_jaxpr/reduce_scatter | solution.py:209
  605.2 41.5 %all-gather.9.cloned.1.call-start = ((), (), s32[]{:S(2)}) async-start(), calls=%async_computation.8 | async-start | bytes 2621440 | tf_op jit(solution)/shard_map/while/body/eval_jaxpr/all_gather | solution.py:241
  611.8 81.2 %reduce-scatter.9.cloned.1.call-start = ((), (), s32[]{:S(2)}) async-start(), calls=%async_computation.9 | async-start | bytes 2621440 | tf_op jit(solution)/shard_map/while/body/eval_jaxpr/reduce_scatter | solution.py:246
  657.6 76.4 %all-gather.11.cloned.1.call-start = ((), (), s32[]{:S(2)}) async-start(), calls=%async_computation.10 | async-start | bytes 2621440 | tf_op jit(solution)/shard_map/while/body/eval_jaxpr/all_gather | solution.py:261
  698.5 111.2 %reduce-scatter.11.cloned.1.call-start = ((), (), s32[]{:S(2)}) async-start(), calls=%async_computation.11 | async-start | bytes 2621440 | tf_op jit(solution)/shard_map/while/body/eval_jaxpr/reduce_scatter | solution.py:283
  816.4 41.5 %all-gather.9.cloned.1.call-start = ((), (), s32[]{:S(2)}) async-start(), calls=%async_computation.8 | async-start | bytes 2621440 | tf_op jit(solution)/shard_map/while/body/eval_jaxpr/all_gather | solution.py:241
  823.0 81.2 %reduce-scatter.9.cloned.1.call-start = ((), (), s32[]{:S(2)}) async-start(), calls=%async_computation.9 | async-start | bytes 2621440 | tf_op jit(solution)/shard_map/while/body/eval_jaxpr/reduce_scatter | solution.py:246
  868.9 76.4 %all-gather.11.cloned.1.call-start = ((), (), s32[]{:S(2)}) async-start(), calls=%async_computation.10 | async-start | bytes 2621440 | tf_op jit(solution)/shard_map/while/body/eval_jaxpr/all_gather | solution.py:261
  909.8 111.2 %reduce-scatter.11.cloned.1.call-start = ((), (), s32[]{:S(2)}) async-start(), calls=%async_computation.11 | async-start | bytes 2621440 | tf_op jit(solution)/shard_map/while/body/eval_jaxpr/reduce_scatter | solution.py:283
  1027.7 41.5 %all-gather.9.cloned.1.call-start = ((), (), s32[]{:S(2)}) async-start(), calls=%async_computation.8 | async-start | bytes 2621440 | tf_op jit(solution)/shard_map/while/body/eval_jaxpr/all_gather | solution.py:241
  1034.3 81.2 %reduce-scatter.9.cloned.1.call-start = ((), (), s32[]{:S(2)}) async-start(), calls=%async_computation.9 | async-start | bytes 2621440 | tf_op jit(solution)/shard_map/while/body/eval_jaxpr/reduce_scatter | solution.py:246
  1080.1 76.4 %all-gather.11.cloned.1.call-start = ((), (), s32[]{:S(2)}) async-start(), calls=%async_computation.10 | async-start | bytes 2621440 | tf_op jit(solution)/shard_map/while/body/eval_jaxpr/all_gather | solution.py:261
  1121.0 111.2 %reduce-scatter.11.cloned.1.call-start = ((), (), s32[]{:S(2)}) async-start(), calls=%async_computation.11 | async-start | bytes 2621440 | tf_op jit(solution)/shard_map/while/body/eval_jaxpr/reduce_scatter | solution.py:283
  (120 other events, 2514.5 us)
Sparse Core Ops, SparseCore 0:
  23.5 36.8 all-gather.4
  82.3 35.1 reduce-scatter.4
  122.5 35.2 all-gather.6
  168.8 35.1 reduce-scatter.6
  215.2 34.7 all-gather.4
  271.9 35.1 reduce-scatter.4
  312.1 35.2 all-gather.6
  358.4 35.1 reduce-scatter.6
  404.8 34.7 all-gather.4
  461.6 35.1 reduce-scatter.4
  501.8 35.2 all-gather.6
  548.2 35.1 reduce-scatter.6
  611.9 34.7 all-gather.8
  657.7 35.2 reduce-scatter.8
  698.7 35.2 all-gather.10
  774.5 35.1 reduce-scatter.10
  823.1 34.7 all-gather.8
  869.0 35.1 reduce-scatter.8
  909.9 35.2 all-gather.10
  985.7 35.1 reduce-scatter.10
  1034.4 34.7 all-gather.8
  1080.2 35.2 reduce-scatter.8
  1121.2 35.2 all-gather.10
  1197.0 35.1 reduce-scatter.10
where the time goes:
time: 1320 us; the launch traced here: 1310 us
  waiting for transfers between devices  772 us (58%)
  matrix products  250 us (19%)
  other arithmetic  148 us (11%)
  blocking collectives  47.5 us (4%)
  local copies, waits for them, and re-layouts  32.2 us (2%)
  loops' own time  28.1 us (2%)
  between operations  14.7 us (1%)
    all_gather x3, waiting for transfers between devices, layer_forward(): lax.all_gather(normed_two, 'tensor', axis=0, tiled=True)  106 us
    reduce_scatter x3, waiting for transfers between devices, layer_forward(): lax.psum_scatter(jnp.dot(context_flat, out_weight, preferred_element_type...  106 us
    all_gather x3, waiting for transfers between devices, layer_backward(): lax.all_gather(grad_branch, 'tensor', axis=0, tiled=True)  103 us
    reduce_scatter x3, waiting for transfers between devices, layer_backward(): lax.psum_scatter(jnp.einsum('tf,df->td', lax.slice_in_dim(grad_hidden_pre...  102 us
    all_gather x3, waiting for transfers between devices, layer_forward(): lax.all_gather(normed, 'tensor', axis=0, tiled=True)  101 us
    reduce_scatter x3, waiting for transfers between devices, layer_forward(): lax.psum_scatter(jnp.dot(hidden, down_weight, preferred_element_type=jnp....  101 us
    reduce_scatter x3, waiting for transfers between devices, layer_backward(): lax.psum_scatter(jnp.einsum('tj,dj->td', lax.slice_in_dim(grad_packed, 0,...  86.2 us
    all_gather x3, waiting for transfers between devices, layer_backward(): lax.all_gather(grad_attn, 'tensor', axis=0, tiled=True)  63.8 us
  transfers between devices with their start and end apart: 30, of which 27 were waited for; matrix products, arithmetic and copies ran while one was open for 6% of the time, Pallas kernels for 0%

commit v1 on v0

v1 whole, which is shorter than its diff:
```python
import functools

import jax
import jax.numpy as jnp
from jax import lax
from jax.experimental import pallas as pl
from jax.experimental.pallas import tpu as pltpu
from jax.sharding import PartitionSpec as P

epsilon = 1e-05
masked_value = -1e30
max_segment = 512
prefix_rows = 16
stat_rows = 8
f32 = jnp.float32
bf16 = jnp.bfloat16


def dot_nn(a, b):
    return lax.dot_general(a, b, (((1,), (0,)), ((), ())), preferred_element_type=f32)


def dot_nt(a, b):
    return lax.dot_general(a, b, (((1,), (1,)), ((), ())), preferred_element_type=f32)


def key_blocks(index, block_rows):
    reach = -(-(max_segment - 1) // block_rows)
    return list(range(max(0, index - reach), index + 1))


def gather_rows(order_ref, sources, target_ref, block_rows):
    for place in range(2 * len(sources)):
        start = pl.multiple_of(order_ref[place] * block_rows, block_rows)
        target_ref[pl.ds(start, block_rows), :] = sources[place // 2][
            pl.ds((place % 2) * block_rows, block_rows), :
        ]


def scatter_rows(order_ref, source_ref, targets, block_rows, columns):
    for place in range(2 * len(targets)):
        start = pl.multiple_of(order_ref[place] * block_rows, block_rows)
        targets[place // 2][pl.ds((place % 2) * block_rows, block_rows), columns] = source_ref[
            pl.ds(start, block_rows), :
        ].astype(targets[place // 2].dtype)


def segment_column(seg_ref, start, rows):
    row = seg_ref[0:1, start : start + rows]
    return jnp.transpose(jnp.broadcast_to(row, (128, rows)))[:, 0:1]


def attention_forward_kernel(count, block_rows, head_dim, prefix_len, order_ref, *refs):
    packed_refs = refs[:count]
    pairs_ref, seg_ref = refs[count : count + 2]
    context_refs = refs[count + 2 : 2 * count + 2]
    lse_ref, rows_ref, context_ref, bias_ref = refs[2 * count + 2 :]
    width = pairs_ref.shape[2]
    heads = width // head_dim
    blocks = 2 * count
    scaling = head_dim ** (-0.5)
    gather_rows(order_ref, packed_refs, rows_ref, block_rows)
    lane = lax.broadcasted_iota(jnp.int32, (1, width), 1) // head_dim
    stat_lane = lax.broadcasted_iota(jnp.int32, (1, 128), 1)
    prefix_bias = jnp.where(
        lax.broadcasted_iota(jnp.int32, (1, 128), 1) < prefix_len, 0.0, masked_value
    )
    prefix_keys, prefix_values = pairs_ref[0], pairs_ref[1]
    for index in range(blocks):
        start = index * block_rows
        keys = key_blocks(index, block_rows)
        seg_query = segment_column(seg_ref, start, block_rows)
        for slot, key in enumerate(keys):
            same = seg_query == seg_ref[0:1, key * block_rows : (key + 1) * block_rows]
            if key == index:
                shape = (block_rows, block_rows)
                same = same & (
                    lax.broadcasted_iota(jnp.int32, shape, 1)
                    <= lax.broadcasted_iota(jnp.int32, shape, 0)
                )
            bias_ref[slot] = jnp.where(same, 0.0, masked_value)
        queries = rows_ref[pl.ds(start, block_rows), 0:width]

        def one_head(head, carry):
            context_total, stats = carry
            chosen = lane == head
            query = jnp.where(chosen, queries, 0.0) * jnp.asarray(scaling, bf16)
            scores = [
                dot_nt(query, rows_ref[key * block_rows : (key + 1) * block_rows, width : 2 * width])
                + bias_ref[slot]
                for slot, key in enumerate(keys)
            ]
            prefix_scores = dot_nt(query, prefix_keys) + prefix_bias
            row_max = jnp.max(prefix_scores, axis=1, keepdims=True)
            for score in scores:
                row_max = jnp.maximum(row_max, jnp.max(score, axis=1, keepdims=True))
            prefix_exp = jnp.exp(prefix_scores - row_max)
            row_sum = jnp.sum(prefix_exp, axis=1, keepdims=True)
            context = dot_nn(prefix_exp.astype(bf16), prefix_values)
            for score, key in zip(scores, keys):
                exped = jnp.exp(score - row_max)
                row_sum = row_sum + jnp.sum(exped, axis=1, keepdims=True)
                context = context + dot_nn(
                    exped.astype(bf16),
                    rows_ref[key * block_rows : (key + 1) * block_rows, 2 * width :],
                )
            context_total = context_total + jnp.where(chosen, context * (1.0 / row_sum), 0.0)
            stats = jnp.where(stat_lane == head, row_max + jnp.log(row_sum), stats)
            return (context_total, stats)

        context_total, stats = lax.fori_loop(
            0,
            heads,
            one_head,
            (jnp.zeros((block_rows, width), f32), jnp.zeros((block_rows, 128), f32)),
        )
        context_ref[pl.ds(start, block_rows), :] = context_total.astype(bf16)
        lse_ref[:, start : start + block_rows] = jnp.transpose(stats)[0:stat_rows]
    scatter_rows(order_ref, context_ref, context_refs, block_rows, slice(0, width))


def attention_backward_kernel(count, block_rows, head_dim, prefix_len, order_ref, *refs):
    packed_refs = refs[:count]
    grad_refs = refs[count : 2 * count]
    pairs_ref, seg_ref, lse_ref = refs[2 * count : 2 * count + 3]
    out_refs = refs[2 * count + 3 : 3 * count + 3]
    prefix_out = refs[3 * count + 3]
    rows_ref, grad_ref, bias_ref, kt_ref, pkt_ref, dqt_ref, dq_ref, dk_ref, dv_ref = refs[
        3 * count + 4 :
    ]
    width = pairs_ref.shape[2]
    heads = width // head_dim
    blocks = 2 * count
    scaling = head_dim ** (-0.5)
    gather_rows(order_ref, packed_refs, rows_ref, block_rows)
    gather_rows(order_ref, grad_refs, grad_ref, block_rows)
    lane = lax.broadcasted_iota(jnp.int32, (1, width), 1) // head_dim
    prefix_bias = jnp.where(
        lax.broadcasted_iota(jnp.int32, (128, 1), 0) < prefix_len, 0.0, masked_value
    )
    prefix_keys, prefix_values = pairs_ref[0], pairs_ref[1]
    pkt_ref[...] = jnp.transpose(prefix_keys.astype(f32)).astype(bf16)
    dk_ref[...] = jnp.zeros_like(dk_ref)
    dv_ref[...] = jnp.zeros_like(dv_ref)
    prefix_out[...] = jnp.zeros_like(prefix_out)
    for index in range(blocks):
        kt_ref[index] = jnp.transpose(
            rows_ref[index * block_rows : (index + 1) * block_rows, width : 2 * width].astype(f32)
        ).astype(bf16)
    for index in range(blocks):
        start = index * block_rows
        keys = key_blocks(index, block_rows)
        seg_query = seg_ref[0:1, start : start + block_rows]
        for slot, key in enumerate(keys):
            same = segment_column(seg_ref, key * block_rows, block_rows) == seg_query
            if key == index:
                shape = (block_rows, block_rows)
                same = same & (
                    lax.broadcasted_iota(jnp.int32, shape, 0)
                    <= lax.broadcasted_iota(jnp.int32, shape, 1)
                )
            bias_ref[slot] = jnp.where(same, 0.0, masked_value)
        queries = rows_ref[pl.ds(start, block_rows), 0:width]
        grads = grad_ref[pl.ds(start, block_rows), :]

        def one_head(head, carry):
            chosen = lane == head
            query = jnp.where(chosen, queries, 0.0) * jnp.asarray(scaling, bf16)
            grad = jnp.where(chosen, grads, 0.0)
            lse = lse_ref[pl.ds(head, 1), start : start + block_rows]
            span = pl.ds(pl.multiple_of(head * head_dim, head_dim), head_dim)
            prefix_prob = jnp.exp(dot_nt(prefix_keys, query) + prefix_bias - lse)
            prefix_dp = dot_nt(prefix_values, grad)
            delta = jnp.sum(prefix_prob * prefix_dp, axis=0, keepdims=True)
            probs, dps = [], []
            for slot, key in enumerate(keys):
                rows = slice(key * block_rows, (key + 1) * block_rows)
                prob = jnp.exp(
                    dot_nt(rows_ref[rows, width : 2 * width], query) + bias_ref[slot] - lse
                )
                dp = dot_nt(rows_ref[rows, 2 * width :], grad)
                delta = delta + jnp.sum(prob * dp, axis=0, keepdims=True)
                probs.append(prob)
                dps.append(dp)
            prefix_ds = (prefix_prob * (prefix_dp - delta)).astype(bf16)
            prefix_out[0] += dot_nn(prefix_ds, query)
            prefix_out[1] += dot_nn(prefix_prob.astype(bf16), grad)
            dqt = dot_nn(pkt_ref[span, :], prefix_ds)
            for prob, dp, key in zip(probs, dps, keys):
                rows = slice(key * block_rows, (key + 1) * block_rows)
                ds = (prob * (dp - delta)).astype(bf16)
                dk_ref[rows, :] += dot_nn(ds, query)
                dv_ref[rows, :] += dot_nn(prob.astype(bf16), grad)
                dqt = dqt + dot_nn(kt_ref[key, span, :], ds)
            dqt_ref[span, :] = dqt
            return carry

        lax.fori_loop(0, heads, one_head, 0)
        dq_ref[pl.ds(start, block_rows), :] = jnp.transpose(dqt_ref[...]) * scaling
    scatter_rows(order_ref, dq_ref, out_refs, block_rows, slice(0, width))
    scatter_rows(order_ref, dk_ref, out_refs, block_rows, slice(width, 2 * width))
    scatter_rows(order_ref, dv_ref, out_refs, block_rows, slice(2 * width, 3 * width))


def whole(memory_space=pltpu.VMEM):
    return pl.BlockSpec(memory_space=memory_space)


def attention_forward(order, packed, pairs, seg_row, head_dim, prefix_len):
    count = len(packed)
    block_rows = packed[0].shape[0] // 2
    width = packed[0].shape[1] // 3
    seq_len = seg_row.shape[1]
    slots = len(key_blocks(2 * count - 1, block_rows))
    results = pl.pallas_call(
        functools.partial(attention_forward_kernel, count, block_rows, head_dim, prefix_len),
        out_shape=[jax.ShapeDtypeStruct((2 * block_rows, width), bf16)] * count
        + [jax.ShapeDtypeStruct((stat_rows, seq_len), f32)],
        in_specs=[whole(pltpu.SMEM)] + [whole()] * (count + 2),
        out_specs=[whole()] * (count + 1),
        scratch_shapes=[
            pltpu.VMEM((seq_len, 3 * width), bf16),
            pltpu.VMEM((seq_len, width), bf16),
            pltpu.VMEM((slots, block_rows, block_rows), f32),
        ],
        compiler_params=pltpu.CompilerParams(vmem_limit_bytes=32 << 20),
        cost_estimate=pl.CostEstimate(
            flops=8 * seq_len * seq_len * width, bytes_accessed=8 * seq_len * width, transcendentals=0
        ),
        name="attention_forward",
    )(order, *packed, pairs, seg_row)
    return (results[:count], results[count])


def attention_backward(order, packed, grads, pairs, seg_row, lse, head_dim, prefix_len):
    count = len(packed)
    block_rows = packed[0].shape[0] // 2
    width = packed[0].shape[1] // 3
    seq_len = seg_row.shape[1]
    blocks = 2 * count
    slots = len(key_blocks(blocks - 1, block_rows))
    results = pl.pallas_call(
        functools.partial(attention_backward_kernel, count, block_rows, head_dim, prefix_len),
        out_shape=[jax.ShapeDtypeStruct((2 * block_rows, 3 * width), bf16)] * count
        + [jax.ShapeDtypeStruct(pairs.shape, f32)],
        in_specs=[whole(pltpu.SMEM)] + [whole()] * (2 * count + 3),
        out_specs=[whole()] * (count + 1),
        scratch_shapes=[
            pltpu.VMEM((seq_len, 3 * width), bf16),
            pltpu.VMEM((seq_len, width), bf16),
            pltpu.VMEM((slots, block_rows, block_rows), f32),
            pltpu.VMEM((blocks, width, block_rows), bf16),
            pltpu.VMEM((width, pairs.shape[1]), bf16),
            pltpu.VMEM((width, block_rows), f32),
            pltpu.VMEM((seq_len, width), f32),
            pltpu.VMEM((seq_len, width), f32),
            pltpu.VMEM((seq_len, width), f32),
        ],
        compiler_params=pltpu.CompilerParams(vmem_limit_bytes=32 << 20),
        cost_estimate=pl.CostEstimate(
            flops=20 * seq_len * seq_len * width,
            bytes_accessed=20 * seq_len * width,
            transcendentals=0,
        ),
        name="attention_backward",
    )(order, *packed, *grads, pairs, seg_row, lse)
    return (results[:count], results[count])


def centered_values(values):
    centered = values - jnp.mean(values, axis=-1, keepdims=True)
    scale = lax.rsqrt(jnp.mean(centered * centered, axis=-1, keepdims=True) + epsilon)
    return (centered * scale, scale)


def layer_norm(values, ln_gain, ln_bias):
    return centered_values(values)[0] * ln_gain + ln_bias


def norm_back(values, ln_gain, grad_normed):
    unit, scale = centered_values(values)
    entry = grad_normed * ln_gain
    return scale * (
        entry
        - jnp.mean(entry, axis=-1, keepdims=True)
        - unit * jnp.mean(entry * unit, axis=-1, keepdims=True)
    )


def gelu_both(values):
    root = 0.7978845608028654
    inner = root * (values + 0.044715 * values * values * values)
    curve = jnp.tanh(inner)
    slope = root * (1.0 + 3 * 0.044715 * values * values)
    return (
        0.5 * values * (1.0 + curve),
        0.5 * (1.0 + curve) + 0.5 * values * (1.0 - curve * curve) * slope,
    )


class Group:
    def __init__(self, tensor_size):
        self.size = tensor_size
        self.count = tensor_size // 2

    def core_swap(self, value):
        return lax.ppermute(value, "section", [(0, 1), (1, 0)])

    def shift(self, value, distance):
        pairs = [
            (half * self.count + place, half * self.count + (place + distance) % self.count)
            for half in range(2)
            for place in range(self.count)
        ]
        return lax.ppermute(value, "tensor", pairs)

    def from_layer(self, value, layer):
        size, count = self.size, self.count
        pairs = [(layer * size + place, size + (place + count) % size) for place in range(size)]
        return lax.ppermute(value, ("section", "tensor"), pairs)

    def to_layer(self, value, core, layer):
        size, count = self.size, self.count
        pairs = [
            (core * size + place, layer * size + (place + core * count) % size)
            for place in range(size)
        ]
        return lax.ppermute(value, ("section", "tensor"), pairs)

    def down(self, value):
        return lax.ppermute(value, "section", [(1, 0)])

    def up(self, value):
        return lax.ppermute(value, "section", [(0, 1)])

    def gather(self, block):
        arrived = [block] + [self.shift(block, distance) for distance in range(1, self.count)]
        return [jnp.concatenate([part, self.core_swap(part)], axis=0) for part in arrived]

    def scatter(self, parts):
        rows = parts[0].shape[0] // 2
        total = None
        for distance in list(range(1, self.count)) + [0]:
            own, other = (parts[distance][:rows], parts[distance][rows:])
            summed = own.astype(f32) + self.core_swap(other).astype(f32)
            if distance:
                summed = self.shift(summed.astype(bf16), -distance).astype(f32)
            total = summed if total is None else total + summed
        return total


def local(
    boundary,
    seg_ids,
    ln1_gain,
    ln1_bias,
    w_qkv,
    b_qkv,
    w_out,
    b_out,
    ln2_gain,
    ln2_bias,
    w_up,
    b_up,
    w_down,
    b_down,
    prefix_embed,
    reparam_w1,
    reparam_b1,
    reparam_w2,
    reparam_b2,
):
    core = lax.axis_index("section")
    place = lax.axis_index("tensor")
    group = Group(lax.axis_size("tensor"))
    count = group.count
    tok_rows, width = boundary.shape[2:]
    heads_local = w_qkv.shape[2]
    head_dim = w_qkv.shape[3] // 3
    head_width = heads_local * head_dim
    prefix_len = prefix_embed.shape[0]
    row = place // count
    low = core == 0

    prefix_pre = dot_nn(prefix_embed, reparam_w1) + reparam_b1.astype(f32)
    curve = jnp.tanh(prefix_pre)
    hidden_low = curve.astype(bf16)
    w2_own = (
        reparam_w2.reshape(reparam_w2.shape[0], heads_local, 2, head_dim)
        .transpose(0, 2, 1, 3)
        .reshape(reparam_w2.shape[0], 2 * head_width)
    )
    b2_own = (
        reparam_b2.reshape(heads_local, 2, head_dim).transpose(1, 0, 2).reshape(2 * head_width)
    )
    prefix_own = (dot_nn(hidden_low, w2_own) + b2_own.astype(f32)).astype(bf16)

    def as_rows(value):
        value = value.reshape(-1, value.shape[-1])
        return jnp.pad(value, ((0, 0), (0, width - value.shape[1])))

    b_qkv_own = b_qkv.reshape(heads_local, 3, head_dim).transpose(1, 0, 2).reshape(1, 3 * head_width)
    pad_prefix = ((0, prefix_rows - prefix_len), (0, 0))
    small_own = jnp.concatenate(
        [
            as_rows(ln1_gain),
            as_rows(ln1_bias),
            as_rows(b_out),
            as_rows(ln2_gain),
            as_rows(ln2_bias),
            as_rows(b_down),
            as_rows(b_up),
            as_rows(b_qkv_own),
            as_rows(jnp.pad(prefix_own[:, :head_width], pad_prefix)),
            as_rows(jnp.pad(prefix_own[:, head_width:], pad_prefix)),
        ],
        axis=0,
    )
    qkv_own = (
        w_qkv.reshape(width, heads_local, 3, head_dim)
        .transpose(0, 2, 1, 3)
        .reshape(width, 3 * head_width)
    )
    out_own = w_out.reshape(head_width, width)

    def both_layers(value):
        return (
            jnp.where(low, value, group.from_layer(value, 0)),
            jnp.where(low, group.down(value), group.from_layer(value, 1)),
        )

    own_row = lax.dynamic_index_in_dim(boundary[0], row, 0, False)
    other_row = lax.dynamic_index_in_dim(boundary[0], 1 - row, 0, False)
    inputs = jnp.where(low, own_row, group.from_layer(other_row, 0)).astype(f32)
    cotangent = jnp.where(low, group.down(own_row), group.from_layer(other_row, 1))

    small = both_layers(small_own)
    qkv = both_layers(qkv_own)
    outs = both_layers(out_own)
    ups = both_layers(w_up[0])
    downs = both_layers(w_down[0])

    seg_row = lax.dynamic_index_in_dim(seg_ids, row, 0, True).astype(f32)
    chip = place % count
    order = jnp.stack(
        [
            jnp.bitwise_xor(row, jnp.bitwise_xor(core, swapped)) * count
            + (chip - distance + count) % count
            for distance in range(count)
            for swapped in range(2)
        ]
    ).astype(jnp.int32)

    class Layer:
        def __init__(self, index):
            vectors = small[index].astype(f32)
            (
                self.ln1_gain,
                self.ln1_bias,
                self.b_out,
                self.ln2_gain,
                self.ln2_bias,
                self.b_down,
                self.b_up,
                self.b_qkv,
            ) = [vectors[at : at + 1] for at in range(8)]
            self.b_up = self.b_up[:, : ups[index].shape[1]]
            self.b_qkv = self.b_qkv[:, : 3 * head_width]
            pairs = small[index][8 : 8 + 2 * prefix_rows, :head_width].reshape(
                2, prefix_rows, head_width
            )
            self.pairs = jnp.pad(pairs, ((0, 0), (0, 128 - prefix_rows), (0, 0)))
            self.qkv, self.out, self.up, self.down = (
                qkv[index],
                outs[index],
                ups[index],
                downs[index],
            )

        def forward(self, inputs):
            self.inputs = inputs
            normed = layer_norm(inputs, self.ln1_gain, self.ln1_bias).astype(bf16)
            self.packed = [
                (dot_nn(part, self.qkv) + self.b_qkv).astype(bf16) for part in group.gather(normed)
            ]
            context, self.lse = attention_forward(
                order, self.packed, self.pairs, seg_row, head_dim, prefix_len
            )
            attn = group.scatter([dot_nn(part, self.out).astype(bf16) for part in context])
            self.middle = inputs + (attn + self.b_out)
            normed_two = layer_norm(self.middle, self.ln2_gain, self.ln2_bias).astype(bf16)
            self.slopes = []
            parts = []
            for part in group.gather(normed_two):
                hidden, slope = gelu_both(dot_nn(part, self.up) + self.b_up)
                self.slopes.append(slope)
                parts.append(dot_nn(hidden.astype(bf16), self.down).astype(bf16))
            return self.middle + (group.scatter(parts) + self.b_down)

        def backward(self, grad_out):
            parts = []
            for part, slope in zip(group.gather(grad_out.astype(bf16)), self.slopes):
                grad_pre = (dot_nt(part, self.down) * slope).astype(bf16)
                parts.append(dot_nt(grad_pre, self.up).astype(bf16))
            grad_middle = grad_out + norm_back(self.middle, self.ln2_gain, group.scatter(parts))
            grads = [
                dot_nt(part, self.out).astype(bf16)
                for part in group.gather(grad_middle.astype(bf16))
            ]
            grad_packed, grad_pairs = attention_backward(
                order, self.packed, grads, self.pairs, seg_row, self.lse, head_dim, prefix_len
            )
            grad_normed = group.scatter(
                [dot_nt(part, self.qkv).astype(bf16) for part in grad_packed]
            )
            grad_in = grad_middle + norm_back(self.inputs, self.ln1_gain, grad_normed)
            return (grad_in, grad_pairs[:, :prefix_rows])

    layers = (Layer(0), Layer(1))
    first_out = layers[0].forward(inputs).astype(bf16)
    last_out = layers[1].forward(first_out.astype(f32)).astype(bf16)
    mid_grad, grad_pairs_one = layers[1].backward(cotangent.astype(f32))
    first_grad, grad_pairs_zero = layers[0].backward(mid_grad.astype(bf16).astype(f32))
    first_grad = first_grad.astype(bf16)

    own_result = jnp.where(low, first_grad, group.up(last_out))
    other_result = jnp.where(
        low, group.to_layer(first_grad, 1, 0), group.to_layer(last_out, 1, 1)
    )
    boundary_result = jnp.where(
        row == 0, jnp.stack([own_result, other_result]), jnp.stack([other_result, own_result])
    )[None]

    grad_prefix = jnp.where(
        low,
        grad_pairs_zero + group.to_layer(grad_pairs_zero, 1, 0),
        group.up(grad_pairs_one) + group.to_layer(grad_pairs_one, 1, 1),
    )
    grad_low = lax.psum(grad_prefix, "dp")[:, :prefix_len].astype(bf16)
    grad_flat = jnp.concatenate([grad_low[0], grad_low[1]], axis=1)
    w2_grad = (
        lax.dot_general(
            hidden_low, grad_flat, (((0,), (0,)), ((), ())), preferred_element_type=f32
        )
        .reshape(reparam_w2.shape[0], 2, heads_local, head_dim)
        .transpose(0, 2, 1, 3)
        .reshape(reparam_w2.shape)
    )
    b2_grad = (
        jnp.sum(grad_flat.astype(f32), axis=0)
        .reshape(2, heads_local, head_dim)
        .transpose(1, 0, 2)
        .reshape(reparam_b2.shape)
    )
    hidden_grad = lax.psum(dot_nt(grad_flat, w2_own), ("section", "tensor"))
    pre_grad = (hidden_grad * (1.0 - curve * curve)).astype(bf16)
    w1_grad = lax.dot_general(
        prefix_embed, pre_grad, (((0,), (0,)), ((), ())), preferred_element_type=f32
    )
    b1_grad = jnp.sum(pre_grad.astype(f32), axis=0)
    embed_grad = dot_nt(pre_grad, reparam_w1)
    return (boundary_result, embed_grad, w1_grad, b1_grad, w2_grad, b2_grad)


def solution(mesh):
    return jax.shard_map(
        local,
        mesh=mesh,
        in_specs=(
            P("section", "dp", "tensor", None),
            P("dp", None),
            P("section", None),
            P("section", None),
            P("section", None, "tensor", None),
            P("section", "tensor", None),
            P("section", "tensor", None, None),
            P("section", None),
            P("section", None),
            P("section", None),
            P("section", None, "tensor"),
            P("section", "tensor"),
            P("section", "tensor", None),
            P("section", None),
            P(),
            P(),
            P(),
            P(None, "section", "tensor", None),
            P("section", "tensor", None),
        ),
        out_specs=(
            P("section", "dp", "tensor", None),
            P(),
            P(),
            P(),
            P(None, "section", "tensor", None),
            P("section", "tensor", None),
        ),
        check_vma=False,
    )
```

time: 1320 us -> 522 us (0.40)
  waiting for transfers between devices: 772 us -> 186 us
  matrix products: 250 us -> 62 us
  other arithmetic: 148 us -> 34.3 us
  starting transfers between devices: 12.6 us -> 93.5 us
  Pallas kernels: 0 us -> 62 us
  loops' own time: 28.1 us -> 0 us
    reduce_scatter x12 -> x0, waiting for transfers between devices: 395 us -> none  [the longest x3 106 us: layer_forward(): lax.psum_scatter(jnp.dot(context_flat, out_weight, preferred_element_type...]
    all_gather x12 -> x0, waiting for transfers between devices: 374 us -> none  [the longest x3 106 us: layer_forward(): lax.all_gather(normed_two, 'tensor', axis=0, tiled=True)]
    dot_general x111 -> x34, matrix products: 250 us -> 62 us  [the longest x14 37.3 us: dot_nt(): lax.dot_general(a, b, (((1,), (1,)), ((), ())), preferred_element_type=f32)]
    ppermute x6 -> x72, waiting for transfers between devices: 3.78 us -> 186 us  [the longest x16 127 us: shift(): return lax.ppermute(value, 'tensor', pairs)]
    ppermute x6 -> x72, starting transfers between devices: 11.7 us -> 93.5 us  [the longest x32 25.7 us: core_swap(): return lax.ppermute(value, 'section', [(0, 1), (1, 0)])]
    pallas_call x0 -> x4, Pallas kernels: none -> 62 us  [the longest x2 33.6 us: attention_backward(): pl.pallas_call(functools.partial(attention_backward_kernel, count, block_...]
    reduce_sum x41 -> x14, other arithmetic: 54.3 us -> 8.29 us  [the longest x4 3.44 us: norm_back(): jnp.mean(entry, axis=-1, keepdims=True)]
    dynamic_update_slice x15 -> x0, other arithmetic: 28.2 us -> none  [local(): lax.scan(forward_step, first_sent, jnp.arange(row_total + 1))]
  transfers between devices with their start and end apart: 30 -> 72, of which waited for: 27 -> 29; matrix products, arithmetic and copies ran while one was open for 6% -> 19% of each run, Pallas kernels for 0% -> 3%
where the time goes in v1:
time: 522 us; the launch traced here: 512 us
  waiting for transfers between devices  186 us (36%)
  starting transfers between devices  93.5 us (18%)
  matrix products  62 us (12%)
  Pallas kernels  62 us (12%)
  blocking collectives  45.4 us (9%)
  other arithmetic  34.3 us (7%)
  local copies, waits for them, and re-layouts  26.3 us (5%)
    ppermute x16, waiting for transfers between devices, shift(): return lax.ppermute(value, 'tensor', pairs)  127 us
    ppermute x12, waiting for transfers between devices, from_layer(): return lax.ppermute(value, ('section', 'tensor'), pairs)  52 us
    dot_general x14, matrix products, dot_nt(): lax.dot_general(a, b, (((1,), (1,)), ((), ())), preferred_element_type=f32)  37.3 us
    pallas_call x2, Pallas kernels, attention_backward(): pl.pallas_call(functools.partial(attention_backward_kernel, count, block_...  33.6 us
    psum x1, blocking collectives, local(): hidden_grad = lax.psum(dot_nt(grad_flat, w2_own), ('section', 'tensor'))  29.9 us
    pallas_call x2, Pallas kernels, attention_forward(): pl.pallas_call(functools.partial(attention_forward_kernel, count, block_r...  28.3 us
    ppermute x32, starting transfers between devices, core_swap(): return lax.ppermute(value, 'section', [(0, 1), (1, 0)])  25.7 us
    ppermute x12, starting transfers between devices, from_layer(): return lax.ppermute(value, ('section', 'tensor'), pairs)  25.6 us
  transfers between devices with their start and end apart: 72, of which 29 were waited for; matrix products, arithmetic and copies ran while one was open for 19% of the time, Pallas kernels for 3%

profile of v1, /device:TPU:1, one launch (start us, length us, event | category | flops | bytes accessed | tf_op | source)
XLA Modules:
  0.0 512.5 jit_solution(7101361686811077648)
XLA Ops:
  29.2 6.8 %collective-permute-done.6 = bf16[256,1024]{1,0:T(8,128)(2,1)} collective-permute-done((bf16[256,1024]{1,0:T(8,128)(2,1)S(1)}, bf16[256,1024]{1,0:T(8,128)(2,1)}, u32[]{:S(2)}, u32[]{:S(2)}) %collective-permute-start.6) | collective-permute-done | bytes 524320 | tf_op jit(solution)/shard_map/ppermute | solution.py:315
  48.2 14.2 %attention_forward.2 = (bf16[512,256]{1,0:T(8,128)(2,1)S(1)}, bf16[512,256]{1,0:T(8,128)(2,1)S(1)}, f32[8,1024]{1,0:T(8,128)S(1)}) custom-call(s32[4]{0:T(128)S(1)} %pad_add_fusion.order_ref, bf16[512,768]{1,0:T(8,128)(2,1)S(1)} %add_convert_fusion.3.refs_0_, bf16[512,768]{1,0:T(8,128)(2,1)S(1)} %add_convert_fusion.2.refs_1_, ...), custom_call_target="tpu_custom_call" | custom-call | flops 2147483648 | bytes 2097152 | tf_op jit(solution)/shard_map/attention_forward/pallas_call | solution.py:215
  69.5 9.6 %collective-permute-done.10 = bf16[256,1024]{1,0:T(8,128)(2,1)S(1)} collective-permute-done((bf16[256,1024]{1,0:T(8,128)(2,1)S(1)}, bf16[256,1024]{1,0:T(8,128)(2,1)S(1)}, u32[]{:S(2)}, u32[]{:S(2)}) %collective-permute-start.10) | collective-permute-done | bytes 524320 | tf_op jit(solution)/shard_map/ppermute | solution.py:315
  95.3 22.2 %collective-permute-done.15 = bf16[1024,1024]{1,0:T(8,128)(2,1)S(1)} collective-permute-done((bf16[1024,1024]{1,0:T(8,128)(2,1)S(1)}, bf16[1024,1024]{1,0:T(8,128)(2,1)S(1)}, u32[]{:S(2)}, u32[]{:S(2)}) %collective-permute-start.15) | collective-permute-done | bytes 2097184 | tf_op jit(solution)/shard_map/ppermute | solution.py:320
  140.5 10.3 %collective-permute-done.25 = bf16[256,1024]{1,0:T(8,128)(2,1)S(1)} collective-permute-done((bf16[256,1024]{1,0:T(8,128)(2,1)S(1)}, bf16[256,1024]{1,0:T(8,128)(2,1)S(1)}, u32[]{:S(2)}, u32[]{:S(2)}) %collective-permute-start.25) | collective-permute-done | bytes 524320 | tf_op jit(solution)/shard_map/ppermute | solution.py:315
  156.7 14.2 %attention_forward.3 = (bf16[512,256]{1,0:T(8,128)(2,1)S(1)}, bf16[512,256]{1,0:T(8,128)(2,1)S(1)}, f32[8,1024]{1,0:T(8,128)S(1)}) custom-call(s32[4]{0:T(128)S(1)} %pad_add_fusion.order_ref, bf16[512,768]{1,0:T(8,128)(2,1)S(1)} %add_convert_fusion.1.refs_0_, bf16[512,768]{1,0:T(8,128)(2,1)S(1)} %add_convert_fusion.refs_1_, ...), custom_call_target="tpu_custom_call" | custom-call | flops 2147483648 | bytes 2097152 | tf_op jit(solution)/shard_map/attention_forward/pallas_call | solution.py:215
  197.1 8.2 %collective-permute-done.39 = bf16[1024,1024]{1,0:T(8,128)(2,1)S(1)} collective-permute-done((bf16[1024,1024]{1,0:T(8,128)(2,1)S(1)}, bf16[1024,1024]{1,0:T(8,128)(2,1)S(1)}, u32[]{:S(2)}, u32[]{:S(2)}) %collective-permute-start.39) | collective-permute-done | bytes 2097184 | tf_op jit(solution)/shard_map/ppermute | solution.py:320
  208.5 10.1 %collective-permute-done.36 = bf16[256,1024]{1,0:T(8,128)(2,1)S(1)} collective-permute-done((bf16[256,1024]{1,0:T(8,128)(2,1)S(1)}, bf16[256,1024]{1,0:T(8,128)(2,1)S(1)}, u32[]{:S(2)}, u32[]{:S(2)}) %collective-permute-start.36) | collective-permute-done | bytes 524320 | tf_op jit(solution)/shard_map/ppermute | solution.py:315
  219.1 8.4 %collective-permute-done.35 = bf16[1024,1024]{1,0:T(8,128)(2,1)S(1)} collective-permute-done((bf16[1024,1024]{1,0:T(8,128)(2,1)S(1)}, bf16[1024,1024]{1,0:T(8,128)(2,1)S(1)}, u32[]{:S(2)}, u32[]{:S(2)}) %collective-permute-start.35) | collective-permute-done | bytes 2097184 | tf_op jit(solution)/shard_map/ppermute | solution.py:320
  235.0 6.9 %convolution_convert_fusion.9 = bf16[512,1024]{1,0:T(8,128)(2,1)} fusion(bf16[1024,1024]{1,0:T(8,128)(2,1)} %copy-done.29, f32[512,1024]{1,0:T(8,128)} %fusion.83, bf16[1024,1024]{1,0:T(8,128)(2,1)} %broadcast_select_fusion.1, bf16[256,1024]{1,0:T(8,128)(2,1)} %copy-done.76, bf16[256,1024]{1,0:T(8,128)(2,1)} %copy-done.75, f32[1024]{0:T(1024)} %bitcast.151), kind=kOutput, calls=%fused_computation.70 | convolution fusion | flops 2160590848 | bytes 8392704 | tf_op jit(solution)/shard_map/dot_general | solution.py:24
  243.8 6.9 %convolution_convert_fusion.8 = bf16[512,1024]{1,0:T(8,128)(2,1)} fusion(bf16[1024,1024]{1,0:T(8,128)(2,1)} %copy-done.29, f32[512,1024]{1,0:T(8,128)} %fusion.90, bf16[1024,1024]{1,0:T(8,128)(2,1)} %broadcast_select_fusion.1, bf16[256,1024]{1,0:T(8,128)(2,1)} %collective-permute-done.42, bf16[256,1024]{1,0:T(8,128)(2,1)} %broadcast_select_fusion.9, ...), kind=kOutput, calls=%fused_computation.69 | convolution fusion | flops 2160590848 | bytes 8392704 | tf_op jit(solution)/shard_map/dot_general | solution.py:24
  262.4 8.7 %collective-permute-done.41 = bf16[256,1024]{1,0:T(8,128)(2,1)S(1)} collective-permute-done((bf16[256,1024]{1,0:T(8,128)(2,1)S(1)}, bf16[256,1024]{1,0:T(8,128)(2,1)S(1)}, u32[]{:S(2)}, u32[]{:S(2)}) %collective-permute-start.41) | collective-permute-done | bytes 524320 | tf_op jit(solution)/shard_map/ppermute | solution.py:315
  271.6 10.7 %collective-permute-done.64 = bf16[256,1024]{1,0:T(8,128)(2,1)S(1)} collective-permute-done((bf16[256,1024]{1,0:T(8,128)(2,1)S(1)}, bf16[256,1024]{1,0:T(8,128)(2,1)S(1)}, u32[]{:S(2)}, u32[]{:S(2)}) %collective-permute-start.64) | collective-permute-done | bytes 524320 | tf_op jit(solution)/shard_map/ppermute | solution.py:315
  287.4 9.6 %collective-permute-done.46 = bf16[256,1024]{1,0:T(8,128)(2,1)S(1)} collective-permute-done((bf16[256,1024]{1,0:T(8,128)(2,1)S(1)}, bf16[256,1024]{1,0:T(8,128)(2,1)S(1)}, u32[]{:S(2)}, u32[]{:S(2)}) %collective-permute-start.46) | collective-permute-done | bytes 524320 | tf_op jit(solution)/shard_map/ppermute | solution.py:315
  301.2 16.7 %attention_backward.2 = (bf16[512,768]{1,0:T(8,128)(2,1)S(1)}, bf16[512,768]{1,0:T(8,128)(2,1)S(1)}, f32[2,128,256]{2,1,0:T(8,128)S(1)}) custom-call(s32[4]{0:T(128)S(1)} %pad_add_fusion.order_ref, bf16[512,768]{1,0:T(8,128)(2,1)S(1)} %copy-done.2, bf16[512,768]{1,0:T(8,128)(2,1)S(1)} %copy-done.4, bf16[512,256]{1,0:T(8,128)(2,1)S(1)} %convolution_convert_fusion.19.refs_2_, ...), custom_call_target="tpu_custom_call" | custom-call | flops 5368709120 | bytes 5242880 | tf_op jit(solution)/shard_map/attention_backward/pallas_call | solution.py:242
  322.4 11.9 %collective-permute-done.49 = bf16[256,1024]{1,0:T(8,128)(2,1)S(1)} collective-permute-done((bf16[256,1024]{1,0:T(8,128)(2,1)S(1)}, bf16[256,1024]{1,0:T(8,128)(2,1)S(1)}, u32[]{:S(2)}, u32[]{:S(2)}) %collective-permute-start.49) | collective-permute-done | bytes 524320 | tf_op jit(solution)/shard_map/ppermute | solution.py:315
  337.4 11.3 %collective-permute-done.51 = bf16[256,1024]{1,0:T(8,128)(2,1)S(1)} collective-permute-done((bf16[256,1024]{1,0:T(8,128)(2,1)}, bf16[256,1024]{1,0:T(8,128)(2,1)S(1)}, u32[]{:S(2)}, u32[]{:S(2)}) %collective-permute-start.51) | collective-permute-done | bytes 524320 | tf_op jit(solution)/shard_map/ppermute | solution.py:315
  354.0 6.9 %convolution_convert_fusion.7 = bf16[512,1024]{1,0:T(8,128)(2,1)} fusion(bf16[1024,1024]{1,0:T(8,128)(2,1)} %copy-done.27, f32[512,1024]{1,0:T(8,128)} %copy-done.79, bf16[1024,1024]{1,0:T(8,128)(2,1)} %copy-done.28, bf16[256,1024]{1,0:T(8,128)(2,1)} %collective-permute-done.52, bf16[256,1024]{1,0:T(8,128)(2,1)} %copy-done.77, f32[1024]{0:T(1024)S(1)} %bitcast.149), kind=kOutput, calls=%fused_computation.68 | convolution fusion | flops 2160590848 | bytes 8392704 | tf_op jit(solution)/shard_map/dot_general | solution.py:24
  363.2 6.9 %convolution_convert_fusion.6 = bf16[512,1024]{1,0:T(8,128)(2,1)} fusion(bf16[1024,1024]{1,0:T(8,128)(2,1)} %copy-done.27, f32[512,1024]{1,0:T(8,128)} %copy-done.78, bf16[1024,1024]{1,0:T(8,128)(2,1)} %copy-done.28, bf16[256,1024]{1,0:T(8,128)(2,1)} %collective-permute-done.55, bf16[256,1024]{1,0:T(8,128)(2,1)} %fusion.50, f32[1024]{0:T(1024)S(1)} %bitcast.150), kind=kOutput, calls=%fused_computation.67 | convolution fusion | flops 2160590848 | bytes 8392704 | tf_op jit(solution)/shard_map/dot_general | solution.py:24
  374.2 12.0 %collective-permute-done.54 = bf16[256,1024]{1,0:T(8,128)(2,1)S(1)} collective-permute-done((bf16[256,1024]{1,0:T(8,128)(2,1)S(1)}, bf16[256,1024]{1,0:T(8,128)(2,1)S(1)}, u32[]{:S(2)}, u32[]{:S(2)}) %collective-permute-start.54) | collective-permute-done | bytes 524320 | tf_op jit(solution)/shard_map/ppermute | solution.py:315
  392.1 9.9 %collective-permute-done.58 = bf16[256,1024]{1,0:T(8,128)(2,1)} collective-permute-done((bf16[256,1024]{1,0:T(8,128)(2,1)}, bf16[256,1024]{1,0:T(8,128)(2,1)}, u32[]{:S(2)}, u32[]{:S(2)}) %collective-permute-start.58) | collective-permute-done | bytes 524320 | tf_op jit(solution)/shard_map/ppermute | solution.py:315
  414.4 16.9 %attention_backward.3 = (bf16[512,768]{1,0:T(8,128)(2,1)S(1)}, bf16[512,768]{1,0:T(8,128)(2,1)S(1)}, f32[2,128,256]{2,1,0:T(8,128)S(1)}) custom-call(s32[4]{0:T(128)S(1)} %pad_add_fusion.order_ref, bf16[512,768]{1,0:T(8,128)(2,1)S(1)} %add_convert_fusion.3.refs_0_, bf16[512,768]{1,0:T(8,128)(2,1)S(1)} %add_convert_fusion.2.refs_1_, ...), custom_call_target="tpu_custom_call" | custom-call | flops 5368709120 | bytes 5242880 | tf_op jit(solution)/shard_map/attention_backward/pallas_call | solution.py:242
  441.9 15.5 %psum.14 = bf16[2,16,256]{2,1,0:T(8,128)(2,1)S(1)} all-reduce(f32[2,16,256]{2,1,0:T(8,128)S(1)} %add_select_fusion), channel_id=1, replica_groups=mesh['section'=2,'dp'=4,'tensor'=4] {'dp'}, use_global_device_ids=true, to_apply=%region_16.17 | all-reduce | flops 8192 | bytes 49152 | tf_op jit(solution)/shard_map/psum | solution.py:539
  464.7 29.9 %psum.15 = f32[10,512]{1,0:T(8,128)S(1)} all-reduce(f32[10,512]{1,0:T(8,128)S(1)} %fusion.147), channel_id=1, replica_groups=mesh['section'=2,'dp'=4,'tensor'=4] {'section','tensor'}, use_global_device_ids=true, to_apply=%region_17.18 | all-reduce | flops 5120 | bytes 40960 | tf_op jit(solution)/shard_map/psum | solution.py:555
  (432 shorter events, 225.1 us)
Async XLA Ops:
  10.9 32.0 %collective-permute-start.5 = (bf16[1024,768]{0,1:T(8,128)(2,1)S(1)}, bf16[1024,768]{0,1:T(8,128)(2,1)}, u32[]{:S(2)}, u32[]{:S(2)}) collective-permute-start(bf16[1024,768]{0,1:T(8,128)(2,1)S(1)} %bitcast.107), channel_id=1, source_target_pairs={{0,18},{1,19},{2,16},{3,17},{4,22},{5,23},{6,20},{7,21},{8,26},{9,... | collective-permute-start | bytes 4718600 | tf_op jit(solution)/shard_map/ppermute | solution.py:320
  26.1 21.0 %collective-permute-start.4 = (bf16[256,1024]{1,0:T(8,128)(2,1)S(1)}, bf16[256,1024]{1,0:T(8,128)(2,1)S(1)}, u32[]{:S(2)}, u32[]{:S(2)}) collective-permute-start(bf16[256,1024]{1,0:T(8,128)(2,1)S(1)} %fusion.53), channel_id=1, source_target_pairs={{0,16},{16,0},{1,17},{17,1},{2,18},{18,2},{3,19},{19,3},{4,20},{20... | collective-permute-start | bytes 1572872 | tf_op jit(solution)/shard_map/ppermute | solution.py:307
  66.9 28.2 %collective-permute-start.14 = (bf16[1024,1024]{1,0:T(8,128)(2,1)S(1)}, bf16[1024,1024]{1,0:T(8,128)(2,1)S(1)}, u32[]{:S(2)}, u32[]{:S(2)}) collective-permute-start(bf16[1024,1024]{1,0:T(8,128)(2,1)S(1)} %bitcast.114), channel_id=1, source_target_pairs={{0,18},{1,19},{2,16},{3,17},{4,22},{5,23},{6,20},{7,21},{8,26},{9,... | collective-permute-start | bytes 6291464 | tf_op jit(solution)/shard_map/ppermute | solution.py:320
  68.2 49.4 %collective-permute-start.15 = (bf16[1024,1024]{1,0:T(8,128)(2,1)S(1)}, bf16[1024,1024]{1,0:T(8,128)(2,1)S(1)}, u32[]{:S(2)}, u32[]{:S(2)}) collective-permute-start(bf16[1024,1024]{1,0:T(8,128)(2,1)S(1)} %bitcast.117), channel_id=1, source_target_pairs={{0,18},{1,19},{2,16},{3,17},{4,22},{5,23},{6,20},{7,21},{8,26},{9,... | collective-permute-start | bytes 6291464 | tf_op jit(solution)/shard_map/ppermute | solution.py:320
  81.6 45.7 %collective-permute-start.21 = (bf16[40,1024]{1,0:T(8,128)(2,1)S(1)}, bf16[40,1024]{1,0:T(8,128)(2,1)S(1)}, u32[]{:S(2)}, u32[]{:S(2)}) collective-permute-start(bf16[40,1024]{1,0:T(8,128)(2,1)S(1)} %concatenate.68), channel_id=1, source_target_pairs={{16,18},{17,19},{18,16},{19,17},{20,22},{21,23},{22,20},{23,21},{2... | collective-permute-start | bytes 245768 | tf_op jit(solution)/shard_map/ppermute | solution.py:320
  84.7 46.0 %collective-permute-start.20 = (bf16[40,1024]{1,0:T(8,128)(2,1)S(1)}, bf16[40,1024]{1,0:T(8,128)(2,1)S(1)}, u32[]{:S(2)}, u32[]{:S(2)}) collective-permute-start(bf16[40,1024]{1,0:T(8,128)(2,1)S(1)} %concatenate.68), channel_id=1, source_target_pairs={{16,0},{17,1},{18,2},{19,3},{20,4},{21,5},{22,6},{23,7},{24,8},{25... | collective-permute-start | bytes 245768 | tf_op jit(solution)/shard_map/ppermute | solution.py:331
  93.1 24.8 %collective-permute-start.13 = (bf16[256,1024]{1,0:T(8,128)(2,1)S(1)}, bf16[256,1024]{1,0:T(8,128)(2,1)S(1)}, u32[]{:S(2)}, u32[]{:S(2)}) collective-permute-start(bf16[256,1024]{1,0:T(8,128)(2,1)S(1)} %collective-permute-done.12), channel_id=1, source_target_pairs={{0,16},{16,0},{1,17},{17,1},{2,18},{18,2},{3,19},{19,3},{4,20},{20... | collective-permute-start | bytes 1572872 | tf_op jit(solution)/shard_map/ppermute | solution.py:307
  130.7 22.4 %collective-permute-start.23 = (bf16[1024,768]{0,1:T(8,128)(2,1)S(1)}, bf16[1024,768]{0,1:T(8,128)(2,1)S(1)}, u32[]{:S(2)}, u32[]{:S(2)}) collective-permute-start(bf16[1024,768]{0,1:T(8,128)(2,1)S(1)} %bitcast.108), channel_id=1, source_target_pairs={{16,0},{17,1},{18,2},{19,3},{20,4},{21,5},{22,6},{23,7},{24,8},{25... | collective-permute-start | bytes 4718600 | tf_op jit(solution)/shard_map/ppermute | solution.py:331
  132.7 21.5 %collective-permute-start.24 = (bf16[1024,768]{0,1:T(8,128)(2,1)S(1)}, bf16[1024,768]{0,1:T(8,128)(2,1)S(1)}, u32[]{:S(2)}, u32[]{:S(2)}) collective-permute-start(bf16[1024,768]{0,1:T(8,128)(2,1)S(1)} %bitcast.109), channel_id=1, source_target_pairs={{16,18},{17,19},{18,16},{19,17},{20,22},{21,23},{22,20},{23,21},{2... | collective-permute-start | bytes 4718600 | tf_op jit(solution)/shard_map/ppermute | solution.py:320
  174.9 21.9 %collective-permute-start.38 = (bf16[1024,1024]{1,0:T(8,128)(2,1)S(1)}, bf16[1024,1024]{1,0:T(8,128)(2,1)S(1)}, u32[]{:S(2)}, u32[]{:S(2)}) collective-permute-start(bf16[1024,1024]{1,0:T(8,128)(2,1)S(1)} %bitcast.115), channel_id=1, source_target_pairs={{16,0},{17,1},{18,2},{19,3},{20,4},{21,5},{22,6},{23,7},{24,8},{25... | collective-permute-start | bytes 6291464 | tf_op jit(solution)/shard_map/ppermute | solution.py:331
  178.2 27.1 %collective-permute-start.39 = (bf16[1024,1024]{1,0:T(8,128)(2,1)S(1)}, bf16[1024,1024]{1,0:T(8,128)(2,1)S(1)}, u32[]{:S(2)}, u32[]{:S(2)}) collective-permute-start(bf16[1024,1024]{1,0:T(8,128)(2,1)S(1)} %bitcast.116), channel_id=1, source_target_pairs={{16,18},{17,19},{18,16},{19,17},{20,22},{21,23},{22,20},{23,21},{2... | collective-permute-start | bytes 6291464 | tf_op jit(solution)/shard_map/ppermute | solution.py:320
  183.0 25.0 %collective-permute-start.34 = (bf16[1024,1024]{1,0:T(8,128)(2,1)S(1)}, bf16[1024,1024]{1,0:T(8,128)(2,1)S(1)}, u32[]{:S(2)}, u32[]{:S(2)}) collective-permute-start(bf16[1024,1024]{1,0:T(8,128)(2,1)S(1)} %bitcast.118), channel_id=1, source_target_pairs={{16,0},{17,1},{18,2},{19,3},{20,4},{21,5},{22,6},{23,7},{24,8},{25... | collective-permute-start | bytes 6291464 | tf_op jit(solution)/shard_map/ppermute | solution.py:331
  184.5 43.0 %collective-permute-start.35 = (bf16[1024,1024]{1,0:T(8,128)(2,1)S(1)}, bf16[1024,1024]{1,0:T(8,128)(2,1)S(1)}, u32[]{:S(2)}, u32[]{:S(2)}) collective-permute-start(bf16[1024,1024]{1,0:T(8,128)(2,1)S(1)} %bitcast.119), channel_id=1, source_target_pairs={{16,18},{17,19},{18,16},{19,17},{20,22},{21,23},{22,20},{23,21},{2... | collective-permute-start | bytes 6291464 | tf_op jit(solution)/shard_map/ppermute | solution.py:320
  196.7 21.9 %collective-permute-start.36 = (bf16[256,1024]{1,0:T(8,128)(2,1)S(1)}, bf16[256,1024]{1,0:T(8,128)(2,1)S(1)}, u32[]{:S(2)}, u32[]{:S(2)}) collective-permute-start(bf16[256,1024]{1,0:T(8,128)(2,1)S(1)} %add_convert_fusion.10), channel_id=1, source_target_pairs={{0,1},{1,0},{2,3},{3,2},{4,5},{5,4},{6,7},{7,6},{8,9},{9,8},{10,11... | collective-permute-start | bytes 1572872 | tf_op jit(solution)/shard_map/ppermute | solution.py:315
  205.3 23.7 %collective-permute-start.43 = (bf16[256,1024]{1,0:T(8,128)(2,1)S(1)}, bf16[256,1024]{1,0:T(8,128)(2,1)S(1)}, u32[]{:S(2)}, u32[]{:S(2)}) collective-permute-start(bf16[256,1024]{1,0:T(8,128)(2,1)S(1)} %add_convert_fusion.10), channel_id=1, source_target_pairs={{0,16},{16,0},{1,17},{17,1},{2,18},{18,2},{3,19},{19,3},{4,20},{20... | collective-permute-start | bytes 1572872 | tf_op jit(solution)/shard_map/ppermute | solution.py:307
  208.0 35.8 %collective-permute-start.42 = (bf16[256,1024]{1,0:T(8,128)(2,1)}, bf16[256,1024]{1,0:T(8,128)(2,1)}, u32[]{:S(2)}, u32[]{:S(2)}) collective-permute-start(bf16[256,1024]{1,0:T(8,128)(2,1)} %broadcast_select_fusion.9), channel_id=1, source_target_pairs={{0,16},{16,0},{1,17},{17,1},{2,18},{18,2},{3,19},{19,3},{4,20},{20... | collective-permute-start | bytes 1572872 | tf_op jit(solution)/shard_map/ppermute | solution.py:307
  208.0 26.2 %collective-permute-start.33 = (bf16[256,1024]{1,0:T(8,128)(2,1)S(1)}, bf16[256,1024]{1,0:T(8,128)(2,1)S(1)}, u32[]{:S(2)}, u32[]{:S(2)}) collective-permute-start(bf16[256,1024]{1,0:T(8,128)(2,1)S(1)} %collective-permute-done.32), channel_id=1, source_target_pairs={{0,16},{16,0},{1,17},{17,1},{2,18},{18,2},{3,19},{19,3},{4,20},{20... | collective-permute-start | bytes 1572872 | tf_op jit(solution)/shard_map/ppermute | solution.py:307
  404.1 103.6 %collective-permute-start.68 = (bf16[256,1024]{1,0:T(8,128)(2,1)}, bf16[256,1024]{1,0:T(8,128)(2,1)}, u32[]{:S(2)}, u32[]{:S(2)}) collective-permute-start(bf16[256,1024]{1,0:T(8,128)(2,1)} %get-tuple-element.77), channel_id=1, source_target_pairs={{16,18},{17,19},{18,16},{19,17},{20,22},{21,23},{22,20},{23,21},{2... | collective-permute-start | bytes 1572872 | tf_op jit(solution)/shard_map/ppermute | solution.py:328
  406.7 32.0 %collective-permute-start.71 = (f32[2,16,256]{2,1,0:T(8,128)S(1)}, f32[2,16,256]{2,1,0:T(8,128)S(1)}, u32[]{:S(2)}, u32[]{:S(2)}) collective-permute-start(f32[2,16,256]{2,1,0:T(8,128)S(1)} %slice.229), channel_id=1, source_target_pairs={{16,18},{17,19},{18,16},{19,17},{20,22},{21,23},{22,20},{23,21},{2... | collective-permute-start | bytes 98312 | tf_op jit(solution)/shard_map/ppermute | solution.py:328
  409.6 30.4 %collective-permute-start.70 = (f32[2,16,256]{2,1,0:T(8,128)S(1)}, f32[2,16,256]{2,1,0:T(8,128)S(1)}, u32[]{:S(2)}, u32[]{:S(2)}) collective-permute-start(f32[2,16,256]{2,1,0:T(8,128)S(1)} %slice.229), channel_id=1, source_target_pairs={{0,16},{1,17},{2,18},{3,19},{4,20},{5,21},{6,22},{7,23},{8,24},{9,... | collective-permute-start | bytes 98312 | tf_op jit(solution)/shard_map/ppermute | solution.py:334
  435.8 21.6 %collective-permute-start.60 = (bf16[256,1024]{1,0:T(8,128)(2,1)S(1)}, bf16[256,1024]{1,0:T(8,128)(2,1)S(1)}, u32[]{:S(2)}, u32[]{:S(2)}) collective-permute-start(bf16[256,1024]{1,0:T(8,128)(2,1)S(1)} %slice.276), channel_id=1, source_target_pairs={{0,16},{16,0},{1,17},{17,1},{2,18},{18,2},{3,19},{19,3},{4,20},{20... | collective-permute-start | bytes 1572872 | tf_op jit(solution)/shard_map/ppermute | solution.py:307
  438.7 58.4 %collective-permute-start.66 = (bf16[256,1024]{1,0:T(8,128)(2,1)}, bf16[256,1024]{1,0:T(8,128)(2,1)}, u32[]{:S(2)}, u32[]{:S(2)}) collective-permute-start(bf16[256,1024]{1,0:T(8,128)(2,1)} %get-tuple-element.77), channel_id=1, source_target_pairs={{0,16},{1,17},{2,18},{3,19},{4,20},{5,21},{6,22},{7,23},{8,24},{9,... | collective-permute-start | bytes 1572872 | tf_op jit(solution)/shard_map/ppermute | solution.py:334
  440.0 55.2 %collective-permute-start.62 = (bf16[256,1024]{1,0:T(8,128)(2,1)}, bf16[256,1024]{1,0:T(8,128)(2,1)}, u32[]{:S(2)}, u32[]{:S(2)}) collective-permute-start(bf16[256,1024]{1,0:T(8,128)(2,1)} %slice.278), channel_id=1, source_target_pairs={{0,16},{16,0},{1,17},{17,1},{2,18},{18,2},{3,19},{19,3},{4,20},{20... | collective-permute-start | bytes 1572872 | tf_op jit(solution)/shard_map/ppermute | solution.py:307
  458.5 36.7 %collective-permute-start.61 = (bf16[256,1024]{1,0:T(8,128)(2,1)}, bf16[256,1024]{1,0:T(8,128)(2,1)}, u32[]{:S(2)}, u32[]{:S(2)}) collective-permute-start(bf16[256,1024]{1,0:T(8,128)(2,1)} %add_convert_fusion.6), channel_id=1, source_target_pairs={{0,1},{1,0},{2,3},{3,2},{4,5},{5,4},{6,7},{7,6},{8,9},{9,8},{10,11... | collective-permute-start | bytes 1572872 | tf_op jit(solution)/shard_map/ppermute | solution.py:315
  (129 other events, 1433.6 us)

commit v2 on v1

v2 whole, which is shorter than its diff:
```python
import functools

import jax
import jax.numpy as jnp
from jax import lax
from jax.experimental import pallas as pl
from jax.experimental.pallas import tpu as pltpu
from jax.sharding import PartitionSpec as P

epsilon = 1e-05
masked_value = -1e30
max_segment = 512
prefix_rows = 16
stat_rows = 8
f32 = jnp.float32
bf16 = jnp.bfloat16


small_cost = pl.CostEstimate(flops=1, bytes_accessed=1, transcendentals=0)


def dot_nn(a, b):
    return lax.dot_general(a, b, (((1,), (0,)), ((), ())), preferred_element_type=f32)


def dot_nt(a, b):
    return lax.dot_general(a, b, (((1,), (1,)), ((), ())), preferred_element_type=f32)


def key_blocks(index, block_rows):
    reach = -(-(max_segment - 1) // block_rows)
    return list(range(max(0, index - reach), index + 1))


def gather_rows(order_ref, sources, target_ref, block_rows):
    for place in range(2 * len(sources)):
        start = pl.multiple_of(order_ref[place] * block_rows, block_rows)
        target_ref[pl.ds(start, block_rows), :] = sources[place // 2][
            pl.ds((place % 2) * block_rows, block_rows), :
        ]


def scatter_rows(order_ref, source_ref, targets, block_rows, columns):
    for place in range(2 * len(targets)):
        start = pl.multiple_of(order_ref[place] * block_rows, block_rows)
        targets[place // 2][pl.ds((place % 2) * block_rows, block_rows), columns] = source_ref[
            pl.ds(start, block_rows), :
        ].astype(targets[place // 2].dtype)


def segment_column(seg_ref, start, rows):
    row = seg_ref[0:1, start : start + rows]
    return jnp.transpose(jnp.broadcast_to(row, (128, rows)))[:, 0:1]


def attention_forward_kernel(count, block_rows, head_dim, prefix_len, order_ref, *refs):
    packed_refs = refs[:count]
    pairs_ref, seg_ref = refs[count : count + 2]
    context_refs = refs[count + 2 : 2 * count + 2]
    lse_ref, rows_ref, context_ref, bias_ref, vt_ref, pvt_ref, ct_ref = refs[2 * count + 2 :]
    width = pairs_ref.shape[2]
    heads = width // head_dim
    blocks = 2 * count
    scaling = head_dim ** (-0.5)
    gather_rows(order_ref, packed_refs, rows_ref, block_rows)
    lane = lax.broadcasted_iota(jnp.int32, (1, width), 1) // head_dim
    prefix_bias = jnp.where(
        lax.broadcasted_iota(jnp.int32, (pairs_ref.shape[1], 1), 0) < prefix_len, 0.0, masked_value
    )
    prefix_keys = pairs_ref[0]
    pvt_ref[...] = jnp.transpose(pairs_ref[1].astype(f32)).astype(bf16)
    for index in range(blocks):
        vt_ref[index] = jnp.transpose(
            rows_ref[index * block_rows : (index + 1) * block_rows, 2 * width :].astype(f32)
        ).astype(bf16)
    for index in range(blocks):
        start = index * block_rows
        keys = key_blocks(index, block_rows)
        fill_bias(seg_ref, bias_ref, index, keys, block_rows)
        queries = rows_ref[pl.ds(start, block_rows), 0:width]

        def one_head(head, carry):
            query = jnp.where(lane == head, queries, 0.0) * jnp.asarray(scaling, bf16)
            span = pl.ds(pl.multiple_of(head * head_dim, head_dim), head_dim)
            prefix_scores = dot_nt(prefix_keys, query) + prefix_bias
            row_max = jnp.max(prefix_scores, axis=0, keepdims=True)
            scores = []
            for slot, key in enumerate(keys):
                rows = slice(key * block_rows, (key + 1) * block_rows)
                score = dot_nt(rows_ref[rows, width : 2 * width], query) + bias_ref[slot]
                row_max = jnp.maximum(row_max, jnp.max(score, axis=0, keepdims=True))
                scores.append(score)
            prefix_exp = jnp.exp(prefix_scores - row_max)
            row_sum = jnp.sum(prefix_exp, axis=0, keepdims=True)
            context = dot_nn(pvt_ref[span, :], prefix_exp.astype(bf16))
            for score, key in zip(scores, keys):
                exped = jnp.exp(score - row_max)
                row_sum = row_sum + jnp.sum(exped, axis=0, keepdims=True)
                context = context + dot_nn(vt_ref[key, span, :], exped.astype(bf16))
            ct_ref[span, :] = context * (1.0 / row_sum)
            lse_ref[pl.ds(head, 1), start : start + block_rows] = row_max + jnp.log(row_sum)
            return carry

        lax.fori_loop(0, heads, one_head, 0, unroll=True)
        context_ref[pl.ds(start, block_rows), :] = jnp.transpose(ct_ref[...]).astype(bf16)
    scatter_rows(order_ref, context_ref, context_refs, block_rows, slice(0, width))


def fill_bias(seg_ref, bias_ref, index, keys, block_rows):
    seg_query = seg_ref[0:1, index * block_rows : (index + 1) * block_rows]
    for slot, key in enumerate(keys):
        same = segment_column(seg_ref, key * block_rows, block_rows) == seg_query
        if key == index:
            shape = (block_rows, block_rows)
            same = same & (
                lax.broadcasted_iota(jnp.int32, shape, 0)
                <= lax.broadcasted_iota(jnp.int32, shape, 1)
            )
        bias_ref[slot] = jnp.where(same, 0.0, masked_value)


def attention_backward_kernel(count, block_rows, head_dim, prefix_len, order_ref, *refs):
    packed_refs = refs[:count]
    grad_refs = refs[count : 2 * count]
    pairs_ref, seg_ref, lse_ref = refs[2 * count : 2 * count + 3]
    out_refs = refs[2 * count + 3 : 3 * count + 3]
    prefix_out = refs[3 * count + 3]
    rows_ref, grad_ref, bias_ref, kt_ref, pkt_ref, dqt_ref, dq_ref, dk_ref, dv_ref = refs[
        3 * count + 4 :
    ]
    width = pairs_ref.shape[2]
    heads = width // head_dim
    blocks = 2 * count
    scaling = head_dim ** (-0.5)
    gather_rows(order_ref, packed_refs, rows_ref, block_rows)
    gather_rows(order_ref, grad_refs, grad_ref, block_rows)
    lane = lax.broadcasted_iota(jnp.int32, (1, width), 1) // head_dim
    prefix_bias = jnp.where(
        lax.broadcasted_iota(jnp.int32, (pairs_ref.shape[1], 1), 0) < prefix_len, 0.0, masked_value
    )
    prefix_keys, prefix_values = pairs_ref[0], pairs_ref[1]
    pkt_ref[...] = jnp.transpose(prefix_keys.astype(f32)).astype(bf16)
    dk_ref[...] = jnp.zeros_like(dk_ref)
    dv_ref[...] = jnp.zeros_like(dv_ref)
    prefix_out[...] = jnp.zeros_like(prefix_out)
    for index in range(blocks):
        kt_ref[index] = jnp.transpose(
            rows_ref[index * block_rows : (index + 1) * block_rows, width : 2 * width].astype(f32)
        ).astype(bf16)
    for index in range(blocks):
        start = index * block_rows
        keys = key_blocks(index, block_rows)
        fill_bias(seg_ref, bias_ref, index, keys, block_rows)
        queries = rows_ref[pl.ds(start, block_rows), 0:width]
        grads = grad_ref[pl.ds(start, block_rows), :]

        def one_head(head, carry):
            chosen = lane == head
            query = jnp.where(chosen, queries, 0.0) * jnp.asarray(scaling, bf16)
            grad = jnp.where(chosen, grads, 0.0)
            lse = lse_ref[pl.ds(head, 1), start : start + block_rows]
            span = pl.ds(pl.multiple_of(head * head_dim, head_dim), head_dim)
            prefix_prob = jnp.exp(dot_nt(prefix_keys, query) + prefix_bias - lse)
            prefix_dp = dot_nt(prefix_values, grad)
            delta = jnp.sum(prefix_prob * prefix_dp, axis=0, keepdims=True)
            probs, dps = [], []
            for slot, key in enumerate(keys):
                rows = slice(key * block_rows, (key + 1) * block_rows)
                prob = jnp.exp(
                    dot_nt(rows_ref[rows, width : 2 * width], query) + bias_ref[slot] - lse
                )
                dp = dot_nt(rows_ref[rows, 2 * width :], grad)
                delta = delta + jnp.sum(prob * dp, axis=0, keepdims=True)
                probs.append(prob)
                dps.append(dp)
            prefix_ds = (prefix_prob * (prefix_dp - delta)).astype(bf16)
            prefix_out[0] += dot_nn(prefix_ds, query)
            prefix_out[1] += dot_nn(prefix_prob.astype(bf16), grad)
            dqt = dot_nn(pkt_ref[span, :], prefix_ds)
            for prob, dp, key in zip(probs, dps, keys):
                rows = slice(key * block_rows, (key + 1) * block_rows)
                ds = (prob * (dp - delta)).astype(bf16)
                dk_ref[rows, :] += dot_nn(ds, query)
                dv_ref[rows, :] += dot_nn(prob.astype(bf16), grad)
                dqt = dqt + dot_nn(kt_ref[key, span, :], ds)
            dqt_ref[span, :] = dqt
            return carry

        lax.fori_loop(0, heads, one_head, 0, unroll=True)
        dq_ref[pl.ds(start, block_rows), :] = jnp.transpose(dqt_ref[...]) * scaling
    scatter_rows(order_ref, dq_ref, out_refs, block_rows, slice(0, width))
    scatter_rows(order_ref, dk_ref, out_refs, block_rows, slice(width, 2 * width))
    scatter_rows(order_ref, dv_ref, out_refs, block_rows, slice(2 * width, 3 * width))


def gelu_parts(values):
    root = 0.7978845608028654
    square = values * values
    curve = jnp.tanh(root * values * (1.0 + 0.044715 * square))
    return (square, curve, root)


def feed_forward_kernel(groups, per, with_output, with_grad, *refs):
    refs = list(refs)
    normed_own, normed_peer, bias_ref = refs[:3]
    del refs[:3]
    grad_own, grad_peer = (refs.pop(0), refs.pop(0)) if with_grad else (None, None)
    chunk_refs = refs[: per * groups]
    del refs[: per * groups]
    out_own, out_peer = (refs.pop(0), refs.pop(0)) if with_output else (None, None)
    back_own, back_peer = (refs.pop(0), refs.pop(0)) if with_grad else (None, None)
    weight_ref, sems, normed_ref, grad_ref, hidden_ref, back_ref = refs
    tokens, width = normed_own.shape
    hidden = bias_ref.shape[2]
    rows = hidden // per
    block = min(256, width)

    def copies_of(group):
        return [
            pltpu.make_async_copy(
                chunk_refs[per * group + part],
                weight_ref.at[pl.ds((per * group + part) * rows, rows)],
                sems.at[group, part],
            )
            for part in range(per)
        ]

    for group in range(min(2, groups)):
        for copy in copies_of(group):
            copy.start()
    normed_ref[0:tokens, :] = normed_own[...]
    normed_ref[tokens:, :] = normed_peer[...]
    if with_grad:
        grad_ref[0:tokens, :] = grad_own[...]
        grad_ref[tokens:, :] = grad_peer[...]
    for group in range(groups):
        span = slice(group * hidden, (group + 1) * hidden)
        for copy in copies_of(group):
            copy.wait()
        if group + 2 < groups:
            for copy in copies_of(group + 2):
                copy.start()
        pre = dot_nt(normed_ref[...], weight_ref[span, 0:width]) + bias_ref[group]
        square, curve, root = gelu_parts(pre)
        if with_output:
            hidden_ref[:, span] = (0.5 * pre * (1.0 + curve)).astype(bf16)
        if with_grad:
            slope = 0.5 * (1.0 + curve) + 0.5 * pre * (1.0 - curve * curve) * (
                root * (1.0 + 3 * 0.044715 * square)
            )
            back_ref[:, span] = (dot_nt(grad_ref[...], weight_ref[span, width:]) * slope).astype(bf16)

    for at in range(0, width, block):
        span = slice(at, at + block)
        if with_output:
            total = dot_nn(hidden_ref[...], weight_ref[:, width + at : width + at + block])
            out_own[:, span] = total[0:tokens]
            out_peer[:, span] = total[tokens:].astype(bf16)
        if with_grad:
            total = dot_nn(back_ref[...], weight_ref[:, span])
            back_own[:, span] = total[0:tokens]
            back_peer[:, span] = total[tokens:].astype(bf16)


def whole(memory_space=pltpu.VMEM):
    return pl.BlockSpec(memory_space=memory_space)


def attention_forward(order, packed, pairs, seg_row, head_dim, prefix_len):
    count = len(packed)
    block_rows = packed[0].shape[0] // 2
    width = packed[0].shape[1] // 3
    seq_len = seg_row.shape[1]
    slots = len(key_blocks(2 * count - 1, block_rows))
    results = pl.pallas_call(
        functools.partial(attention_forward_kernel, count, block_rows, head_dim, prefix_len),
        out_shape=[jax.ShapeDtypeStruct((2 * block_rows, width), bf16)] * count
        + [jax.ShapeDtypeStruct((stat_rows, seq_len), f32)],
        in_specs=[whole(pltpu.SMEM)] + [whole()] * (count + 2),
        out_specs=[whole()] * (count + 1),
        scratch_shapes=[
            pltpu.VMEM((seq_len, 3 * width), bf16),
            pltpu.VMEM((seq_len, width), bf16),
            pltpu.VMEM((slots, block_rows, block_rows), f32),
            pltpu.VMEM((2 * count, width, block_rows), bf16),
            pltpu.VMEM((width, pairs.shape[1]), bf16),
            pltpu.VMEM((width, block_rows), f32),
        ],
        compiler_params=pltpu.CompilerParams(vmem_limit_bytes=32 << 20),
        cost_estimate=small_cost,
        name="attention_forward",
    )(order, *packed, pairs, seg_row)
    return (results[:count], results[count])


def attention_backward(order, packed, grads, pairs, seg_row, lse, head_dim, prefix_len):
    count = len(packed)
    block_rows = packed[0].shape[0] // 2
    width = packed[0].shape[1] // 3
    seq_len = seg_row.shape[1]
    blocks = 2 * count
    slots = len(key_blocks(blocks - 1, block_rows))
    results = pl.pallas_call(
        functools.partial(attention_backward_kernel, count, block_rows, head_dim, prefix_len),
        out_shape=[jax.ShapeDtypeStruct((2 * block_rows, 3 * width), bf16)] * count
        + [jax.ShapeDtypeStruct(pairs.shape, f32)],
        in_specs=[whole(pltpu.SMEM)] + [whole()] * (2 * count + 3),
        out_specs=[whole()] * (count + 1),
        scratch_shapes=[
            pltpu.VMEM((seq_len, 3 * width), bf16),
            pltpu.VMEM((seq_len, width), bf16),
            pltpu.VMEM((slots, block_rows, block_rows), f32),
            pltpu.VMEM((blocks, width, block_rows), bf16),
            pltpu.VMEM((width, pairs.shape[1]), bf16),
            pltpu.VMEM((width, block_rows), f32),
            pltpu.VMEM((seq_len, width), f32),
            pltpu.VMEM((seq_len, width), f32),
            pltpu.VMEM((seq_len, width), f32),
        ],
        compiler_params=pltpu.CompilerParams(vmem_limit_bytes=32 << 20),
        cost_estimate=small_cost,
        name="attention_backward",
    )(order, *packed, *grads, pairs, seg_row, lse)
    return (results[:count], results[count])


def chunk_kernel(place_ref, up_ref, down_ref, keep_ref, give_ref, up, down, chunks, sems, out_sems):
    hidden, width = down.shape
    rows = hidden // 4
    core, parity = place_ref[0], place_ref[1]
    half = width // 2
    loads = []
    for at in range(2):
        span = pl.ds(at * half, half)
        loads.append(pltpu.make_async_copy(up_ref.at[span], up.at[span], sems.at[at]))
    for at in range(2):
        span = pl.ds(at * 2 * rows, 2 * rows)
        loads.append(pltpu.make_async_copy(down_ref.at[span], down.at[span], sems.at[2 + at]))
    for load in loads:
        load.start()
    spots = []
    for side in range(2):
        for which in range(2):
            spots.append(
                (1 - core if side else core, 1 - parity if which else parity, 2 * side + which)
            )
    for at in range(2):
        loads[at].wait()
        span = slice(at * half, (at + 1) * half)
        for side, slot, index in spots:
            chunks[side, slot, :, span] = jnp.transpose(up[span, index * rows : (index + 1) * rows])
    for at in range(2):
        loads[2 + at].wait()
        for side, slot, index in spots[2 * at : 2 * at + 2]:
            chunks[side, slot, :, width:] = down[index * rows : (index + 1) * rows, :]
    stores = [
        pltpu.make_async_copy(chunks.at[side], target, out_sems.at[side])
        for side, target in enumerate((keep_ref, give_ref))
    ]
    for store in stores:
        store.start()
    for store in stores:
        store.wait()


def feed_forward_chunks(place, up, down):
    hidden, width = down.shape
    shape = (2, hidden // 4, 2 * width)
    return pl.pallas_call(
        chunk_kernel,
        out_shape=[jax.ShapeDtypeStruct(shape, bf16)] * 2,
        in_specs=[whole(pltpu.SMEM), whole(pltpu.HBM), whole(pltpu.HBM)],
        out_specs=[whole(pltpu.HBM)] * 2,
        scratch_shapes=[
            pltpu.VMEM((width, hidden), bf16),
            pltpu.VMEM((hidden, width), bf16),
            pltpu.VMEM((2,) + shape, bf16),
            pltpu.SemaphoreType.DMA((4,)),
            pltpu.SemaphoreType.DMA((2,)),
        ],
        compiler_params=pltpu.CompilerParams(vmem_limit_bytes=20 << 20),
        cost_estimate=small_cost,
        name="feed_forward_chunks",
    )(place, up, down)


def feed_forward(normed, bias, chunks, grads, with_output, per):
    rows = chunks[0].shape[0]
    groups, hidden = (len(chunks) // per, per * rows)
    bias = bias.reshape(groups, 1, hidden)
    tokens, width = normed[0].shape
    with_grad = grads is not None
    kinds = with_output + with_grad
    small = (8, 128)
    return pl.pallas_call(
        functools.partial(feed_forward_kernel, groups, per, with_output, with_grad),
        out_shape=[
            jax.ShapeDtypeStruct((tokens, width), f32),
            jax.ShapeDtypeStruct((tokens, width), bf16),
        ]
        * kinds,
        in_specs=[whole()] * (3 + 2 * with_grad) + [whole(pltpu.HBM)] * len(chunks),
        out_specs=[whole()] * (2 * kinds),
        scratch_shapes=[
            pltpu.VMEM((groups * hidden, 2 * width), bf16),
            pltpu.SemaphoreType.DMA((groups, per)),
            pltpu.VMEM((2 * tokens, width), bf16),
            pltpu.VMEM((2 * tokens, width) if with_grad else small, bf16),
            pltpu.VMEM((2 * tokens, groups * hidden) if with_output else small, bf16),
            pltpu.VMEM((2 * tokens, groups * hidden) if with_grad else small, bf16),
        ],
        compiler_params=pltpu.CompilerParams(vmem_limit_bytes=58 << 20),
        cost_estimate=small_cost,
        name="feed_forward",
    )(*normed, bias, *(grads if with_grad else ()), *chunks)


def place_kernel(spot_ref, low_own, low_other, high_own, high_other, out_ref):
    row = spot_ref[1]

    @pl.when(spot_ref[0] == 0)
    def _():
        out_ref[row] = low_own[...]
        out_ref[1 - row] = low_other[...]

    @pl.when(spot_ref[0] == 1)
    def _():
        out_ref[row] = high_own[...]
        out_ref[1 - row] = high_other[...]


def place_rows(spot, *blocks):
    return pl.pallas_call(
        place_kernel,
        out_shape=jax.ShapeDtypeStruct((2,) + blocks[0].shape, bf16),
        in_specs=[whole(pltpu.SMEM)] + [whole()] * 4,
        out_specs=whole(),
        compiler_params=pltpu.CompilerParams(vmem_limit_bytes=8 << 20),
        cost_estimate=small_cost,
        name="place_rows",
    )(spot, *blocks)


def centered_values(values):
    centered = values - jnp.mean(values, axis=-1, keepdims=True)
    scale = lax.rsqrt(jnp.mean(centered * centered, axis=-1, keepdims=True) + epsilon)
    return (centered * scale, scale)


def layer_norm(values, ln_gain, ln_bias):
    return centered_values(values)[0] * ln_gain + ln_bias


def norm_back(values, ln_gain, grad_normed):
    unit, scale = centered_values(values)
    entry = grad_normed * ln_gain
    return scale * (
        entry
        - jnp.mean(entry, axis=-1, keepdims=True)
        - unit * jnp.mean(entry * unit, axis=-1, keepdims=True)
    )


class Group:
    def __init__(self, tensor_size):
        self.size = tensor_size
        self.count = tensor_size // 2

    def core_swap(self, value):
        return lax.ppermute(value, "section", [(0, 1), (1, 0)])

    def shift(self, value, distance):
        pairs = [
            (half * self.count + place, half * self.count + (place + distance) % self.count)
            for half in range(2)
            for place in range(self.count)
        ]
        return lax.ppermute(value, "tensor", pairs)

    def cross(self, value):
        size, count = self.size, self.count
        pairs = [
            (core * size + place, (1 - core) * size + (place + count) % size)
            for core in range(2)
            for place in range(size)
        ]
        return lax.ppermute(value, ("section", "tensor"), pairs)

    def half_swap(self, value):
        pairs = [(place, (place + self.count) % self.size) for place in range(self.size)]
        return lax.ppermute(value, "tensor", pairs)

    def plane_swap(self, value, distance=1):
        planes = lax.axis_size("dp")
        pairs = [(plane, plane ^ distance) for plane in range(planes)]
        return lax.ppermute(value, "dp", pairs)

    def cross_from(self, value, core):
        size, count = self.size, self.count
        pairs = [
            (core * size + place, (1 - core) * size + (place + count) % size)
            for place in range(size)
        ]
        return lax.ppermute(value, ("section", "tensor"), pairs)

    def sum_planes(self, value):
        planes = lax.axis_size("dp")
        if planes & (planes - 1):
            return lax.psum(value, "dp")
        distance = 1
        while distance < planes:
            value = value + self.plane_swap(value, distance)
            distance *= 2
        return value

    def sum_shards(self, value):
        if self.size & (self.size - 1):
            return lax.psum(value, ("section", "tensor"))
        value = value + self.core_swap(value)
        distance = 1
        while distance < self.size:
            pairs = [(place, place ^ distance) for place in range(self.size)]
            value = value + lax.ppermute(value, "tensor", pairs)
            distance *= 2
        return value

    def shifts(self, stages, block):
        return [
            stages.send(functools.partial(self.shift, distance=distance), block)
            for distance in range(1, self.count)
        ]

    def paired(self, blocks):
        return [jnp.concatenate([part, self.core_swap(part)], axis=0) for part in blocks]

    def gather(self, stages, block):
        return self.paired([block] + self.shifts(stages, block))

    def scatter(self, stages, parts):
        rows = parts[0].shape[0] // 2
        total = None
        for distance in list(range(1, self.count)) + [0]:
            own, other = (parts[distance][:rows], parts[distance][rows:])
            summed = own.astype(f32) + self.core_swap(other).astype(f32)
            if distance:
                back = functools.partial(self.shift, distance=-distance)
                self.leaving = summed.astype(bf16)
                self.arrived = stages.send(back, self.leaving)
                summed = self.arrived.astype(f32)
            total = summed if total is None else total + summed
        return total


class Stages:
    def __init__(self):
        self.before, self.now = ([], [])

    def send(self, transfer, value):
        if self.before:
            value = lax.optimization_barrier((value, *self.before))[0]
        self.now.append(transfer(value))
        return self.now[-1]

    def next(self):
        self.before, self.now = (self.now, [])


def local(
    boundary,
    seg_ids,
    ln1_gain,
    ln1_bias,
    w_qkv,
    b_qkv,
    w_out,
    b_out,
    ln2_gain,
    ln2_bias,
    w_up,
    b_up,
    w_down,
    b_down,
    prefix_embed,
    reparam_w1,
    reparam_b1,
    reparam_w2,
    reparam_b2,
):
    core = lax.axis_index("section")
    place = lax.axis_index("tensor")
    group = Group(lax.axis_size("tensor"))
    count = group.count
    tok_rows, width = boundary.shape[2:]
    heads_local = w_qkv.shape[2]
    head_dim = w_qkv.shape[3] // 3
    head_width = heads_local * head_dim
    prefix_len = prefix_embed.shape[0]
    row = place // count
    low = core == 0

    def tied(value, *others):
        return lax.optimization_barrier((value,) + others)[0]

    stages = Stages()
    steps = range(1, count)

    own_row = lax.dynamic_index_in_dim(boundary[0], row, 0, False)
    other_row = lax.dynamic_index_in_dim(boundary[0], 1 - row, 0, False)
    came_row = stages.send(functools.partial(group.cross_from, core=0), other_row)
    inputs = jnp.where(low, own_row, came_row).astype(f32)
    proj_own = w_out.reshape(head_width, width)

    def layer_pair(own, far):
        return (jnp.where(low, own, far), jnp.where(low, far, own))


    def as_rows(value):
        value = value.reshape(-1, value.shape[-1])
        return jnp.pad(value, ((0, 0), (0, width - value.shape[1])))

    b_qkv_own = b_qkv.reshape(heads_local, 3, head_dim).transpose(1, 0, 2).reshape(1, 3 * head_width)
    small_parts = (ln1_gain, ln1_bias, b_out, ln2_gain, ln2_bias, b_down, b_up, b_up)
    small_own = jnp.concatenate([as_rows(part) for part in small_parts], axis=0)

    def on_chip(value):
        peer = group.core_swap(value)
        return jnp.stack([jnp.where(low, value, peer), jnp.where(low, peer, value)])

    small_chip = on_chip(small_own)

    def vectors_of(layer):
        return small_chip[layer, :8].astype(f32)

    def normed_one(layer, values):
        vectors = vectors_of(layer)
        return layer_norm(values, vectors[0:1], vectors[1:2]).astype(bf16)

    hidden_width = w_up.shape[2]
    rows = hidden_width // 4
    shared = lax.axis_size("dp") % 2 == 0
    parity = lax.axis_index("dp") % 2
    spot = jnp.stack([core, parity]).astype(jnp.int32)
    keep, give = feed_forward_chunks(spot, w_up[0], w_down[0])
    handed = group.core_swap(give)
    even_0 = jnp.where(low, keep[0], handed[0])
    later_keep, later_handed, _ = lax.optimization_barrier((keep, handed, even_0))
    even = [even_0, jnp.where(low, later_handed[0], later_keep[0])]
    odd = [
        jnp.where(low, later_keep[1], later_handed[1]),
        jnp.where(low, later_handed[1], later_keep[1]),
    ]

    prefix_pre = dot_nn(tied(prefix_embed, even[0]), reparam_w1) + reparam_b1.astype(f32)
    curve = jnp.tanh(prefix_pre)
    hidden_low = curve.astype(bf16)
    w2_own = (
        tied(reparam_w2, even[0])
        .reshape(reparam_w2.shape[0], heads_local, 2, head_dim)
        .transpose(0, 2, 1, 3)
        .reshape(reparam_w2.shape[0], 2 * head_width)
    )
    b2_own = (
        reparam_b2.reshape(heads_local, 2, head_dim).transpose(1, 0, 2).reshape(2 * head_width)
    )
    prefix_own = (dot_nn(hidden_low, w2_own) + b2_own.astype(f32)).astype(bf16)
    pairs_own = jnp.concatenate(
        [
            jnp.pad(value, ((0, prefix_rows - value.shape[0]), (0, width - value.shape[1])))
            for value in (prefix_own[:, :head_width], prefix_own[:, head_width:], b_qkv_own)
        ],
        axis=0,
    )
    qkv_own = (
        w_qkv.reshape(width, heads_local, 3, head_dim)
        .transpose(0, 2, 1, 3)
        .reshape(width, 3 * head_width)
    )

    def plane_send(value):
        return stages.send(group.plane_swap, value)

    def half_send(value):
        return stages.send(group.half_swap, value)

    stages.next()
    normed_0 = normed_one(0, inputs)
    gathered_0 = [normed_0] + group.shifts(stages, normed_0)
    side_even_0 = group.shifts(stages, tied(even[0], *gathered_0[1:]))
    small_half = half_send(small_chip)
    qkv_far = stages.send(group.cross, qkv_own)
    proj_far = stages.send(group.cross, proj_own)

    stages.next()
    came_grad = stages.send(functools.partial(group.cross_from, core=1), other_row)
    cotangent = jnp.where(low, came_grad, own_row)
    qkv = layer_pair(qkv_own, qkv_far)
    projs = layer_pair(proj_own, proj_far)
    pairs = layer_pair(pairs_own, stages.send(group.cross, pairs_own))
    up_bias = jnp.stack([small_chip[:, 6, :hidden_width], small_half[:, 6, :hidden_width]], axis=1)
    up_bias = jnp.stack([up_bias] + group.shifts(stages, up_bias), axis=1).astype(f32)
    up_bias = up_bias.reshape(2, 2 * count, 2, 2, rows)
    up_bias = jnp.where(low, up_bias[:, :, 0], up_bias[:, :, 1])
    up_bias = jnp.where(parity == 0, up_bias, up_bias[:, :, ::-1])
    up_bias = up_bias.reshape(2, 4 * count, rows)
    half_even_0 = half_send(even[0])
    side_even_1 = group.shifts(stages, even[1])
    if shared:
        side_odd_0 = [plane_send(value) for value in side_even_0]
    else:
        side_odd_0 = group.shifts(stages, odd[0])

    def all_chunks(layer, half, side, corner):
        chunks = [even[layer], odd[layer], *half]
        for at in range(count - 1):
            chunks += [side[0][at], side[1][at], corner[0][at], corner[1][at]]
        return chunks

    seg_row = lax.dynamic_index_in_dim(seg_ids, row, 0, True).astype(f32)
    chip = place % count
    orders = [
        jnp.stack(
            [
                jnp.bitwise_xor(row, jnp.bitwise_xor(core, swapped ^ layer)) * count
                + (chip - distance + count) % count
                for distance in range(count)
                for swapped in range(2)
            ]
        ).astype(jnp.int32)
        for layer in range(2)
    ]

    class Layer:
        def __init__(self, index):
            self.vectors = vectors_of(index)
            self.ln1_gain, self.ln1_bias, self.b_out = [self.vectors[at : at + 1] for at in range(3)]
            shard = tied(pairs[index], up_bias)
            self.pairs = shard[: 2 * prefix_rows, :head_width].reshape(2, prefix_rows, head_width)
            self.b_qkv = shard[2 * prefix_rows : 2 * prefix_rows + 1, : 3 * head_width].astype(f32)
            self.order = orders[index]
            self.qkv, self.out = (tied(qkv[index], *stages.before), projs[index])
            self.bias = up_bias[index]

        def attention(self, inputs, gathered):
            self.inputs = inputs
            gathered = lax.optimization_barrier((*gathered, *stages.before))[:count]
            self.packed = [
                (dot_nn(part, self.qkv) + self.b_qkv).astype(bf16)
                for part in group.paired(gathered)
            ]
            self.context, self.lse = attention_forward(
                self.order, self.packed, self.pairs, seg_row, head_dim, prefix_len
            )

        def project(self):
            context = lax.optimization_barrier((*self.context, *stages.before))[:count]
            parts = [dot_nn(part, self.out).astype(bf16) for part in context]
            self.middle = self.inputs + (group.scatter(stages, parts) + self.b_out)

        def project_here(self):
            context = lax.optimization_barrier((*self.context, *stages.before))[:count]
            branch = dot_nn(context[0], self.out)
            for distance in steps:
                came = group.shift(context[distance], -distance)
                branch = branch + dot_nn(came, self.out_side[distance - 1])
            rows = branch.shape[0] // 2
            own, peer = (branch[:rows], branch[rows:].astype(bf16))
            self.middle = self.inputs + (self.shared((own, peer)) + self.b_out)

        def norm_two(self, values):
            return layer_norm(values, self.vectors[3:4], self.vectors[4:5]).astype(bf16)

        def shared(self, *pairs):
            return sum([own + group.core_swap(peer).astype(f32) for own, peer in pairs])

        def output(self, middle, *pairs):
            return (middle + (self.shared(*pairs) + self.vectors[5:6])).astype(bf16)

        def middle_back(self, grad_out, *pairs):
            branch = self.shared(*pairs)
            return grad_out.astype(f32) + norm_back(self.middle, self.vectors[3:4], branch)

        def feed_forward(self, normed, grads, with_output):
            return feed_forward(normed, self.bias, self.chunks, grads, with_output, 2)

        def backward(self, grad_middle):
            stages.before = []
            grad_branch = grad_middle.astype(bf16)
            (grad_chip,) = group.paired([grad_branch])
            sides = [dot_nt(grad_chip, side).astype(bf16) for side in self.out_side]
            came = [group.shift(side, at + 1) for at, side in enumerate(sides)]
            grads = [dot_nt(grad_chip, self.out).astype(bf16)] + came
            grad_packed, grad_pairs = attention_backward(
                self.order, self.packed, grads, self.pairs, seg_row, self.lse, head_dim, prefix_len
            )
            parts = [dot_nt(part, self.qkv).astype(bf16) for part in grad_packed]
            grad_normed = group.scatter(stages, parts)
            grad_in = grad_middle + norm_back(self.inputs, self.ln1_gain, grad_normed)
            return (grad_in.astype(bf16), grad_pairs)

    layer_0 = Layer(0)
    layer_0.attention(inputs, gathered_0)

    stages.next()
    corner_even_0 = group.shifts(stages, half_even_0)
    half_even_1 = half_send(even[1])
    if shared:
        side_odd_1 = [plane_send(value) for value in side_even_1]
    else:
        side_odd_1 = group.shifts(stages, odd[1])
    layer_0.project()

    stages.next()
    half_odd_0 = half_send(odd[0])
    if shared:
        corner_odd_0 = [plane_send(value) for value in corner_even_0]
    else:
        corner_odd_0 = group.shifts(stages, half_odd_0)
    corner_even_1 = group.shifts(stages, half_even_1)
    layer_0.chunks = all_chunks(
        0,
        (half_even_0, half_odd_0),
        (side_even_0, side_odd_0),
        (corner_even_0, corner_odd_0),
    )
    middle_peer = group.core_swap(layer_0.middle)
    normed_pair = (layer_0.norm_two(layer_0.middle), layer_0.norm_two(middle_peer))

    stages.next()
    half_odd_1 = half_send(odd[1])
    if shared:
        corner_odd_1 = [plane_send(value) for value in corner_even_1]
    else:
        corner_odd_1 = group.shifts(stages, half_odd_1)
    out_sides = [
        [stages.send(functools.partial(group.shift, distance=-distance), proj) for distance in steps]
        for proj in projs
    ]
    normed_swapped = (tied(normed_pair[1], *stages.before), normed_pair[0])
    out_kept, out_sent = layer_0.feed_forward(normed_swapped, None, True)
    first_out = layer_0.output(middle_peer, (out_kept, tied(out_sent, *stages.now)))
    inputs_1 = first_out.astype(f32)
    normed_1 = normed_one(1, inputs_1)
    gathered_1 = [normed_1] + group.shifts(stages, normed_1)
    layer_1 = Layer(1)
    layer_0.out_side, layer_1.out_side = out_sides
    layer_1.attention(inputs_1, gathered_1)
    layer_1.chunks = all_chunks(
        1,
        (half_even_1, half_odd_1),
        (side_even_1, side_odd_1),
        (corner_even_1, corner_odd_1),
    )

    stages.next()
    w2_far = stages.send(group.cross, w2_own)
    w2_side = layer_pair(w2_own, w2_far)
    layer_1.project_here()
    normed = layer_1.norm_two(layer_1.middle)
    normed = (normed, group.core_swap(normed))
    cotangents = (cotangent, group.core_swap(cotangent))
    parts = layer_1.feed_forward(normed, cotangents, True)
    last_out = layer_1.output(layer_1.middle, parts[:2])
    grad_middle = layer_1.middle_back(cotangent, parts[2:])
    mid_grad, grad_pairs_one = layer_1.backward(grad_middle)
    high_other = group.cross_from(last_out, 0)
    mid_grad = tied(mid_grad, high_other, w2_far)
    mid_peer = group.core_swap(mid_grad)
    back_part = layer_0.feed_forward(normed_pair, (mid_peer, mid_grad), False)
    grad_middle = layer_0.middle_back(mid_peer, back_part)
    first_grad, grad_pairs_zero = layer_0.backward(grad_middle)

    low_other = group.cross_from(first_grad, 1)
    spot = jnp.stack([core, row]).astype(jnp.int32)
    boundary_result = place_rows(spot, first_grad, low_other, last_out, high_other)[None]

    def joined(pairs):
        return jnp.concatenate([pairs[0], pairs[1]], axis=1)

    grads = (joined(grad_pairs_zero), joined(grad_pairs_one))
    hidden_part = sum(
        lax.dot_general(
            grad,
            side.astype(f32),
            (((1,), (1,)), ((), ())),
            precision=lax.Precision.HIGHEST,
            preferred_element_type=f32,
        )
        for grad, side in zip(grads, w2_side)
    )
    kept, sent = layer_pair(*grads)
    summed = tied(jnp.concatenate([hidden_part, kept, sent], axis=1), group.leaving)
    summed = group.sum_planes(summed)
    hidden_width = hidden_part.shape[1]
    hidden_part = tied(summed[:, :hidden_width], group.arrived)
    hidden_grad = group.sum_shards(hidden_part)[:prefix_len]
    kept = summed[:, hidden_width : hidden_width + 2 * head_width]
    sent = summed[:, hidden_width + 2 * head_width :]
    grad_low = (kept + group.cross(sent))[:prefix_len].astype(bf16)
    grad_flat = (
        grad_low.reshape(prefix_len, 2, heads_local, head_dim)
        .transpose(0, 2, 1, 3)
        .reshape(prefix_len, 2 * head_width)
    )
    w2_grad = lax.dot_general(
        hidden_low, grad_flat, (((0,), (0,)), ((), ())), preferred_element_type=f32
    ).reshape(reparam_w2.shape)
    b2_grad = jnp.sum(grad_flat.astype(f32), axis=0).reshape(reparam_b2.shape)
    pre_grad = (hidden_grad * (1.0 - curve * curve)).astype(bf16)
    w1_grad = lax.dot_general(
        prefix_embed, pre_grad, (((0,), (0,)), ((), ())), preferred_element_type=f32
    )
    b1_grad = jnp.sum(pre_grad.astype(f32), axis=0)
    embed_grad = dot_nt(pre_grad, reparam_w1)
    return (boundary_result, embed_grad, w1_grad, b1_grad, w2_grad, b2_grad)


def solution(mesh):
    return jax.shard_map(
        local,
        mesh=mesh,
        in_specs=(
            P("section", "dp", "tensor", None),
            P("dp", None),
            P("section", None),
            P("section", None),
            P("section", None, "tensor", None),
            P("section", "tensor", None),
            P("section", "tensor", None, None),
            P("section", None),
            P("section", None),
            P("section", None),
            P("section", None, "tensor"),
            P("section", "tensor"),
            P("section", "tensor", None),
            P("section", None),
            P(),
            P(),
            P(),
            P(None, "section", "tensor", None),
            P("section", "tensor", None),
        ),
        out_specs=(
            P("section", "dp", "tensor", None),
            P(),
            P(),
            P(),
            P(None, "section", "tensor", None),
            P("section", "tensor", None),
        ),
        check_vma=False,
    )
```

time: 522 us -> 418 us (0.80)
  blocking collectives: 45.4 us -> 0 us
  matrix products: 62 us -> 18.9 us
  starting transfers between devices: 93.5 us -> 62.7 us
  Pallas kernels: 62 us -> 82.1 us
  waiting for transfers between devices: 186 us -> 176 us
  other arithmetic: 34.3 us -> 43.2 us
    psum x2 -> x0, blocking collectives: 45.4 us -> none  [the longest x1 29.9 us: local(): hidden_grad = lax.psum(dot_nt(grad_flat, w2_own), ('section', 'tensor'))]
    pallas_call x0 -> x5, Pallas kernels: none -> 42 us  [the longest x3 37.2 us: feed_forward(): pl.pallas_call(functools.partial(feed_forward_kernel, groups, per, with_o...]
    ppermute x16 -> x15, waiting for transfers between devices: 127 us -> 87.6 us  [shift(): return lax.ppermute(value, 'tensor', pairs)]
    dot_general x14 -> x9, matrix products: 37.3 us -> 7.09 us  [dot_nt(): lax.dot_general(a, b, (((1,), (1,)), ((), ())), preferred_element_type=f32)]
    ppermute x24 -> x22, starting transfers between devices: 51.1 us -> 29.2 us  [the longest x4 9.91 us: cross_from(): return lax.ppermute(value, ('section', 'tensor'), pairs)]
    ppermute x24 -> x22, waiting for transfers between devices: 54.3 us -> 73.7 us  [the longest x5 37.7 us: cross(): return lax.ppermute(value, ('section', 'tensor'), pairs)]
    dot_general x18 -> x10, matrix products: 23.9 us -> 9.07 us  [dot_nn(): lax.dot_general(a, b, (((1,), (0,)), ((), ())), preferred_element_type=f32)]
    pallas_call x2, Pallas kernels: 28.3 us -> 16.2 us  [attention_forward(): pl.pallas_call(functools.partial(attention_forward_kernel, count, block_r...]
  transfers between devices with their start and end apart: 72 -> 61, of which waited for: 29 -> 31; matrix products, arithmetic and copies ran while one was open for 19% -> 16% of each run, Pallas kernels for 3% -> 5%
where the time goes in v2:
time: 418 us; the launch traced here: 411 us
  waiting for transfers between devices  176 us (42%)
  Pallas kernels  82.1 us (20%)
  starting transfers between devices  62.7 us (15%)
  other arithmetic  43.2 us (10%)
  local copies, waits for them, and re-layouts  25.9 us (6%)
  matrix products  18.9 us (5%)
    ppermute x15, waiting for transfers between devices, shift(): return lax.ppermute(value, 'tensor', pairs)  87.6 us
    ppermute x5, waiting for transfers between devices, cross(): return lax.ppermute(value, ('section', 'tensor'), pairs)  37.7 us
    pallas_call x3, Pallas kernels, feed_forward(): pl.pallas_call(functools.partial(feed_forward_kernel, groups, per, with_o...  37.2 us
    pallas_call x2, Pallas kernels, attention_backward(): pl.pallas_call(functools.partial(attention_backward_kernel, count, block_...  24 us
    ppermute x24, starting transfers between devices, core_swap(): return lax.ppermute(value, 'section', [(0, 1), (1, 0)])  22.7 us
    pallas_call x2, Pallas kernels, attention_forward(): pl.pallas_call(functools.partial(attention_forward_kernel, count, block_r...  16.2 us
    ppermute x5, waiting for transfers between devices, half_swap(): return lax.ppermute(value, 'tensor', pairs)  15.9 us
    ppermute x4, waiting for transfers between devices, cross_from(): return lax.ppermute(value, ('section', 'tensor'), pairs)  14.9 us
  transfers between devices with their start and end apart: 61, of which 31 were waited for; matrix products, arithmetic and copies ran while one was open for 16% of the time, Pallas kernels for 5%

profile of v2, /device:TPU:1, one launch (start us, length us, event | category | flops | bytes accessed | tf_op | source)
XLA Modules:
  0.0 410.7 jit_solution(1857310652128945395)
XLA Ops:
  11.3 4.5 %collective-permute-start.3 = (bf16[2,256,2048]{2,1,0:T(8,128)(2,1)}, bf16[2,256,2048]{2,1,0:T(8,128)(2,1)}, u32[]{:S(2)}, u32[]{:S(2)}) collective-permute-start(bf16[2,256,2048]{2,1,0:T(8,128)(2,1)} %get-tuple-element.76), channel_id=1, source_target_pairs={{0,16},{16,0},{1,17},{17,1},{2,18},{18,2},{3,19},{19,3},{4,20},{20... | collective-permute-start | bytes 6291464 | tf_op jit(solution)/shard_map/ppermute | solution.py:470
  26.1 9.0 %collective-permute-done.7 = bf16[256,1024]{1,0:T(8,128)(2,1)S(1)} collective-permute-done((bf16[256,1024]{1,0:T(8,128)(2,1)S(1)}, bf16[256,1024]{1,0:T(8,128)(2,1)S(1)}, u32[]{:S(2)}, u32[]{:S(2)}) %collective-permute-start.7) | collective-permute-done | bytes 524320 | tf_op jit(solution)/shard_map/ppermute | solution.py:487
  43.7 24.4 %collective-permute-done.6 = bf16[1024,768]{0,1:T(8,128)(2,1)} collective-permute-done((bf16[1024,768]{0,1:T(8,128)(2,1)}, bf16[1024,768]{0,1:T(8,128)(2,1)}, u32[]{:S(2)}, u32[]{:S(2)}) %collective-permute-start.6) | collective-permute-done | bytes 1572896 | tf_op jit(solution)/shard_map/ppermute | solution.py:487
  68.1 3.8 broadcast_select_fusion
  91.3 8.0 %attention_forward.2 = (bf16[512,256]{1,0:T(8,128)(2,1)S(1)}, bf16[512,256]{1,0:T(8,128)(2,1)S(1)}, f32[8,1024]{1,0:T(8,128)S(1)}) custom-call(s32[4]{0:T(128)S(1)} %pad_add_fusion.2.order_ref, bf16[512,768]{1,0:T(8,128)(2,1)S(1)} %add_convert_fusion.3.refs_0_, bf16[512,768]{1,0:T(8,128)(2,1)S(1)} %add_convert_fusion.2.refs_1_, ...), custom_call_target="tpu_custom_call" | custom-call | flops 1 | bytes 1 | tf_op jit(solution)/shard_map/attention_forward/pallas_call | solution.py:275
  99.3 9.6 %collective-permute-done.8 = bf16[256,1024]{1,0:T(8,128)(2,1)S(1)} collective-permute-done((bf16[256,1024]{1,0:T(8,128)(2,1)}, bf16[256,1024]{1,0:T(8,128)(2,1)S(1)}, u32[]{:S(2)}, u32[]{:S(2)}) %collective-permute-start.8) | collective-permute-done | bytes 524320 | tf_op jit(solution)/shard_map/ppermute | solution.py:504
  117.1 30.4 %collective-permute-done.17 = bf16[256,1024]{1,0:T(8,128)(2,1)S(1)} collective-permute-done((bf16[256,1024]{1,0:T(8,128)(2,1)S(1)}, bf16[256,1024]{1,0:T(8,128)(2,1)S(1)}, u32[]{:S(2)}, u32[]{:S(2)}) %collective-permute-start.17) | collective-permute-done | bytes 524320 | tf_op jit(solution)/shard_map/ppermute | solution.py:478
  155.8 15.9 %collective-permute-done.23.refs_6_.refs_8_ = bf16[256,2048]{1,0:T(8,128)(2,1)} collective-permute-done((bf16[256,2048]{1,0:T(8,128)(2,1)}, bf16[256,2048]{1,0:T(8,128)(2,1)}, u32[]{:S(2)}, u32[]{:S(2)}) %collective-permute-start.23) | collective-permute-done | bytes 1048608 | tf_op jit(solution)/shard_map/ppermute | solution.py:491
  181.6 9.9 %feed_forward.3 = (f32[256,1024]{1,0:T(8,128)}, bf16[256,1024]{1,0:T(8,128)(2,1)}) custom-call(bf16[256,1024]{1,0:T(8,128)(2,1)} %get-tuple-element.107.refs_0_.refs_1_, bf16[256,1024]{1,0:T(8,128)(2,1)} %get-tuple-element.222.refs_1_.refs_0_, f32[4,1,512]{2,1,0:T(1,128)} %reshape_squeeze.7.refs_2_, bf16[256,2048]{1,0:T(8,128)(2,1)} %fusion.29.refs_3_.refs_5_, ...), custom_call_target="tpu_custom_call" | custom-call | flops 1 | bytes 1 | tf_op jit(solution)/shard_map/feed_forward/pallas_call | solution.py:395
  191.6 7.5 %collective-permute-done.29 = bf16[256,1024]{1,0:T(8,128)(2,1)S(1)} collective-permute-done((bf16[256,1024]{1,0:T(8,128)(2,1)}, bf16[256,1024]{1,0:T(8,128)(2,1)S(1)}, u32[]{:S(2)}, u32[]{:S(2)}) %collective-permute-start.29) | collective-permute-done | bytes 524320 | tf_op jit(solution)/shard_map/ppermute | solution.py:478
  199.1 3.7 collective-permute-start.30
  207.4 12.9 %collective-permute-done.31 = bf16[256,1024]{1,0:T(8,128)(2,1)S(1)} collective-permute-done((bf16[256,1024]{1,0:T(8,128)(2,1)S(1)}, bf16[256,1024]{1,0:T(8,128)(2,1)S(1)}, u32[]{:S(2)}, u32[]{:S(2)}) %collective-permute-start.31) | collective-permute-done | bytes 524320 | tf_op jit(solution)/shard_map/ppermute | solution.py:478
  225.2 8.2 %attention_forward.3 = (bf16[512,256]{1,0:T(8,128)(2,1)S(1)}, bf16[512,256]{1,0:T(8,128)(2,1)S(1)}, f32[8,1024]{1,0:T(8,128)S(1)}) custom-call(s32[4]{0:T(128)S(1)} %pad_add_fusion.3.order_ref, bf16[512,768]{1,0:T(8,128)(2,1)S(1)} %add_convert_fusion.1.refs_0_, bf16[512,768]{1,0:T(8,128)(2,1)S(1)} %add_convert_fusion.refs_1_, ...), custom_call_target="tpu_custom_call" | custom-call | flops 1 | bytes 1 | tf_op jit(solution)/shard_map/attention_forward/pallas_call | solution.py:275
  233.7 7.3 %collective-permute-done.34 = bf16[512,256]{1,0:T(8,128)(2,1)S(1)} collective-permute-done((bf16[512,256]{1,0:T(8,128)(2,1)S(1)}, bf16[512,256]{1,0:T(8,128)(2,1)S(1)}, u32[]{:S(2)}, u32[]{:S(2)}) %collective-permute-start.34) | collective-permute-done | bytes 262176 | tf_op jit(solution)/shard_map/ppermute | solution.py:478
  249.5 15.1 %feed_forward.4 = (f32[256,1024]{1,0:T(8,128)}, bf16[256,1024]{1,0:T(8,128)(2,1)}, f32[256,1024]{1,0:T(8,128)}, bf16[256,1024]{1,0:T(8,128)(2,1)}) custom-call(bf16[256,1024]{1,0:T(8,128)(2,1)} %add_convert_fusion.7.refs_0_, bf16[256,1024]{1,0:T(8,128)(2,1)} %collective-permute-done.36.refs_1_, f32[4,1,512]{2,1,0:T(1,128)} %reshape_squeeze.8.refs_2_, ...), custom_call_target="tpu_custom_call" | custom-call | flops 1 | bytes 1 | tf_op jit(solution)/shard_map/feed_forward/pallas_call | solution.py:395
  274.1 6.8 %collective-permute-done.40.refs_3_ = bf16[512,256]{1,0:T(8,128)(2,1)S(1)} collective-permute-done((bf16[512,256]{1,0:T(8,128)(2,1)S(1)}, bf16[512,256]{1,0:T(8,128)(2,1)S(1)}, u32[]{:S(2)}, u32[]{:S(2)}) %collective-permute-start.40) | collective-permute-done | bytes 262176 | tf_op jit(solution)/shard_map/ppermute | solution.py:478
  280.9 11.9 %attention_backward.2 = (bf16[512,768]{1,0:T(8,128)(2,1)S(1)}, bf16[512,768]{1,0:T(8,128)(2,1)S(1)}, f32[2,16,256]{2,1,0:T(8,128)S(1)}) custom-call(s32[4]{0:T(128)S(1)} %pad_add_fusion.3.order_ref, bf16[512,768]{1,0:T(8,128)(2,1)S(1)} %add_convert_fusion.1.refs_0_, bf16[512,768]{1,0:T(8,128)(2,1)S(1)} %copy-done.2, ...), custom_call_target="tpu_custom_call" | custom-call | flops 1 | bytes 1 | tf_op jit(solution)/shard_map/attention_backward/pallas_call | solution.py:303
  300.2 10.1 %collective-permute-done.42 = bf16[256,1024]{1,0:T(8,128)(2,1)S(1)} collective-permute-done((bf16[256,1024]{1,0:T(8,128)(2,1)S(1)}, bf16[256,1024]{1,0:T(8,128)(2,1)S(1)}, u32[]{:S(2)}, u32[]{:S(2)}) %collective-permute-start.42) | collective-permute-done | bytes 524320 | tf_op jit(solution)/shard_map/ppermute | solution.py:478
  311.8 5.4 %collective-permute-done.45.high_other = bf16[256,1024]{1,0:T(8,128)(2,1)S(1)} collective-permute-done((bf16[256,1024]{1,0:T(8,128)(2,1)S(1)}, bf16[256,1024]{1,0:T(8,128)(2,1)S(1)}, u32[]{:S(2)}, u32[]{:S(2)}) %collective-permute-start.45) | collective-permute-done | bytes 524320 | tf_op jit(solution)/shard_map/ppermute | solution.py:504
  319.9 12.2 %feed_forward.5 = (f32[256,1024]{1,0:T(8,128)}, bf16[256,1024]{1,0:T(8,128)(2,1)}) custom-call(bf16[256,1024]{1,0:T(8,128)(2,1)} %get-tuple-element.222.refs_1_.refs_0_, bf16[256,1024]{1,0:T(8,128)(2,1)} %get-tuple-element.107.refs_0_.refs_1_, f32[4,1,512]{2,1,0:T(1,128)} %reshape_squeeze.7.refs_2_, bf16[256,1024]{1,0:T(8,128)(2,1)} %copy-done.28, ...), custom_call_target="tpu_custom_call" | custom-call | flops 1 | bytes 1 | tf_op jit(solution)/shard_map/feed_forward/pallas_call | solution.py:395
  343.5 5.7 %collective-permute-done.50.refs_3_ = bf16[512,256]{1,0:T(8,128)(2,1)S(1)} collective-permute-done((bf16[512,256]{1,0:T(8,128)(2,1)S(1)}, bf16[512,256]{1,0:T(8,128)(2,1)S(1)}, u32[]{:S(2)}, u32[]{:S(2)}) %collective-permute-start.50) | collective-permute-done | bytes 262176 | tf_op jit(solution)/shard_map/ppermute | solution.py:478
  349.2 12.1 %attention_backward.3 = (bf16[512,768]{1,0:T(8,128)(2,1)S(1)}, bf16[512,768]{1,0:T(8,128)(2,1)S(1)}, f32[2,16,256]{2,1,0:T(8,128)S(1)}) custom-call(s32[4]{0:T(128)S(1)} %pad_add_fusion.2.order_ref, bf16[512,768]{1,0:T(8,128)(2,1)S(1)} %add_convert_fusion.3.refs_0_, bf16[512,768]{1,0:T(8,128)(2,1)S(1)} %add_convert_fusion.2.refs_1_, ...), custom_call_target="tpu_custom_call" | custom-call | flops 1 | bytes 1 | tf_op jit(solution)/shard_map/attention_backward/pallas_call | solution.py:303
  384.7 5.8 %collective-permute-done.52 = bf16[256,1024]{1,0:T(8,128)(2,1)} collective-permute-done((bf16[256,1024]{1,0:T(8,128)(2,1)}, bf16[256,1024]{1,0:T(8,128)(2,1)}, u32[]{:S(2)}, u32[]{:S(2)}) %collective-permute-start.52) | collective-permute-done | bytes 524320 | tf_op jit(solution)/shard_map/ppermute | solution.py:478
  398.7 3.8 collective-permute-start.54
  (410 shorter events, 164.5 us)
Async XLA Ops:
  1.6 17.6 %collective-permute-start.1 = (bf16[8,1024]{1,0:T(8,128)(2,1)S(1)}, bf16[8,1024]{1,0:T(8,128)(2,1)S(1)}, u32[]{:S(2)}, u32[]{:S(2)}) collective-permute-start(bf16[8,1024]{1,0:T(8,128)(2,1)S(1)} %concatenate.33), channel_id=1, source_target_pairs={{0,16},{16,0},{1,17},{17,1},{2,18},{18,2},{3,19},{19,3},{4,20},{20... | collective-permute-start | bytes 49160 | tf_op jit(solution)/shard_map/ppermute | solution.py:470
  3.6 16.3 %collective-permute-start = (bf16[256,1024]{1,0:T(8,128)(2,1)}, bf16[256,1024]{1,0:T(8,128)(2,1)}, u32[]{:S(2)}, u32[]{:S(2)}) collective-permute-start(bf16[256,1024]{1,0:T(8,128)(2,1)} %dynamic-slice_bitcast_fusion), channel_id=1, source_target_pairs={{0,18},{1,19},{2,16},{3,17},{4,22},{5,23},{6,20},{7,21},{8,26},{9,... | collective-permute-start | bytes 1572872 | tf_op jit(solution)/shard_map/ppermute | solution.py:504
  11.3 24.9 %collective-permute-start.3 = (bf16[2,256,2048]{2,1,0:T(8,128)(2,1)}, bf16[2,256,2048]{2,1,0:T(8,128)(2,1)}, u32[]{:S(2)}, u32[]{:S(2)}) collective-permute-start(bf16[2,256,2048]{2,1,0:T(8,128)(2,1)} %get-tuple-element.76), channel_id=1, source_target_pairs={{0,16},{16,0},{1,17},{17,1},{2,18},{18,2},{3,19},{19,3},{4,20},{20... | collective-permute-start | bytes 6291464 | tf_op jit(solution)/shard_map/ppermute | solution.py:470
  20.0 15.2 %collective-permute-start.7 = (bf16[256,1024]{1,0:T(8,128)(2,1)S(1)}, bf16[256,1024]{1,0:T(8,128)(2,1)S(1)}, u32[]{:S(2)}, u32[]{:S(2)}) collective-permute-start(bf16[256,1024]{1,0:T(8,128)(2,1)S(1)} %bitcast.133), channel_id=1, source_target_pairs={{0,18},{1,19},{2,16},{3,17},{16,2},{17,3},{18,0},{19,1},{4,22},{5,... | collective-permute-start | bytes 1572872 | tf_op jit(solution)/shard_map/ppermute | solution.py:487
  26.1 42.1 %collective-permute-start.6 = (bf16[1024,768]{0,1:T(8,128)(2,1)}, bf16[1024,768]{0,1:T(8,128)(2,1)}, u32[]{:S(2)}, u32[]{:S(2)}) collective-permute-start(bf16[1024,768]{0,1:T(8,128)(2,1)} %bitcast.14), channel_id=1, source_target_pairs={{0,18},{1,19},{2,16},{3,17},{16,2},{17,3},{18,0},{19,1},{4,22},{5,... | collective-permute-start | bytes 4718600 | tf_op jit(solution)/shard_map/ppermute | solution.py:487
  41.9 33.4 %collective-permute-start.4 = (bf16[256,2048]{1,0:T(8,128)(2,1)}, bf16[256,2048]{1,0:T(8,128)(2,1)}, u32[]{:S(2)}, u32[]{:S(2)}) collective-permute-start(bf16[256,2048]{1,0:T(8,128)(2,1)} %fusion.29.refs_3_.refs_5_), channel_id=1, source_target_pairs={{0,1},{1,0},{2,3},{3,2},{4,5},{5,4},{6,7},{7,6},{8,9},{9,8},{10,11... | collective-permute-start | bytes 3145736 | tf_op jit(solution)/shard_map/ppermute | solution.py:478
  78.1 30.8 %collective-permute-start.13 = (bf16[256,2048]{1,0:T(8,128)(2,1)}, bf16[256,2048]{1,0:T(8,128)(2,1)}, u32[]{:S(2)}, u32[]{:S(2)}) collective-permute-start(bf16[256,2048]{1,0:T(8,128)(2,1)} %fusion.29.refs_3_.refs_5_), channel_id=1, source_target_pairs={{0,2},{1,3},{2,0},{3,1},{4,6},{5,7},{6,4},{7,5},{8,10},{9,11},{10,... | collective-permute-start | bytes 3145736 | tf_op jit(solution)/shard_map/ppermute | solution.py:491
  78.6 30.3 %collective-permute-start.14 = (bf16[256,2048]{1,0:T(8,128)(2,1)}, bf16[256,2048]{1,0:T(8,128)(2,1)}, u32[]{:S(2)}, u32[]{:S(2)}) collective-permute-start(bf16[256,2048]{1,0:T(8,128)(2,1)} %get-tuple-element.102.refs_5_), channel_id=1, source_target_pairs={{0,1},{1,0},{2,3},{3,2},{4,5},{5,4},{6,7},{7,6},{8,9},{9,8},{10,11... | collective-permute-start | bytes 3145736 | tf_op jit(solution)/shard_map/ppermute | solution.py:478
  78.7 30.2 %collective-permute-start.15 = (bf16[256,2048]{1,0:T(8,128)(2,1)}, bf16[256,2048]{1,0:T(8,128)(2,1)}, u32[]{:S(2)}, u32[]{:S(2)}) collective-permute-start(bf16[256,2048]{1,0:T(8,128)(2,1)} %collective-permute-done.4.refs_7_.refs_9_), channel_id=1, source_target_pairs={{0,4},{4,0},{8,12},{12,8},{1,5},{5,1},{9,13},{13,9},{2,6},{6,2},{1... | collective-permute-start | bytes 3145736 | tf_op jit(solution)/shard_map/ppermute | solution.py:496
  83.0 25.9 %collective-permute-start.8 = (bf16[256,1024]{1,0:T(8,128)(2,1)}, bf16[256,1024]{1,0:T(8,128)(2,1)S(1)}, u32[]{:S(2)}, u32[]{:S(2)}) collective-permute-start(bf16[256,1024]{1,0:T(8,128)(2,1)} %dynamic-slice_bitcast_fusion), channel_id=1, source_target_pairs={{16,2},{17,3},{18,0},{19,1},{20,6},{21,7},{22,4},{23,5},{24,10},{2... | collective-permute-start | bytes 1572872 | tf_op jit(solution)/shard_map/ppermute | solution.py:504
  111.3 36.2 %collective-permute-start.20 = (bf16[256,2048]{1,0:T(8,128)(2,1)}, bf16[256,2048]{1,0:T(8,128)(2,1)}, u32[]{:S(2)}, u32[]{:S(2)}) collective-permute-start(bf16[256,2048]{1,0:T(8,128)(2,1)} %collective-permute-done.13.refs_5_.refs_7_), channel_id=1, source_target_pairs={{0,1},{1,0},{2,3},{3,2},{4,5},{5,4},{6,7},{7,6},{8,9},{9,8},{10,11... | collective-permute-start | bytes 3145736 | tf_op jit(solution)/shard_map/ppermute | solution.py:478
  111.4 36.1 %collective-permute-start.21 = (bf16[256,2048]{1,0:T(8,128)(2,1)}, bf16[256,2048]{1,0:T(8,128)(2,1)}, u32[]{:S(2)}, u32[]{:S(2)}) collective-permute-start(bf16[256,2048]{1,0:T(8,128)(2,1)} %get-tuple-element.102.refs_5_), channel_id=1, source_target_pairs={{0,2},{1,3},{2,0},{3,1},{4,6},{5,7},{6,4},{7,5},{8,10},{9,11},{10,... | collective-permute-start | bytes 3145736 | tf_op jit(solution)/shard_map/ppermute | solution.py:491
  112.6 35.0 %collective-permute-start.22 = (bf16[256,2048]{1,0:T(8,128)(2,1)}, bf16[256,2048]{1,0:T(8,128)(2,1)}, u32[]{:S(2)}, u32[]{:S(2)}) collective-permute-start(bf16[256,2048]{1,0:T(8,128)(2,1)} %collective-permute-done.14.refs_9_), channel_id=1, source_target_pairs={{0,4},{4,0},{8,12},{12,8},{1,5},{5,1},{9,13},{13,9},{2,6},{6,2},{1... | collective-permute-start | bytes 3145736 | tf_op jit(solution)/shard_map/ppermute | solution.py:496
  114.1 33.5 %collective-permute-start.17 = (bf16[256,1024]{1,0:T(8,128)(2,1)S(1)}, bf16[256,1024]{1,0:T(8,128)(2,1)S(1)}, u32[]{:S(2)}, u32[]{:S(2)}) collective-permute-start(bf16[256,1024]{1,0:T(8,128)(2,1)S(1)} %add_convert_fusion.11), channel_id=1, source_target_pairs={{0,1},{1,0},{2,3},{3,2},{4,5},{5,4},{6,7},{7,6},{8,9},{9,8},{10,11... | collective-permute-start | bytes 1572872 | tf_op jit(solution)/shard_map/ppermute | solution.py:478
  115.8 34.3 %collective-permute-start.18 = (bf16[256,1024]{1,0:T(8,128)(2,1)S(1)}, bf16[256,1024]{1,0:T(8,128)(2,1)S(1)}, u32[]{:S(2)}, u32[]{:S(2)}) collective-permute-start(bf16[256,1024]{1,0:T(8,128)(2,1)S(1)} %slice.237), channel_id=1, source_target_pairs={{0,16},{16,0},{1,17},{17,1},{2,18},{18,2},{3,19},{19,3},{4,20},{20... | collective-permute-start | bytes 1572872 | tf_op jit(solution)/shard_map/ppermute | solution.py:470
  147.5 24.2 %collective-permute-start.23 = (bf16[256,2048]{1,0:T(8,128)(2,1)}, bf16[256,2048]{1,0:T(8,128)(2,1)}, u32[]{:S(2)}, u32[]{:S(2)}) collective-permute-start(bf16[256,2048]{1,0:T(8,128)(2,1)} %get-tuple-element.104.refs_4_.refs_6_), channel_id=1, source_target_pairs={{0,2},{1,3},{2,0},{3,1},{4,6},{5,7},{6,4},{7,5},{8,10},{9,11},{10,... | collective-permute-start | bytes 3145736 | tf_op jit(solution)/shard_map/ppermute | solution.py:491
  148.6 23.8 %collective-permute-start.24 = (bf16[256,2048]{1,0:T(8,128)(2,1)}, bf16[256,2048]{1,0:T(8,128)(2,1)}, u32[]{:S(2)}, u32[]{:S(2)}) collective-permute-start(bf16[256,2048]{1,0:T(8,128)(2,1)} %collective-permute-done.20.refs_9_.refs_11_), channel_id=1, source_target_pairs={{0,4},{4,0},{8,12},{12,8},{1,5},{5,1},{9,13},{13,9},{2,6},{6,2},{1... | collective-permute-start | bytes 3145736 | tf_op jit(solution)/shard_map/ppermute | solution.py:496
  149.8 23.6 %collective-permute-start.25 = (bf16[256,2048]{1,0:T(8,128)(2,1)}, bf16[256,2048]{1,0:T(8,128)(2,1)}, u32[]{:S(2)}, u32[]{:S(2)}) collective-permute-start(bf16[256,2048]{1,0:T(8,128)(2,1)} %collective-permute-done.21.refs_7_), channel_id=1, source_target_pairs={{0,1},{1,0},{2,3},{3,2},{4,5},{5,4},{6,7},{7,6},{8,9},{9,8},{10,11... | collective-permute-start | bytes 3145736 | tf_op jit(solution)/shard_map/ppermute | solution.py:478
  151.4 22.8 %collective-permute-start.19 = (f32[256,1024]{1,0:T(8,128)}, f32[256,1024]{1,0:T(8,128)}, u32[]{:S(2)}, u32[]{:S(2)}) collective-permute-start(f32[256,1024]{1,0:T(8,128)} %get-tuple-element.179), channel_id=1, source_target_pairs={{0,16},{16,0},{1,17},{17,1},{2,18},{18,2},{3,19},{19,3},{4,20},{20... | collective-permute-start | bytes 3145736 | tf_op jit(solution)/shard_map/ppermute | solution.py:470
  173.4 25.7 %collective-permute-start.26 = (bf16[256,2048]{1,0:T(8,128)(2,1)}, bf16[256,2048]{1,0:T(8,128)(2,1)}, u32[]{:S(2)}, u32[]{:S(2)}) collective-permute-start(bf16[256,2048]{1,0:T(8,128)(2,1)} %get-tuple-element.110.refs_6_), channel_id=1, source_target_pairs={{0,2},{1,3},{2,0},{3,1},{4,6},{5,7},{6,4},{7,5},{8,10},{9,11},{10,... | collective-permute-start | bytes 3145736 | tf_op jit(solution)/shard_map/ppermute | solution.py:491
  173.9 25.2 %collective-permute-start.27 = (bf16[256,2048]{1,0:T(8,128)(2,1)}, bf16[256,2048]{1,0:T(8,128)(2,1)}, u32[]{:S(2)}, u32[]{:S(2)}) collective-permute-start(bf16[256,2048]{1,0:T(8,128)(2,1)} %collective-permute-done.25.refs_11_), channel_id=1, source_target_pairs={{0,4},{4,0},{8,12},{12,8},{1,5},{5,1},{9,13},{13,9},{2,6},{6,2},{1... | collective-permute-start | bytes 3145736 | tf_op jit(solution)/shard_map/ppermute | solution.py:496
  177.4 21.7 %collective-permute-start.29 = (bf16[256,1024]{1,0:T(8,128)(2,1)}, bf16[256,1024]{1,0:T(8,128)(2,1)S(1)}, u32[]{:S(2)}, u32[]{:S(2)}) collective-permute-start(bf16[256,1024]{1,0:T(8,128)(2,1)} %get-tuple-element.113), channel_id=1, source_target_pairs={{0,1},{1,0},{2,3},{3,2},{4,5},{5,4},{6,7},{7,6},{8,9},{9,8},{10,11... | collective-permute-start | bytes 1572872 | tf_op jit(solution)/shard_map/ppermute | solution.py:478
  298.9 18.3 %collective-permute-start.45 = (bf16[256,1024]{1,0:T(8,128)(2,1)S(1)}, bf16[256,1024]{1,0:T(8,128)(2,1)S(1)}, u32[]{:S(2)}, u32[]{:S(2)}) collective-permute-start(bf16[256,1024]{1,0:T(8,128)(2,1)S(1)} %get-tuple-element.187.high_own), channel_id=1, source_target_pairs={{0,18},{1,19},{2,16},{3,17},{4,22},{5,23},{6,20},{7,21},{8,26},{9,... | collective-permute-start | bytes 1572872 | tf_op jit(solution)/shard_map/ppermute | solution.py:504
  375.2 16.1 %collective-permute-start.53 = (bf16[256,1024]{1,0:T(8,128)(2,1)}, bf16[256,1024]{1,0:T(8,128)(2,1)}, u32[]{:S(2)}, u32[]{:S(2)}) collective-permute-start(bf16[256,1024]{1,0:T(8,128)(2,1)} %slice.259), channel_id=1, source_target_pairs={{0,16},{16,0},{1,17},{17,1},{2,18},{18,2},{3,19},{19,3},{4,20},{20... | collective-permute-start | bytes 1572872 | tf_op jit(solution)/shard_map/ppermute | solution.py:470
  (120 other events, 1467.2 us)

commit v3 on v2

--- a/solution.py
+++ b/solution.py
@@ -233,31 +233,44 @@
     if with_grad:
         grad_ref[0:tokens, :] = grad_own[...]
         grad_ref[tokens:, :] = grad_peer[...]
-    for group in range(groups):
-        span = slice(group * hidden, (group + 1) * hidden)
-        for copy in copies_of(group):
-            copy.wait()
-        if group + 2 < groups:
-            for copy in copies_of(group + 2):
-                copy.start()
+    @pl.loop(0, groups)
+    def _(group):
+        for part in range(per):
+            pltpu.make_async_copy(
+                chunk_refs[0], weight_ref.at[pl.ds(0, rows)], sems.at[group, part]
+            ).wait()
+        for later in range(2, groups):
+
+            @pl.when(group == later - 2)
+            def _():
+                for copy in copies_of(later):
+                    copy.start()
+
+        span = pl.ds(pl.multiple_of(group * hidden, hidden), hidden)
         pre = dot_nt(normed_ref[...], weight_ref[span, 0:width]) + bias_ref[group]
         square, curve, root = gelu_parts(pre)
         if with_output:
-            hidden_ref[:, span] = (0.5 * pre * (1.0 + curve)).astype(bf16)
+            hidden_ref[group] = (0.5 * pre * (1.0 + curve)).astype(bf16)
         if with_grad:
             slope = 0.5 * (1.0 + curve) + 0.5 * pre * (1.0 - curve * curve) * (
                 root * (1.0 + 3 * 0.044715 * square)
             )
-            back_ref[:, span] = (dot_nt(grad_ref[...], weight_ref[span, width:]) * slope).astype(bf16)
+            back_ref[group] = (dot_nt(grad_ref[...], weight_ref[span, width:]) * slope).astype(bf16)
+
+    def summed(values_ref, columns):
+        return sum(
+            dot_nn(values_ref[group], weight_ref[group * hidden : (group + 1) * hidden, columns])
+            for group in range(groups)
+        )
 
     for at in range(0, width, block):
         span = slice(at, at + block)
         if with_output:
-            total = dot_nn(hidden_ref[...], weight_ref[:, width + at : width + at + block])
+            total = summed(hidden_ref, slice(width + at, width + at + block))
             out_own[:, span] = total[0:tokens]
             out_peer[:, span] = total[tokens:].astype(bf16)
         if with_grad:
-            total = dot_nn(back_ref[...], weight_ref[:, span])
+            total = summed(back_ref, span)
             back_own[:, span] = total[0:tokens]
             back_peer[:, span] = total[tokens:].astype(bf16)
 
@@ -406,13 +419,70 @@
             pltpu.SemaphoreType.DMA((groups, per)),
             pltpu.VMEM((2 * tokens, width), bf16),
             pltpu.VMEM((2 * tokens, width) if with_grad else small, bf16),
-            pltpu.VMEM((2 * tokens, groups * hidden) if with_output else small, bf16),
-            pltpu.VMEM((2 * tokens, groups * hidden) if with_grad else small, bf16),
+            pltpu.VMEM((groups, 2 * tokens, hidden) if with_output else small, bf16),
+            pltpu.VMEM((groups, 2 * tokens, hidden) if with_grad else small, bf16),
         ],
         compiler_params=pltpu.CompilerParams(vmem_limit_bytes=58 << 20),
         cost_estimate=small_cost,
         name="feed_forward",
     )(*normed, bias, *(grads if with_grad else ()), *chunks)
+
+
+def dot_tn(a, b):
+    return lax.dot_general(a, b, (((0,), (0,)), ((), ())), preferred_element_type=f32)
+
+
+def second_grad_kernel(head_dim, kept_ref, came_ref, hidden_ref, w2_ref, b2_ref):
+    grad = (kept_ref[...] + came_ref[...]).astype(bf16)
+    heads = w2_ref.shape[1]
+    for head in range(heads):
+        columns = [
+            grad[:, (heads * side + head) * head_dim : (heads * side + head + 1) * head_dim]
+            for side in range(2)
+        ]
+        block = jnp.concatenate(columns, axis=1)
+        w2_ref[:, head, :] = dot_tn(hidden_ref[...], block)
+        b2_ref[head : head + 1, :] = jnp.sum(block.astype(f32), axis=0, keepdims=True)
+
+
+def second_grads(kept, came, hidden, heads):
+    head_dim = kept.shape[1] // (2 * heads)
+    return pl.pallas_call(
+        functools.partial(second_grad_kernel, head_dim),
+        out_shape=[
+            jax.ShapeDtypeStruct((hidden.shape[1], heads, 2 * head_dim), f32),
+            jax.ShapeDtypeStruct((heads, 2 * head_dim), f32),
+        ],
+        in_specs=[whole()] * 3,
+        out_specs=[whole()] * 2,
+        compiler_params=pltpu.CompilerParams(vmem_limit_bytes=8 << 20),
+        cost_estimate=small_cost,
+        name="second_grads",
+    )(kept, came, hidden)
+
+
+def first_grad_kernel(grad_ref, curve_ref, embed_ref, w1_ref, embed_out, w1_out, b1_out):
+    curve = curve_ref[...]
+    grad = (grad_ref[...] * (1.0 - curve * curve)).astype(bf16)
+    w1_out[...] = dot_tn(embed_ref[...], grad)
+    b1_out[...] = jnp.sum(grad.astype(f32), axis=0, keepdims=True)
+    embed_out[...] = dot_nt(grad, w1_ref[...])[: embed_out.shape[0]]
+
+
+def first_grads(grad, curve, embed, w1, prefix_len):
+    return pl.pallas_call(
+        first_grad_kernel,
+        out_shape=[
+            jax.ShapeDtypeStruct((prefix_len, embed.shape[1]), f32),
+            jax.ShapeDtypeStruct(w1.shape, f32),
+            jax.ShapeDtypeStruct((1, w1.shape[1]), f32),
+        ],
+        in_specs=[whole()] * 4,
+        out_specs=[whole()] * 3,
+        compiler_params=pltpu.CompilerParams(vmem_limit_bytes=12 << 20),
+        cost_estimate=small_cost,
+        name="first_grads",
+    )(grad, curve, embed, w1)
 
 
 def place_kernel(spot_ref, low_own, low_other, high_own, high_other, out_ref):
@@ -507,20 +577,27 @@
         planes = lax.axis_size("dp")
         if planes & (planes - 1):
             return lax.psum(value, "dp")
-        distance = 1
+        step = min(planes, 4)
+        value = sum([value] + [self.plane_swap(value, distance) for distance in range(1, step)])
+        distance = step
         while distance < planes:
             value = value + self.plane_swap(value, distance)
             distance *= 2
         return value
 
+    def tensor_swap(self, value, distance):
+        pairs = [(place, place ^ distance) for place in range(self.size)]
+        return lax.ppermute(value, "tensor", pairs)
+
     def sum_shards(self, value):
         if self.size & (self.size - 1):
             return lax.psum(value, ("section", "tensor"))
         value = value + self.core_swap(value)
-        distance = 1
+        step = min(self.size, 4)
+        value = sum([value] + [self.tensor_swap(value, distance) for distance in range(1, step)])
+        distance = step
         while distance < self.size:
-            pairs = [(place, place ^ distance) for place in range(self.size)]
-            value = value + lax.ppermute(value, "tensor", pairs)
+            value = value + self.tensor_swap(value, distance)
             distance *= 2
         return value
 
@@ -541,12 +618,14 @@
         total = None
         for distance in list(range(1, self.count)) + [0]:
             own, other = (parts[distance][:rows], parts[distance][rows:])
-            summed = own.astype(f32) + self.core_swap(other).astype(f32)
+            if total is not None:
+                other = lax.optimization_barrier((other, leaving))[0]
+            self.swapped = self.core_swap(other)
+            summed = own.astype(f32) + self.swapped.astype(f32)
             if distance:
                 back = functools.partial(self.shift, distance=-distance)
-                self.leaving = summed.astype(bf16)
-                self.arrived = stages.send(back, self.leaving)
-                summed = self.arrived.astype(f32)
+                leaving = summed.astype(bf16)
+                summed = stages.send(back, leaving).astype(f32)
             total = summed if total is None else total + summed
         return total
 
@@ -640,7 +719,7 @@
     shared = lax.axis_size("dp") % 2 == 0
     parity = lax.axis_index("dp") % 2
     spot = jnp.stack([core, parity]).astype(jnp.int32)
-    keep, give = feed_forward_chunks(spot, w_up[0], w_down[0])
+    keep, give = feed_forward_chunks(tied(spot, other_row), w_up[0], w_down[0])
     handed = group.core_swap(give)
     even_0 = jnp.where(low, keep[0], handed[0])
     later_keep, later_handed, _ = lax.optimization_barrier((keep, handed, even_0))
@@ -682,26 +761,22 @@
     def half_send(value):
         return stages.send(group.half_swap, value)
 
+    def far(value, layer):
+        return stages.send(functools.partial(group.cross_from, core=layer), value)
+
+    side_bias = small_chip[:, 6, : w_up.shape[2]]
+    side_bias = jnp.stack([side_bias] + group.shifts(stages, side_bias), axis=1)
+
     stages.next()
+    half_bias = half_send(side_bias)
     normed_0 = normed_one(0, inputs)
     gathered_0 = [normed_0] + group.shifts(stages, normed_0)
     side_even_0 = group.shifts(stages, tied(even[0], *gathered_0[1:]))
-    small_half = half_send(small_chip)
-    qkv_far = stages.send(group.cross, qkv_own)
-    proj_far = stages.send(group.cross, proj_own)
+    qkv_far = stages.send(group.cross, tied(qkv_own, half_bias))
 
     stages.next()
-    came_grad = stages.send(functools.partial(group.cross_from, core=1), other_row)
-    cotangent = jnp.where(low, came_grad, own_row)
-    qkv = layer_pair(qkv_own, qkv_far)
-    projs = layer_pair(proj_own, proj_far)
     pairs = layer_pair(pairs_own, stages.send(group.cross, pairs_own))
-    up_bias = jnp.stack([small_chip[:, 6, :hidden_width], small_half[:, 6, :hidden_width]], axis=1)
-    up_bias = jnp.stack([up_bias] + group.shifts(stages, up_bias), axis=1).astype(f32)
-    up_bias = up_bias.reshape(2, 2 * count, 2, 2, rows)
-    up_bias = jnp.where(low, up_bias[:, :, 0], up_bias[:, :, 1])
-    up_bias = jnp.where(parity == 0, up_bias, up_bias[:, :, ::-1])
-    up_bias = up_bias.reshape(2, 4 * count, rows)
+    proj_far_0 = far(proj_own, 0)
     half_even_0 = half_send(even[0])
     side_even_1 = group.shifts(stages, even[1])
     if shared:
@@ -730,15 +805,14 @@
     ]
 
     class Layer:
-        def __init__(self, index):
+        def __init__(self, index, qkv):
             self.vectors = vectors_of(index)
             self.ln1_gain, self.ln1_bias, self.b_out = [self.vectors[at : at + 1] for at in range(3)]
-            shard = tied(pairs[index], up_bias)
+            shard = pairs[index]
             self.pairs = shard[: 2 * prefix_rows, :head_width].reshape(2, prefix_rows, head_width)
             self.b_qkv = shard[2 * prefix_rows : 2 * prefix_rows + 1, : 3 * head_width].astype(f32)
             self.order = orders[index]
-            self.qkv, self.out = (tied(qkv[index], *stages.before), projs[index])
-            self.bias = up_bias[index]
+            self.qkv = tied(qkv, *stages.before)
 
         def attention(self, inputs, gathered):
             self.inputs = inputs
@@ -753,6 +827,8 @@
 
         def project(self):
             context = lax.optimization_barrier((*self.context, *stages.before))[:count]
+            own, far_own = lax.optimization_barrier((*self.far_out, *self.context))[:2]
+            self.out = jnp.where(low, own, far_own)
             parts = [dot_nn(part, self.out).astype(bf16) for part in context]
             self.middle = self.inputs + (group.scatter(stages, parts) + self.b_out)
 
@@ -797,12 +873,15 @@
             grad_in = grad_middle + norm_back(self.inputs, self.ln1_gain, grad_normed)
             return (grad_in.astype(bf16), grad_pairs)
 
-    layer_0 = Layer(0)
+    pack_own = jnp.concatenate([proj_own, other_row], axis=0)
+    layer_0 = Layer(0, tied(jnp.where(low, qkv_own, qkv_far), pack_own))
+    layer_0.far_out = (proj_own, proj_far_0)
     layer_0.attention(inputs, gathered_0)
 
     stages.next()
     corner_even_0 = group.shifts(stages, half_even_0)
     half_even_1 = half_send(even[1])
+    far_pack = far(pack_own, 1)
     if shared:
         side_odd_1 = [plane_send(value) for value in side_even_1]
     else:
@@ -816,6 +895,12 @@
     else:
         corner_odd_0 = group.shifts(stages, half_odd_0)
     corner_even_1 = group.shifts(stages, half_even_1)
+    up_bias = jnp.stack([side_bias, half_bias], axis=2).astype(f32)
+    up_bias = up_bias.reshape(2, 2 * count, 2, 2, rows)
+    up_bias = jnp.where(low, up_bias[:, :, 0], up_bias[:, :, 1])
+    up_bias = jnp.where(parity == 0, up_bias, up_bias[:, :, ::-1])
+    up_bias = up_bias.reshape(2, 4 * count, rows)
+    layer_0.bias = up_bias[0]
     layer_0.chunks = all_chunks(
         0,
         (half_even_0, half_odd_0),
@@ -827,6 +912,10 @@
 
     stages.next()
     half_odd_1 = half_send(odd[1])
+    own_proj, far_pack = lax.optimization_barrier((proj_own, far_pack, *stages.before))[:2]
+    cotangent = jnp.where(low, far_pack[head_width:], own_row)
+    proj_1 = jnp.where(low, far_pack[:head_width], own_proj)
+    projs = (layer_0.out, proj_1)
     if shared:
         corner_odd_1 = [plane_send(value) for value in corner_even_1]
     else:
@@ -841,8 +930,11 @@
     inputs_1 = first_out.astype(f32)
     normed_1 = normed_one(1, inputs_1)
     gathered_1 = [normed_1] + group.shifts(stages, normed_1)
-    layer_1 = Layer(1)
+    w2_far = group.cross(tied(w2_own, first_out))
+    layer_1 = Layer(1, jnp.where(low, *lax.optimization_barrier((qkv_far, qkv_own, w2_far))[:2]))
     layer_0.out_side, layer_1.out_side = out_sides
+    layer_1.out = proj_1
+    layer_1.bias = up_bias[1]
     layer_1.attention(inputs_1, gathered_1)
     layer_1.chunks = all_chunks(
         1,
@@ -852,7 +944,6 @@
     )
 
     stages.next()
-    w2_far = stages.send(group.cross, w2_own)
     w2_side = layer_pair(w2_own, w2_far)
     layer_1.project_here()
     normed = layer_1.norm_two(layer_1.middle)
@@ -863,7 +954,7 @@
     grad_middle = layer_1.middle_back(cotangent, parts[2:])
     mid_grad, grad_pairs_one = layer_1.backward(grad_middle)
     high_other = group.cross_from(last_out, 0)
-    mid_grad = tied(mid_grad, high_other, w2_far)
+    mid_grad = tied(mid_grad, high_other)
     mid_peer = group.core_swap(mid_grad)
     back_part = layer_0.feed_forward(normed_pair, (mid_peer, mid_grad), False)
     grad_middle = layer_0.middle_back(mid_peer, back_part)
@@ -888,30 +979,27 @@
         for grad, side in zip(grads, w2_side)
     )
     kept, sent = layer_pair(*grads)
-    summed = tied(jnp.concatenate([hidden_part, kept, sent], axis=1), group.leaving)
+    message = jnp.concatenate([hidden_part, kept, sent], axis=1)
+    summed = tied(message, group.swapped)
     summed = group.sum_planes(summed)
     hidden_width = hidden_part.shape[1]
-    hidden_part = tied(summed[:, :hidden_width], group.arrived)
-    hidden_grad = group.sum_shards(hidden_part)[:prefix_len]
+    hidden_part = summed[:, :hidden_width]
+    hidden_grad = group.sum_shards(hidden_part)
     kept = summed[:, hidden_width : hidden_width + 2 * head_width]
     sent = summed[:, hidden_width + 2 * head_width :]
-    grad_low = (kept + group.cross(sent))[:prefix_len].astype(bf16)
-    grad_flat = (
-        grad_low.reshape(prefix_len, 2, heads_local, head_dim)
-        .transpose(0, 2, 1, 3)
-        .reshape(prefix_len, 2 * head_width)
-    )
-    w2_grad = lax.dot_general(
-        hidden_low, grad_flat, (((0,), (0,)), ((), ())), preferred_element_type=f32
-    ).reshape(reparam_w2.shape)
-    b2_grad = jnp.sum(grad_flat.astype(f32), axis=0).reshape(reparam_b2.shape)
-    pre_grad = (hidden_grad * (1.0 - curve * curve)).astype(bf16)
-    w1_grad = lax.dot_general(
-        prefix_embed, pre_grad, (((0,), (0,)), ((), ())), preferred_element_type=f32
-    )
-    b1_grad = jnp.sum(pre_grad.astype(f32), axis=0)
-    embed_grad = dot_nt(pre_grad, reparam_w1)
-    return (boundary_result, embed_grad, w1_grad, b1_grad, w2_grad, b2_grad)
+    pad = ((0, prefix_rows - prefix_len), (0, 0))
+    w2_grad, b2_grad = second_grads(kept, group.cross(sent), jnp.pad(hidden_low, pad), heads_local)
+    embed_grad, w1_grad, b1_grad = first_grads(
+        hidden_grad, jnp.pad(curve, pad), jnp.pad(prefix_embed, pad), reparam_w1, prefix_len
+    )
+    return (
+        boundary_result,
+        embed_grad,
+        w1_grad,
+        b1_grad.reshape(reparam_b1.shape),
+        w2_grad.reshape(reparam_w2.shape),
+        b2_grad.reshape(reparam_b2.shape),
+    )
 
 
 def solution(mesh):

time: 418 us -> 398 us (0.952)
  waiting for transfers between devices: 176 us -> 167 us
  local copies, waits for them, and re-layouts: 25.9 us -> 18.8 us
  Pallas kernels: 82.1 us -> 87.6 us
    ppermute x5 -> x4, waiting for transfers between devices: 37.7 us -> 16.3 us  [cross(): return lax.ppermute(value, ('section', 'tensor'), pairs)]
    ppermute x15, waiting for transfers between devices: 87.6 us -> 93.4 us  [shift(): return lax.ppermute(value, 'tensor', pairs)]
    select_n x4 -> x2, other arithmetic: 5.62 us -> 0.04 us  [layer_pair(): return (jnp.where(low, own, far), jnp.where(low, far, own))]
    select_n x1 -> x4, other arithmetic: 0.89 us -> 6.1 us  [the longest x1 2.42 us: local(): cotangent = jnp.where(low, far_pack[head_width:], own_row)]
    ppermute x2 -> x3, waiting for transfers between devices: 1.56 us -> 6.35 us  [tensor_swap(): return lax.ppermute(value, 'tensor', pairs)]
    unnamed x168 -> x105, local copies, waits for them, and re-layouts: 11.4 us -> 7.98 us
    ppermute x4 -> x5, waiting for transfers between devices: 14.9 us -> 16.3 us  [cross_from(): return lax.ppermute(value, ('section', 'tensor'), pairs)]
    ppermute x4 -> x5, starting transfers between devices: 9.91 us -> 11.1 us  [cross_from(): return lax.ppermute(value, ('section', 'tensor'), pairs)]
  transfers between devices with their start and end apart: 61 -> 63, of which waited for: 31 -> 30; matrix products, arithmetic and copies ran while one was open for 16% -> 12% of each run, Pallas kernels for 5% -> 6%
where the time goes in v3:
time: 398 us; the launch traced here: 393 us
  waiting for transfers between devices  167 us (42%)
  Pallas kernels  87.6 us (22%)
  starting transfers between devices  61.3 us (15%)
  other arithmetic  40.5 us (10%)
  local copies, waits for them, and re-layouts  18.8 us (5%)
  matrix products  16 us (4%)
    ppermute x15, waiting for transfers between devices, shift(): return lax.ppermute(value, 'tensor', pairs)  93.4 us
    pallas_call x3, Pallas kernels, feed_forward(): pl.pallas_call(functools.partial(feed_forward_kernel, groups, per, with_o...  39.1 us
    pallas_call x2, Pallas kernels, attention_backward(): pl.pallas_call(functools.partial(attention_backward_kernel, count, block_...  24.2 us
    ppermute x24, starting transfers between devices, core_swap(): return lax.ppermute(value, 'section', [(0, 1), (1, 0)])  21.7 us
    ppermute x5, waiting for transfers between devices, half_swap(): return lax.ppermute(value, 'tensor', pairs)  18.9 us
    ppermute x5, waiting for transfers between devices, cross_from(): return lax.ppermute(value, ('section', 'tensor'), pairs)  16.3 us
    ppermute x4, waiting for transfers between devices, cross(): return lax.ppermute(value, ('section', 'tensor'), pairs)  16.3 us
    pallas_call x2, Pallas kernels, attention_forward(): pl.pallas_call(functools.partial(attention_forward_kernel, count, block_r...  16 us
  transfers between devices with their start and end apart: 63, of which 30 were waited for; matrix products, arithmetic and copies ran while one was open for 12% of the time, Pallas kernels for 6%

profile of v3, /device:TPU:1, one launch (start us, length us, event | category | flops | bytes accessed | tf_op | source)
XLA Modules:
  0.0 393.2 jit_solution(1186499598084329865)
XLA Ops:
  8.0 3.2 feed_forward_chunks.1
  11.2 4.6 %collective-permute-start = (bf16[2,256,2048]{2,1,0:T(8,128)(2,1)}, bf16[2,256,2048]{2,1,0:T(8,128)(2,1)}, u32[]{:S(2)}, u32[]{:S(2)}) collective-permute-start(bf16[2,256,2048]{2,1,0:T(8,128)(2,1)} %get-tuple-element.89), channel_id=1, source_target_pairs={{0,16},{16,0},{1,17},{17,1},{2,18},{18,2},{3,19},{19,3},{4,20},{20... | collective-permute-start | bytes 6291464 | tf_op jit(solution)/shard_map/ppermute | solution.py:540
  31.6 7.7 %collective-permute-done.5 = bf16[256,1024]{1,0:T(8,128)(2,1)S(1)} collective-permute-done((bf16[256,1024]{1,0:T(8,128)(2,1)S(1)}, bf16[256,1024]{1,0:T(8,128)(2,1)S(1)}, u32[]{:S(2)}, u32[]{:S(2)}) %collective-permute-start.5) | collective-permute-done | bytes 524320 | tf_op jit(solution)/shard_map/ppermute | solution.py:548
  45.6 3.5 select_bitcast_fusion
  49.1 15.1 %collective-permute-done.7 = bf16[1024,768]{0,1:T(8,128)(2,1)} collective-permute-done((bf16[1024,768]{0,1:T(8,128)(2,1)}, bf16[1024,768]{0,1:T(8,128)(2,1)}, u32[]{:S(2)}, u32[]{:S(2)}) %collective-permute-start.7) | collective-permute-done | bytes 1572896 | tf_op jit(solution)/shard_map/ppermute | solution.py:557
  75.7 8.0 %attention_forward.2 = (bf16[512,256]{1,0:T(8,128)(2,1)S(1)}, bf16[512,256]{1,0:T(8,128)(2,1)S(1)}, f32[8,1024]{1,0:T(8,128)S(1)}) custom-call(s32[4]{0:T(128)S(1)} %pad_add_fusion.2.order_ref, bf16[512,768]{1,0:T(8,128)(2,1)S(1)} %add_convert_fusion.3.refs_0_, bf16[512,768]{1,0:T(8,128)(2,1)S(1)} %add_convert_fusion.2.refs_1_, ...), custom_call_target="tpu_custom_call" | custom-call | flops 1 | bytes 1 | tf_op jit(solution)/shard_map/attention_forward/pallas_call | solution.py:288
  83.7 16.3 %collective-permute-done.9 = bf16[256,1024]{1,0:T(8,128)(2,1)S(1)} collective-permute-done((bf16[256,1024]{1,0:T(8,128)(2,1)S(1)}, bf16[256,1024]{1,0:T(8,128)(2,1)S(1)}, u32[]{:S(2)}, u32[]{:S(2)}) %collective-permute-start.9) | collective-permute-done | bytes 524320 | tf_op jit(solution)/shard_map/ppermute | solution.py:574
  105.1 5.0 %collective-permute-start.13 = (bf16[512,1024]{1,0:T(8,128)(2,1)}, bf16[512,1024]{1,0:T(8,128)(2,1)}, u32[]{:S(2)}, u32[]{:S(2)}) collective-permute-start(bf16[512,1024]{1,0:T(8,128)(2,1)} %pad_maximum_fusion), channel_id=1, source_target_pairs={{16,2},{17,3},{18,0},{19,1},{20,6},{21,7},{22,4},{23,5},{24,10},{2... | collective-permute-start | bytes 3145736 | tf_op jit(solution)/shard_map/ppermute | solution.py:574
  112.7 26.9 %collective-permute-done.20 = bf16[256,1024]{1,0:T(8,128)(2,1)} collective-permute-done((bf16[256,1024]{1,0:T(8,128)(2,1)}, bf16[256,1024]{1,0:T(8,128)(2,1)}, u32[]{:S(2)}, u32[]{:S(2)}) %collective-permute-start.20) | collective-permute-done | bytes 524320 | tf_op jit(solution)/shard_map/ppermute | solution.py:548
  149.8 18.8 %collective-permute-done.21.refs_6_.refs_8_ = bf16[256,2048]{1,0:T(8,128)(2,1)} collective-permute-done((bf16[256,2048]{1,0:T(8,128)(2,1)}, bf16[256,2048]{1,0:T(8,128)(2,1)}, u32[]{:S(2)}, u32[]{:S(2)}) %collective-permute-start.21) | collective-permute-done | bytes 1048608 | tf_op jit(solution)/shard_map/ppermute | solution.py:561
  179.5 10.5 %feed_forward.3 = (f32[256,1024]{1,0:T(8,128)}, bf16[256,1024]{1,0:T(8,128)(2,1)}) custom-call(bf16[256,1024]{1,0:T(8,128)(2,1)} %get-tuple-element.125.refs_0_.refs_1_, bf16[256,1024]{1,0:T(8,128)(2,1)} %get-tuple-element.244.refs_1_.refs_0_, f32[4,1,512]{2,1,0:T(1,128)} %reshape_squeeze.7.refs_2_, bf16[256,2048]{1,0:T(8,128)(2,1)} %fusion.29.refs_3_.refs_5_, ...), custom_call_target="tpu_custom_call" | custom-call | flops 1 | bytes 1 | tf_op jit(solution)/shard_map/feed_forward/pallas_call | solution.py:408
  190.0 5.5 %collective-permute-done.29 = bf16[256,1024]{1,0:T(8,128)(2,1)} collective-permute-done((bf16[256,1024]{1,0:T(8,128)(2,1)S(1)}, bf16[256,1024]{1,0:T(8,128)(2,1)}, u32[]{:S(2)}, u32[]{:S(2)}) %collective-permute-start.29) | collective-permute-done | bytes 524320 | tf_op jit(solution)/shard_map/ppermute | solution.py:548
  204.8 11.1 %collective-permute-done.31 = bf16[256,1024]{1,0:T(8,128)(2,1)S(1)} collective-permute-done((bf16[256,1024]{1,0:T(8,128)(2,1)S(1)}, bf16[256,1024]{1,0:T(8,128)(2,1)S(1)}, u32[]{:S(2)}, u32[]{:S(2)}) %collective-permute-start.31) | collective-permute-done | bytes 524320 | tf_op jit(solution)/shard_map/ppermute | solution.py:548
  223.4 8.0 %attention_forward.3 = (bf16[512,256]{1,0:T(8,128)(2,1)S(1)}, bf16[512,256]{1,0:T(8,128)(2,1)S(1)}, f32[8,1024]{1,0:T(8,128)S(1)}) custom-call(s32[4]{0:T(128)S(1)} %pad_add_fusion.3.order_ref, bf16[512,768]{1,0:T(8,128)(2,1)S(1)} %add_convert_fusion.1.refs_0_, bf16[512,768]{1,0:T(8,128)(2,1)S(1)} %add_convert_fusion.refs_1_, ...), custom_call_target="tpu_custom_call" | custom-call | flops 1 | bytes 1 | tf_op jit(solution)/shard_map/attention_forward/pallas_call | solution.py:288
  231.7 7.6 %collective-permute-done.35 = bf16[512,256]{1,0:T(8,128)(2,1)S(1)} collective-permute-done((bf16[512,256]{1,0:T(8,128)(2,1)S(1)}, bf16[512,256]{1,0:T(8,128)(2,1)S(1)}, u32[]{:S(2)}, u32[]{:S(2)}) %collective-permute-start.35) | collective-permute-done | bytes 262176 | tf_op jit(solution)/shard_map/ppermute | solution.py:548
  247.7 15.7 %feed_forward.4 = (f32[256,1024]{1,0:T(8,128)}, bf16[256,1024]{1,0:T(8,128)(2,1)}, f32[256,1024]{1,0:T(8,128)}, bf16[256,1024]{1,0:T(8,128)(2,1)}) custom-call(bf16[256,1024]{1,0:T(8,128)(2,1)} %copy-done.30, bf16[256,1024]{1,0:T(8,128)(2,1)} %collective-permute-done.37.refs_1_, f32[4,1,512]{2,1,0:T(1,128)} %reshape_squeeze.8.refs_2_, ...), custom_call_target="tpu_custom_call" | custom-call | flops 1 | bytes 1 | tf_op jit(solution)/shard_map/feed_forward/pallas_call | solution.py:408
  273.2 6.8 %collective-permute-done.41.refs_3_ = bf16[512,256]{1,0:T(8,128)(2,1)S(1)} collective-permute-done((bf16[512,256]{1,0:T(8,128)(2,1)S(1)}, bf16[512,256]{1,0:T(8,128)(2,1)S(1)}, u32[]{:S(2)}, u32[]{:S(2)}) %collective-permute-start.41) | collective-permute-done | bytes 262176 | tf_op jit(solution)/shard_map/ppermute | solution.py:548
  280.1 12.1 %attention_backward.2 = (bf16[512,768]{1,0:T(8,128)(2,1)S(1)}, bf16[512,768]{1,0:T(8,128)(2,1)S(1)}, f32[2,16,256]{2,1,0:T(8,128)S(1)}) custom-call(s32[4]{0:T(128)S(1)} %pad_add_fusion.3.order_ref, bf16[512,768]{1,0:T(8,128)(2,1)S(1)} %copy-done.2, bf16[512,768]{1,0:T(8,128)(2,1)S(1)} %copy-done.4, bf16[512,256]{1,0:T(8,128)(2,1)S(1)} %convolution_convert_fusion.9.refs_2_, ...), custom_call_target="tpu_custom_call" | custom-call | flops 1 | bytes 1 | tf_op jit(solution)/shard_map/attention_backward/pallas_call | solution.py:316
  298.2 11.8 %collective-permute-done.43 = bf16[256,1024]{1,0:T(8,128)(2,1)S(1)} collective-permute-done((bf16[256,1024]{1,0:T(8,128)(2,1)S(1)}, bf16[256,1024]{1,0:T(8,128)(2,1)S(1)}, u32[]{:S(2)}, u32[]{:S(2)}) %collective-permute-start.43) | collective-permute-done | bytes 524320 | tf_op jit(solution)/shard_map/ppermute | solution.py:548
  314.5 12.9 %feed_forward.5 = (f32[256,1024]{1,0:T(8,128)}, bf16[256,1024]{1,0:T(8,128)(2,1)}) custom-call(bf16[256,1024]{1,0:T(8,128)(2,1)} %get-tuple-element.244.refs_1_.refs_0_, bf16[256,1024]{1,0:T(8,128)(2,1)} %get-tuple-element.125.refs_0_.refs_1_, f32[4,1,512]{2,1,0:T(1,128)} %reshape_squeeze.7.refs_2_, bf16[256,1024]{1,0:T(8,128)(2,1)} %copy-done.27, ...), custom_call_target="tpu_custom_call" | custom-call | flops 1 | bytes 1 | tf_op jit(solution)/shard_map/feed_forward/pallas_call | solution.py:408
  338.0 6.5 %collective-permute-done.50.refs_3_ = bf16[512,256]{1,0:T(8,128)(2,1)S(1)} collective-permute-done((bf16[512,256]{1,0:T(8,128)(2,1)S(1)}, bf16[512,256]{1,0:T(8,128)(2,1)S(1)}, u32[]{:S(2)}, u32[]{:S(2)}) %collective-permute-start.50) | collective-permute-done | bytes 262176 | tf_op jit(solution)/shard_map/ppermute | solution.py:548
  344.5 12.1 %attention_backward.3 = (bf16[512,768]{1,0:T(8,128)(2,1)S(1)}, bf16[512,768]{1,0:T(8,128)(2,1)S(1)}, f32[2,16,256]{2,1,0:T(8,128)S(1)}) custom-call(s32[4]{0:T(128)S(1)} %pad_add_fusion.2.order_ref, bf16[512,768]{1,0:T(8,128)(2,1)S(1)} %add_convert_fusion.3.refs_0_, bf16[512,768]{1,0:T(8,128)(2,1)S(1)} %add_convert_fusion.2.refs_1_, ...), custom_call_target="tpu_custom_call" | custom-call | flops 1 | bytes 1 | tf_op jit(solution)/shard_map/attention_backward/pallas_call | solution.py:316
  366.7 7.2 %collective-permute-done.52 = bf16[256,1024]{1,0:T(8,128)(2,1)S(1)} collective-permute-done((bf16[256,1024]{1,0:T(8,128)(2,1)S(1)}, bf16[256,1024]{1,0:T(8,128)(2,1)S(1)}, u32[]{:S(2)}, u32[]{:S(2)}) %collective-permute-start.52) | collective-permute-done | bytes 524320 | tf_op jit(solution)/shard_map/ppermute | solution.py:548
  382.3 5.6 %collective-permute-done.60 = f32[16,512]{1,0:T(8,128)S(1)} collective-permute-done((f32[16,512]{1,0:T(8,128)S(1)}, f32[16,512]{1,0:T(8,128)S(1)}, u32[]{:S(2)}, u32[]{:S(2)}) %collective-permute-start.60) | collective-permute-done | bytes 32800 | tf_op jit(solution)/shard_map/ppermute | solution.py:590
  (345 shorter events, 148.7 us)
Async XLA Ops:
  1.5 19.7 %collective-permute-start.1 = (bf16[8,1024]{1,0:T(8,128)(2,1)S(1)}, bf16[8,1024]{1,0:T(8,128)(2,1)S(1)}, u32[]{:S(2)}, u32[]{:S(2)}) collective-permute-start(bf16[8,1024]{1,0:T(8,128)(2,1)S(1)} %concatenate.38), channel_id=1, source_target_pairs={{0,16},{16,0},{1,17},{17,1},{2,18},{18,2},{3,19},{19,3},{4,20},{20... | collective-permute-start | bytes 49160 | tf_op jit(solution)/shard_map/ppermute | solution.py:540
  3.5 20.4 %collective-permute-start.3 = (bf16[256,1024]{1,0:T(8,128)(2,1)}, bf16[256,1024]{1,0:T(8,128)(2,1)}, u32[]{:S(2)}, u32[]{:S(2)}) collective-permute-start(bf16[256,1024]{1,0:T(8,128)(2,1)} %dynamic-slice_bitcast_fusion), channel_id=1, source_target_pairs={{0,18},{1,19},{2,16},{3,17},{4,22},{5,23},{6,20},{7,21},{8,26},{9,... | collective-permute-start | bytes 1572872 | tf_op jit(solution)/shard_map/ppermute | solution.py:574
  11.2 17.9 %collective-permute-start = (bf16[2,256,2048]{2,1,0:T(8,128)(2,1)}, bf16[2,256,2048]{2,1,0:T(8,128)(2,1)}, u32[]{:S(2)}, u32[]{:S(2)}) collective-permute-start(bf16[2,256,2048]{2,1,0:T(8,128)(2,1)} %get-tuple-element.89), channel_id=1, source_target_pairs={{0,16},{16,0},{1,17},{17,1},{2,18},{18,2},{3,19},{19,3},{4,20},{20... | collective-permute-start | bytes 6291464 | tf_op jit(solution)/shard_map/ppermute | solution.py:540
  27.3 36.8 %collective-permute-start.7 = (bf16[1024,768]{0,1:T(8,128)(2,1)}, bf16[1024,768]{0,1:T(8,128)(2,1)}, u32[]{:S(2)}, u32[]{:S(2)}) collective-permute-start(bf16[1024,768]{0,1:T(8,128)(2,1)} %bitcast.21), channel_id=1, source_target_pairs={{0,18},{1,19},{2,16},{3,17},{16,2},{17,3},{18,0},{19,1},{4,22},{5,... | collective-permute-start | bytes 4718600 | tf_op jit(solution)/shard_map/ppermute | solution.py:557
  40.2 24.1 %collective-permute-start.6 = (bf16[256,2048]{1,0:T(8,128)(2,1)}, bf16[256,2048]{1,0:T(8,128)(2,1)}, u32[]{:S(2)}, u32[]{:S(2)}) collective-permute-start(bf16[256,2048]{1,0:T(8,128)(2,1)} %fusion.29.refs_3_.refs_5_), channel_id=1, source_target_pairs={{0,1},{1,0},{2,3},{3,2},{4,5},{5,4},{6,7},{7,6},{8,9},{9,8},{10,11... | collective-permute-start | bytes 3145736 | tf_op jit(solution)/shard_map/ppermute | solution.py:548
  69.2 30.8 %collective-permute-start.10 = (bf16[256,2048]{1,0:T(8,128)(2,1)}, bf16[256,2048]{1,0:T(8,128)(2,1)}, u32[]{:S(2)}, u32[]{:S(2)}) collective-permute-start(bf16[256,2048]{1,0:T(8,128)(2,1)} %fusion.29.refs_3_.refs_5_), channel_id=1, source_target_pairs={{0,2},{1,3},{2,0},{3,1},{4,6},{5,7},{6,4},{7,5},{8,10},{9,11},{10,... | collective-permute-start | bytes 3145736 | tf_op jit(solution)/shard_map/ppermute | solution.py:561
  69.6 30.4 %collective-permute-start.11 = (bf16[256,2048]{1,0:T(8,128)(2,1)}, bf16[256,2048]{1,0:T(8,128)(2,1)}, u32[]{:S(2)}, u32[]{:S(2)}) collective-permute-start(bf16[256,2048]{1,0:T(8,128)(2,1)} %get-tuple-element.107.refs_5_), channel_id=1, source_target_pairs={{0,1},{1,0},{2,3},{3,2},{4,5},{5,4},{6,7},{7,6},{8,9},{9,8},{10,11... | collective-permute-start | bytes 3145736 | tf_op jit(solution)/shard_map/ppermute | solution.py:548
  70.7 29.4 %collective-permute-start.12 = (bf16[256,2048]{1,0:T(8,128)(2,1)}, bf16[256,2048]{1,0:T(8,128)(2,1)S(1)}, u32[]{:S(2)}, u32[]{:S(2)}) collective-permute-start(bf16[256,2048]{1,0:T(8,128)(2,1)} %collective-permute-done.6.refs_7_.refs_9_), channel_id=1, source_target_pairs={{0,4},{4,0},{8,12},{12,8},{1,5},{5,1},{9,13},{13,9},{2,6},{6,2},{1... | collective-permute-start | bytes 3145736 | tf_op jit(solution)/shard_map/ppermute | solution.py:566
  72.1 27.9 %collective-permute-start.9 = (bf16[256,1024]{1,0:T(8,128)(2,1)S(1)}, bf16[256,1024]{1,0:T(8,128)(2,1)S(1)}, u32[]{:S(2)}, u32[]{:S(2)}) collective-permute-start(bf16[256,1024]{1,0:T(8,128)(2,1)S(1)} %bitcast.120), channel_id=1, source_target_pairs={{0,18},{1,19},{2,16},{3,17},{4,22},{5,23},{6,20},{7,21},{8,26},{9,... | collective-permute-start | bytes 1572872 | tf_op jit(solution)/shard_map/ppermute | solution.py:574
  103.7 39.8 %collective-permute-start.14 = (bf16[256,2048]{1,0:T(8,128)(2,1)}, bf16[256,2048]{1,0:T(8,128)(2,1)}, u32[]{:S(2)}, u32[]{:S(2)}) collective-permute-start(bf16[256,2048]{1,0:T(8,128)(2,1)} %collective-permute-done.10.refs_5_.refs_7_), channel_id=1, source_target_pairs={{0,1},{1,0},{2,3},{3,2},{4,5},{5,4},{6,7},{7,6},{8,9},{9,8},{10,11... | collective-permute-start | bytes 3145736 | tf_op jit(solution)/shard_map/ppermute | solution.py:548
  104.9 38.6 %collective-permute-start.15 = (bf16[256,2048]{1,0:T(8,128)(2,1)}, bf16[256,2048]{1,0:T(8,128)(2,1)}, u32[]{:S(2)}, u32[]{:S(2)}) collective-permute-start(bf16[256,2048]{1,0:T(8,128)(2,1)} %get-tuple-element.107.refs_5_), channel_id=1, source_target_pairs={{0,2},{1,3},{2,0},{3,1},{4,6},{5,7},{6,4},{7,5},{8,10},{9,11},{10,... | collective-permute-start | bytes 3145736 | tf_op jit(solution)/shard_map/ppermute | solution.py:561
  105.1 38.4 %collective-permute-start.13 = (bf16[512,1024]{1,0:T(8,128)(2,1)}, bf16[512,1024]{1,0:T(8,128)(2,1)}, u32[]{:S(2)}, u32[]{:S(2)}) collective-permute-start(bf16[512,1024]{1,0:T(8,128)(2,1)} %pad_maximum_fusion), channel_id=1, source_target_pairs={{16,2},{17,3},{18,0},{19,1},{20,6},{21,7},{22,4},{23,5},{24,10},{2... | collective-permute-start | bytes 3145736 | tf_op jit(solution)/shard_map/ppermute | solution.py:574
  110.1 33.4 %collective-permute-start.16 = (bf16[256,2048]{1,0:T(8,128)(2,1)}, bf16[256,2048]{1,0:T(8,128)(2,1)}, u32[]{:S(2)}, u32[]{:S(2)}) collective-permute-start(bf16[256,2048]{1,0:T(8,128)(2,1)} %collective-permute-done.11.refs_9_), channel_id=1, source_target_pairs={{0,4},{4,0},{8,12},{12,8},{1,5},{5,1},{9,13},{13,9},{2,6},{6,2},{1... | collective-permute-start | bytes 3145736 | tf_op jit(solution)/shard_map/ppermute | solution.py:566
  112.2 27.4 %collective-permute-start.20 = (bf16[256,1024]{1,0:T(8,128)(2,1)}, bf16[256,1024]{1,0:T(8,128)(2,1)}, u32[]{:S(2)}, u32[]{:S(2)}) collective-permute-start(bf16[256,1024]{1,0:T(8,128)(2,1)} %add_convert_fusion.11), channel_id=1, source_target_pairs={{0,1},{1,0},{2,3},{3,2},{4,5},{5,4},{6,7},{7,6},{8,9},{9,8},{10,11... | collective-permute-start | bytes 1572872 | tf_op jit(solution)/shard_map/ppermute | solution.py:548
  143.5 25.2 %collective-permute-start.21 = (bf16[256,2048]{1,0:T(8,128)(2,1)}, bf16[256,2048]{1,0:T(8,128)(2,1)}, u32[]{:S(2)}, u32[]{:S(2)}) collective-permute-start(bf16[256,2048]{1,0:T(8,128)(2,1)} %get-tuple-element.119.refs_4_.refs_6_), channel_id=1, source_target_pairs={{0,2},{1,3},{2,0},{3,1},{4,6},{5,7},{6,4},{7,5},{8,10},{9,11},{10,... | collective-permute-start | bytes 3145736 | tf_op jit(solution)/shard_map/ppermute | solution.py:561
  143.9 24.8 %collective-permute-start.22 = (bf16[256,2048]{1,0:T(8,128)(2,1)}, bf16[256,2048]{1,0:T(8,128)(2,1)}, u32[]{:S(2)}, u32[]{:S(2)}) collective-permute-start(bf16[256,2048]{1,0:T(8,128)(2,1)} %collective-permute-done.14.refs_9_.refs_11_), channel_id=1, source_target_pairs={{0,4},{4,0},{8,12},{12,8},{1,5},{5,1},{9,13},{13,9},{2,6},{6,2},{1... | collective-permute-start | bytes 3145736 | tf_op jit(solution)/shard_map/ppermute | solution.py:566
  145.1 24.4 %collective-permute-start.23 = (bf16[256,2048]{1,0:T(8,128)(2,1)}, bf16[256,2048]{1,0:T(8,128)(2,1)}, u32[]{:S(2)}, u32[]{:S(2)}) collective-permute-start(bf16[256,2048]{1,0:T(8,128)(2,1)} %collective-permute-done.15.refs_7_), channel_id=1, source_target_pairs={{0,1},{1,0},{2,3},{3,2},{4,5},{5,4},{6,7},{7,6},{8,9},{9,8},{10,11... | collective-permute-start | bytes 3145736 | tf_op jit(solution)/shard_map/ppermute | solution.py:548
  169.5 26.0 %collective-permute-start.26 = (bf16[256,2048]{1,0:T(8,128)(2,1)}, bf16[256,2048]{1,0:T(8,128)(2,1)S(1)}, u32[]{:S(2)}, u32[]{:S(2)}) collective-permute-start(bf16[256,2048]{1,0:T(8,128)(2,1)} %get-tuple-element.128.refs_6_), channel_id=1, source_target_pairs={{0,2},{1,3},{2,0},{3,1},{4,6},{5,7},{6,4},{7,5},{8,10},{9,11},{10,... | collective-permute-start | bytes 3145736 | tf_op jit(solution)/shard_map/ppermute | solution.py:561
  170.8 24.8 %collective-permute-start.27 = (bf16[256,2048]{1,0:T(8,128)(2,1)}, bf16[256,2048]{1,0:T(8,128)(2,1)S(1)}, u32[]{:S(2)}, u32[]{:S(2)}) collective-permute-start(bf16[256,2048]{1,0:T(8,128)(2,1)} %collective-permute-done.23.refs_11_), channel_id=1, source_target_pairs={{0,4},{4,0},{8,12},{12,8},{1,5},{5,1},{9,13},{13,9},{2,6},{6,2},{1... | collective-permute-start | bytes 3145736 | tf_op jit(solution)/shard_map/ppermute | solution.py:566
  172.6 17.4 %collective-permute-start.28 = (bf16[256,1024]{1,0:T(8,128)(2,1)S(1)}, bf16[256,1024]{1,0:T(8,128)(2,1)}, u32[]{:S(2)}, u32[]{:S(2)}) collective-permute-start(bf16[256,1024]{1,0:T(8,128)(2,1)S(1)} %copy-done.18), channel_id=1, source_target_pairs={{0,1},{1,0},{2,3},{3,2},{4,5},{5,4},{6,7},{7,6},{8,9},{9,8},{10,11... | collective-permute-start | bytes 1572872 | tf_op jit(solution)/shard_map/ppermute | solution.py:548
  176.3 19.3 %collective-permute-start.29 = (bf16[256,1024]{1,0:T(8,128)(2,1)S(1)}, bf16[256,1024]{1,0:T(8,128)(2,1)}, u32[]{:S(2)}, u32[]{:S(2)}) collective-permute-start(bf16[256,1024]{1,0:T(8,128)(2,1)S(1)} %get-tuple-element.132), channel_id=1, source_target_pairs={{0,1},{1,0},{2,3},{3,2},{4,5},{5,4},{6,7},{7,6},{8,9},{9,8},{10,11... | collective-permute-start | bytes 1572872 | tf_op jit(solution)/shard_map/ppermute | solution.py:548
  204.0 14.4 %collective-permute-start.33 = (bf16[512,512]{0,1:T(8,128)(2,1)S(1)}, bf16[512,512]{0,1:T(8,128)(2,1)S(1)}, u32[]{:S(2)}, u32[]{:S(2)}) collective-permute-start(bf16[512,512]{0,1:T(8,128)(2,1)S(1)} %bitcast.115), channel_id=1, source_target_pairs={{0,18},{1,19},{2,16},{3,17},{16,2},{17,3},{18,0},{19,1},{4,22},{5,... | collective-permute-start | bytes 1572872 | tf_op jit(solution)/shard_map/ppermute | solution.py:557
  296.9 14.3 %collective-permute-start.46 = (bf16[256,1024]{1,0:T(8,128)(2,1)S(1)}, bf16[256,1024]{1,0:T(8,128)(2,1)S(1)}, u32[]{:S(2)}, u32[]{:S(2)}) collective-permute-start(bf16[256,1024]{1,0:T(8,128)(2,1)S(1)} %get-tuple-element.209.high_own), channel_id=1, source_target_pairs={{0,18},{1,19},{2,16},{3,17},{4,22},{5,23},{6,20},{7,21},{8,26},{9,... | collective-permute-start | bytes 1572872 | tf_op jit(solution)/shard_map/ppermute | solution.py:574
  376.3 15.2 %collective-permute-start.54 = (bf16[256,1024]{1,0:T(8,128)(2,1)S(1)}, bf16[256,1024]{1,0:T(8,128)(2,1)S(1)}, u32[]{:S(2)}, u32[]{:S(2)}) collective-permute-start(bf16[256,1024]{1,0:T(8,128)(2,1)S(1)} %fusion.26.low_own), channel_id=1, source_target_pairs={{16,2},{17,3},{18,0},{19,1},{20,6},{21,7},{22,4},{23,5},{24,10},{2... | collective-permute-start | bytes 1572872 | tf_op jit(solution)/shard_map/ppermute | solution.py:574
  (91 other events, 720.0 us)

commit v4 on v3

--- a/solution.py
+++ b/solution.py
@@ -750,7 +750,8 @@
         axis=0,
     )
     qkv_own = (
-        w_qkv.reshape(width, heads_local, 3, head_dim)
+        tied(w_qkv, even[0])
+        .reshape(width, heads_local, 3, head_dim)
         .transpose(0, 2, 1, 3)
         .reshape(width, 3 * head_width)
     )
@@ -764,15 +765,14 @@
     def far(value, layer):
         return stages.send(functools.partial(group.cross_from, core=layer), value)
 
+    side_even_0 = [group.shift(even[0], distance) for distance in steps]
+    stages.next()
+    normed_0 = tied(normed_one(0, inputs), *side_even_0)
+    gathered_0 = [normed_0] + group.shifts(stages, normed_0)
+    stages.now += side_even_0
     side_bias = small_chip[:, 6, : w_up.shape[2]]
     side_bias = jnp.stack([side_bias] + group.shifts(stages, side_bias), axis=1)
-
-    stages.next()
-    half_bias = half_send(side_bias)
-    normed_0 = normed_one(0, inputs)
-    gathered_0 = [normed_0] + group.shifts(stages, normed_0)
-    side_even_0 = group.shifts(stages, tied(even[0], *gathered_0[1:]))
-    qkv_far = stages.send(group.cross, tied(qkv_own, half_bias))
+    qkv_far = stages.send(group.cross, qkv_own)
 
     stages.next()
     pairs = layer_pair(pairs_own, stages.send(group.cross, pairs_own))
@@ -873,7 +873,7 @@
             grad_in = grad_middle + norm_back(self.inputs, self.ln1_gain, grad_normed)
             return (grad_in.astype(bf16), grad_pairs)
 
-    pack_own = jnp.concatenate([proj_own, other_row], axis=0)
+    pack_own = jnp.concatenate([tied(proj_own, qkv_far), other_row], axis=0)
     layer_0 = Layer(0, tied(jnp.where(low, qkv_own, qkv_far), pack_own))
     layer_0.far_out = (proj_own, proj_far_0)
     layer_0.attention(inputs, gathered_0)
@@ -895,6 +895,7 @@
     else:
         corner_odd_0 = group.shifts(stages, half_odd_0)
     corner_even_1 = group.shifts(stages, half_even_1)
+    half_bias = half_send(side_bias)
     up_bias = jnp.stack([side_bias, half_bias], axis=2).astype(f32)
     up_bias = up_bias.reshape(2, 2 * count, 2, 2, rows)
     up_bias = jnp.where(low, up_bias[:, :, 0], up_bias[:, :, 1])

time: 398 us -> 393 us (0.987)
  waiting for transfers between devices: 167 us -> 160 us
    ppermute x4, waiting for transfers between devices: 16.3 us -> 1.86 us  [cross(): return lax.ppermute(value, ('section', 'tensor'), pairs)]
    ppermute x15, waiting for transfers between devices: 93.4 us -> 97.6 us  [shift(): return lax.ppermute(value, 'tensor', pairs)]
    ppermute x5, waiting for transfers between devices: 16.3 us -> 20.4 us  [cross_from(): return lax.ppermute(value, ('section', 'tensor'), pairs)]
    unnamed x105 -> x107, local copies, waits for them, and re-layouts: 7.98 us -> 7.32 us
  transfers between devices with their start and end apart: 63 -> 63, of which waited for: 30 -> 33; matrix products, arithmetic and copies ran while one was open for 12% -> 12% of each run, Pallas kernels for 6% -> 6%
where the time goes in v4:
time: 393 us; the launch traced here: 388 us
  waiting for transfers between devices  160 us (41%)
  Pallas kernels  87.6 us (22%)
  starting transfers between devices  64.5 us (16%)
  other arithmetic  40.4 us (10%)
  matrix products  18.2 us (5%)
  local copies, waits for them, and re-layouts  15.1 us (4%)
    ppermute x15, waiting for transfers between devices, shift(): return lax.ppermute(value, 'tensor', pairs)  97.6 us
    pallas_call x3, Pallas kernels, feed_forward(): pl.pallas_call(functools.partial(feed_forward_kernel, groups, per, with_o...  39.1 us
    pallas_call x2, Pallas kernels, attention_backward(): pl.pallas_call(functools.partial(attention_backward_kernel, count, block_...  24.2 us
    ppermute x24, starting transfers between devices, core_swap(): return lax.ppermute(value, 'section', [(0, 1), (1, 0)])  21.9 us
    ppermute x5, waiting for transfers between devices, cross_from(): return lax.ppermute(value, ('section', 'tensor'), pairs)  20.4 us
    ppermute x5, waiting for transfers between devices, half_swap(): return lax.ppermute(value, 'tensor', pairs)  18.3 us
    ppermute x24, waiting for transfers between devices, core_swap(): return lax.ppermute(value, 'section', [(0, 1), (1, 0)])  16.3 us
    pallas_call x2, Pallas kernels, attention_forward(): pl.pallas_call(functools.partial(attention_forward_kernel, count, block_r...  16 us
  transfers between devices with their start and end apart: 63, of which 33 were waited for; matrix products, arithmetic and copies ran while one was open for 12% of the time, Pallas kernels for 6%

profile of v4, /device:TPU:1, one launch (start us, length us, event | category | flops | bytes accessed | tf_op | source)
XLA Modules:
  0.0 387.7 jit_solution(4870786809777355220)
XLA Ops:
  10.0 4.5 %collective-permute-start.3 = (bf16[8,1024]{1,0:T(8,128)(2,1)S(1)}, bf16[8,1024]{1,0:T(8,128)(2,1)S(1)}, u32[]{:S(2)}, u32[]{:S(2)}) collective-permute-start(bf16[8,1024]{1,0:T(8,128)(2,1)S(1)} %concatenate.38), channel_id=1, source_target_pairs={{0,16},{16,0},{1,17},{17,1},{2,18},{18,2},{3,19},{19,3},{4,20},{20... | collective-permute-start | bytes 49160 | tf_op jit(solution)/shard_map/ppermute | solution.py:540
  15.5 4.0 %collective-permute-done.1 = bf16[256,1024]{1,0:T(8,128)(2,1)} collective-permute-done((bf16[256,1024]{1,0:T(8,128)(2,1)S(1)}, bf16[256,1024]{1,0:T(8,128)(2,1)}, u32[]{:S(2)}, u32[]{:S(2)}) %collective-permute-start.1) | collective-permute-done | bytes 524320 | tf_op jit(solution)/shard_map/ppermute | solution.py:574
  33.1 17.1 %collective-permute-done.4.refs_7_.refs_9_ = bf16[256,2048]{1,0:T(8,128)(2,1)} collective-permute-done((bf16[256,2048]{1,0:T(8,128)(2,1)}, bf16[256,2048]{1,0:T(8,128)(2,1)}, u32[]{:S(2)}, u32[]{:S(2)}) %collective-permute-start.4) | collective-permute-done | bytes 1048608 | tf_op jit(solution)/shard_map/ppermute | solution.py:548
  55.2 8.3 %collective-permute-done.5 = bf16[256,1024]{1,0:T(8,128)(2,1)S(1)} collective-permute-done((bf16[256,1024]{1,0:T(8,128)(2,1)S(1)}, bf16[256,1024]{1,0:T(8,128)(2,1)S(1)}, u32[]{:S(2)}, u32[]{:S(2)}) %collective-permute-start.5) | collective-permute-done | bytes 524320 | tf_op jit(solution)/shard_map/ppermute | solution.py:548
  75.7 8.0 %attention_forward.2 = (bf16[512,256]{1,0:T(8,128)(2,1)S(1)}, bf16[512,256]{1,0:T(8,128)(2,1)S(1)}, f32[8,1024]{1,0:T(8,128)S(1)}) custom-call(s32[4]{0:T(128)S(1)} %pad_add_fusion.2.order_ref, bf16[512,768]{1,0:T(8,128)(2,1)S(1)} %add_convert_fusion.3.refs_0_, bf16[512,768]{1,0:T(8,128)(2,1)S(1)} %add_convert_fusion.2.refs_1_, ...), custom_call_target="tpu_custom_call" | custom-call | flops 1 | bytes 1 | tf_op jit(solution)/shard_map/attention_forward/pallas_call | solution.py:288
  83.7 14.9 %collective-permute-done.8 = bf16[256,1024]{1,0:T(8,128)(2,1)S(1)} collective-permute-done((bf16[256,1024]{1,0:T(8,128)(2,1)S(1)}, bf16[256,1024]{1,0:T(8,128)(2,1)S(1)}, u32[]{:S(2)}, u32[]{:S(2)}) %collective-permute-start.8) | collective-permute-done | bytes 524320 | tf_op jit(solution)/shard_map/ppermute | solution.py:574
  105.3 4.0 %collective-permute-start.12 = (bf16[512,1024]{1,0:T(8,128)(2,1)}, bf16[512,1024]{1,0:T(8,128)(2,1)}, u32[]{:S(2)}, u32[]{:S(2)}) collective-permute-start(bf16[512,1024]{1,0:T(8,128)(2,1)} %pad_maximum_fusion), channel_id=1, source_target_pairs={{16,2},{17,3},{18,0},{19,1},{20,6},{21,7},{22,4},{23,5},{24,10},{2... | collective-permute-start | bytes 3145736 | tf_op jit(solution)/shard_map/ppermute | solution.py:574
  111.7 4.1 %collective-permute-done.19 = bf16[256,1024]{1,0:T(8,128)(2,1)} collective-permute-done((bf16[256,1024]{1,0:T(8,128)(2,1)}, bf16[256,1024]{1,0:T(8,128)(2,1)}, u32[]{:S(2)}, u32[]{:S(2)}) %collective-permute-start.19) | collective-permute-done | bytes 524320 | tf_op jit(solution)/shard_map/ppermute | solution.py:548
  120.5 17.8 %collective-permute-done.13.refs_9_.refs_11_ = bf16[256,2048]{1,0:T(8,128)(2,1)} collective-permute-done((bf16[256,2048]{1,0:T(8,128)(2,1)}, bf16[256,2048]{1,0:T(8,128)(2,1)}, u32[]{:S(2)}, u32[]{:S(2)}) %collective-permute-start.13) | collective-permute-done | bytes 1048608 | tf_op jit(solution)/shard_map/ppermute | solution.py:548
  145.5 18.3 %collective-permute-done.23 = bf16[2,2,1024]{2,1,0:T(2,128)(2,1)S(1)} collective-permute-done((bf16[2,2,1024]{2,1,0:T(2,128)(2,1)S(1)}, bf16[2,2,1024]{2,1,0:T(2,128)(2,1)S(1)}, u32[]{:S(2)}, u32[]{:S(2)}) %collective-permute-start.23) | collective-permute-done | bytes 8224 | tf_op jit(solution)/shard_map/ppermute | solution.py:561
  176.0 10.5 %feed_forward.3 = (f32[256,1024]{1,0:T(8,128)}, bf16[256,1024]{1,0:T(8,128)(2,1)}) custom-call(bf16[256,1024]{1,0:T(8,128)(2,1)} %get-tuple-element.127.refs_0_.refs_1_, bf16[256,1024]{1,0:T(8,128)(2,1)} %get-tuple-element.246.refs_1_.refs_0_, f32[4,1,512]{2,1,0:T(1,128)} %reshape_squeeze.7.refs_2_, bf16[256,2048]{1,0:T(8,128)(2,1)} %fusion.29.refs_3_.refs_5_, ...), custom_call_target="tpu_custom_call" | custom-call | flops 1 | bytes 1 | tf_op jit(solution)/shard_map/feed_forward/pallas_call | solution.py:408
  188.3 3.8 collective-permute-start.30
  199.6 10.0 %collective-permute-done.31 = bf16[256,1024]{1,0:T(8,128)(2,1)S(1)} collective-permute-done((bf16[256,1024]{1,0:T(8,128)(2,1)S(1)}, bf16[256,1024]{1,0:T(8,128)(2,1)S(1)}, u32[]{:S(2)}, u32[]{:S(2)}) %collective-permute-start.31) | collective-permute-done | bytes 524320 | tf_op jit(solution)/shard_map/ppermute | solution.py:548
  216.9 8.0 %attention_forward.3 = (bf16[512,256]{1,0:T(8,128)(2,1)S(1)}, bf16[512,256]{1,0:T(8,128)(2,1)S(1)}, f32[8,1024]{1,0:T(8,128)S(1)}) custom-call(s32[4]{0:T(128)S(1)} %pad_add_fusion.3.order_ref, bf16[512,768]{1,0:T(8,128)(2,1)S(1)} %add_convert_fusion.1.refs_0_, bf16[512,768]{1,0:T(8,128)(2,1)S(1)} %add_convert_fusion.refs_1_, ...), custom_call_target="tpu_custom_call" | custom-call | flops 1 | bytes 1 | tf_op jit(solution)/shard_map/attention_forward/pallas_call | solution.py:288
  225.2 7.5 %collective-permute-done.35 = bf16[512,256]{1,0:T(8,128)(2,1)S(1)} collective-permute-done((bf16[512,256]{1,0:T(8,128)(2,1)S(1)}, bf16[512,256]{1,0:T(8,128)(2,1)S(1)}, u32[]{:S(2)}, u32[]{:S(2)}) %collective-permute-start.35) | collective-permute-done | bytes 262176 | tf_op jit(solution)/shard_map/ppermute | solution.py:548
  243.1 15.6 %feed_forward.4 = (f32[256,1024]{1,0:T(8,128)}, bf16[256,1024]{1,0:T(8,128)(2,1)}, f32[256,1024]{1,0:T(8,128)}, bf16[256,1024]{1,0:T(8,128)(2,1)}) custom-call(bf16[256,1024]{1,0:T(8,128)(2,1)} %add_convert_fusion.7.refs_0_, bf16[256,1024]{1,0:T(8,128)(2,1)} %collective-permute-done.37.refs_1_, f32[4,1,512]{2,1,0:T(1,128)} %reshape_squeeze.8.refs_2_, ...), custom_call_target="tpu_custom_call" | custom-call | flops 1 | bytes 1 | tf_op jit(solution)/shard_map/feed_forward/pallas_call | solution.py:408
  268.9 5.6 %collective-permute-done.41.refs_3_ = bf16[512,256]{1,0:T(8,128)(2,1)S(1)} collective-permute-done((bf16[512,256]{1,0:T(8,128)(2,1)S(1)}, bf16[512,256]{1,0:T(8,128)(2,1)S(1)}, u32[]{:S(2)}, u32[]{:S(2)}) %collective-permute-start.41) | collective-permute-done | bytes 262176 | tf_op jit(solution)/shard_map/ppermute | solution.py:548
  274.5 12.1 %attention_backward.2 = (bf16[512,768]{1,0:T(8,128)(2,1)S(1)}, bf16[512,768]{1,0:T(8,128)(2,1)S(1)}, f32[2,16,256]{2,1,0:T(8,128)S(1)}) custom-call(s32[4]{0:T(128)S(1)} %pad_add_fusion.3.order_ref, bf16[512,768]{1,0:T(8,128)(2,1)S(1)} %copy-done.2, bf16[512,768]{1,0:T(8,128)(2,1)S(1)} %copy-done.4, bf16[512,256]{1,0:T(8,128)(2,1)S(1)} %convolution_convert_fusion.9.refs_2_, ...), custom_call_target="tpu_custom_call" | custom-call | flops 1 | bytes 1 | tf_op jit(solution)/shard_map/attention_backward/pallas_call | solution.py:316
  292.7 11.8 %collective-permute-done.43 = bf16[256,1024]{1,0:T(8,128)(2,1)S(1)} collective-permute-done((bf16[256,1024]{1,0:T(8,128)(2,1)S(1)}, bf16[256,1024]{1,0:T(8,128)(2,1)S(1)}, u32[]{:S(2)}, u32[]{:S(2)}) %collective-permute-start.43) | collective-permute-done | bytes 524320 | tf_op jit(solution)/shard_map/ppermute | solution.py:548
  309.0 12.9 %feed_forward.5 = (f32[256,1024]{1,0:T(8,128)}, bf16[256,1024]{1,0:T(8,128)(2,1)}) custom-call(bf16[256,1024]{1,0:T(8,128)(2,1)} %get-tuple-element.246.refs_1_.refs_0_, bf16[256,1024]{1,0:T(8,128)(2,1)} %get-tuple-element.127.refs_0_.refs_1_, f32[4,1,512]{2,1,0:T(1,128)} %reshape_squeeze.7.refs_2_, bf16[256,1024]{1,0:T(8,128)(2,1)} %copy-done.26, ...), custom_call_target="tpu_custom_call" | custom-call | flops 1 | bytes 1 | tf_op jit(solution)/shard_map/feed_forward/pallas_call | solution.py:408
  332.5 6.4 %collective-permute-done.50.refs_3_ = bf16[512,256]{1,0:T(8,128)(2,1)S(1)} collective-permute-done((bf16[512,256]{1,0:T(8,128)(2,1)S(1)}, bf16[512,256]{1,0:T(8,128)(2,1)S(1)}, u32[]{:S(2)}, u32[]{:S(2)}) %collective-permute-start.50) | collective-permute-done | bytes 262176 | tf_op jit(solution)/shard_map/ppermute | solution.py:548
  338.9 12.1 %attention_backward.3 = (bf16[512,768]{1,0:T(8,128)(2,1)S(1)}, bf16[512,768]{1,0:T(8,128)(2,1)S(1)}, f32[2,16,256]{2,1,0:T(8,128)S(1)}) custom-call(s32[4]{0:T(128)S(1)} %pad_add_fusion.2.order_ref, bf16[512,768]{1,0:T(8,128)(2,1)S(1)} %add_convert_fusion.3.refs_0_, bf16[512,768]{1,0:T(8,128)(2,1)S(1)} %add_convert_fusion.2.refs_1_, ...), custom_call_target="tpu_custom_call" | custom-call | flops 1 | bytes 1 | tf_op jit(solution)/shard_map/attention_backward/pallas_call | solution.py:316
  361.2 7.1 %collective-permute-done.52 = bf16[256,1024]{1,0:T(8,128)(2,1)S(1)} collective-permute-done((bf16[256,1024]{1,0:T(8,128)(2,1)S(1)}, bf16[256,1024]{1,0:T(8,128)(2,1)S(1)}, u32[]{:S(2)}, u32[]{:S(2)}) %collective-permute-start.52) | collective-permute-done | bytes 524320 | tf_op jit(solution)/shard_map/ppermute | solution.py:548
  378.0 4.4 %collective-permute-done.60 = f32[16,512]{1,0:T(8,128)S(1)} collective-permute-done((f32[16,512]{1,0:T(8,128)S(1)}, f32[16,512]{1,0:T(8,128)S(1)}, u32[]{:S(2)}, u32[]{:S(2)}) %collective-permute-start.60) | collective-permute-done | bytes 32800 | tf_op jit(solution)/shard_map/ppermute | solution.py:590
  (347 shorter events, 156.7 us)
Async XLA Ops:
  23.9 26.3 %collective-permute-start.4 = (bf16[256,2048]{1,0:T(8,128)(2,1)}, bf16[256,2048]{1,0:T(8,128)(2,1)}, u32[]{:S(2)}, u32[]{:S(2)}) collective-permute-start(bf16[256,2048]{1,0:T(8,128)(2,1)} %fusion.29.refs_3_.refs_5_), channel_id=1, source_target_pairs={{0,1},{1,0},{2,3},{3,2},{4,5},{5,4},{6,7},{7,6},{8,9},{9,8},{10,11... | collective-permute-start | bytes 3145736 | tf_op jit(solution)/shard_map/ppermute | solution.py:548
  26.4 28.9 %collective-permute-start.6 = (bf16[2,1024]{1,0:T(2,128)(2,1)S(1)}, bf16[2,1024]{1,0:T(2,128)(2,1)S(1)}, u32[]{:S(2)}, u32[]{:S(2)}) collective-permute-start(bf16[2,1024]{1,0:T(2,128)(2,1)S(1)} %bitcast.149), channel_id=1, source_target_pairs={{0,1},{1,0},{2,3},{3,2},{4,5},{5,4},{6,7},{7,6},{8,9},{9,8},{10,11... | collective-permute-start | bytes 12296 | tf_op jit(solution)/shard_map/ppermute | solution.py:548
  27.7 36.6 %collective-permute-start.2 = (bf16[1024,768]{0,1:T(8,128)(2,1)}, bf16[1024,768]{0,1:T(8,128)(2,1)}, u32[]{:S(2)}, u32[]{:S(2)}) collective-permute-start(bf16[1024,768]{0,1:T(8,128)(2,1)} %bitcast.10), channel_id=1, source_target_pairs={{0,18},{1,19},{2,16},{3,17},{16,2},{17,3},{18,0},{19,1},{4,22},{5,... | collective-permute-start | bytes 4718600 | tf_op jit(solution)/shard_map/ppermute | solution.py:557
  67.9 30.8 %collective-permute-start.9 = (bf16[256,2048]{1,0:T(8,128)(2,1)}, bf16[256,2048]{1,0:T(8,128)(2,1)}, u32[]{:S(2)}, u32[]{:S(2)}) collective-permute-start(bf16[256,2048]{1,0:T(8,128)(2,1)} %fusion.29.refs_3_.refs_5_), channel_id=1, source_target_pairs={{0,2},{1,3},{2,0},{3,1},{4,6},{5,7},{6,4},{7,5},{8,10},{9,11},{10,... | collective-permute-start | bytes 3145736 | tf_op jit(solution)/shard_map/ppermute | solution.py:561
  69.4 29.3 %collective-permute-start.10 = (bf16[256,2048]{1,0:T(8,128)(2,1)}, bf16[256,2048]{1,0:T(8,128)(2,1)}, u32[]{:S(2)}, u32[]{:S(2)}) collective-permute-start(bf16[256,2048]{1,0:T(8,128)(2,1)} %get-tuple-element.108.refs_5_), channel_id=1, source_target_pairs={{0,1},{1,0},{2,3},{3,2},{4,5},{5,4},{6,7},{7,6},{8,9},{9,8},{10,11... | collective-permute-start | bytes 3145736 | tf_op jit(solution)/shard_map/ppermute | solution.py:548
  70.8 28.0 %collective-permute-start.11 = (bf16[256,2048]{1,0:T(8,128)(2,1)}, bf16[256,2048]{1,0:T(8,128)(2,1)S(1)}, u32[]{:S(2)}, u32[]{:S(2)}) collective-permute-start(bf16[256,2048]{1,0:T(8,128)(2,1)} %collective-permute-done.4.refs_7_.refs_9_), channel_id=1, source_target_pairs={{0,4},{4,0},{8,12},{12,8},{1,5},{5,1},{9,13},{13,9},{2,6},{6,2},{1... | collective-permute-start | bytes 3145736 | tf_op jit(solution)/shard_map/ppermute | solution.py:566
  72.1 26.5 %collective-permute-start.8 = (bf16[256,1024]{1,0:T(8,128)(2,1)S(1)}, bf16[256,1024]{1,0:T(8,128)(2,1)S(1)}, u32[]{:S(2)}, u32[]{:S(2)}) collective-permute-start(bf16[256,1024]{1,0:T(8,128)(2,1)S(1)} %bitcast.120), channel_id=1, source_target_pairs={{0,18},{1,19},{2,16},{3,17},{4,22},{5,23},{6,20},{7,21},{8,26},{9,... | collective-permute-start | bytes 1572872 | tf_op jit(solution)/shard_map/ppermute | solution.py:574
  102.4 13.5 %collective-permute-start.19 = (bf16[256,1024]{1,0:T(8,128)(2,1)}, bf16[256,1024]{1,0:T(8,128)(2,1)}, u32[]{:S(2)}, u32[]{:S(2)}) collective-permute-start(bf16[256,1024]{1,0:T(8,128)(2,1)} %add_convert_fusion.11), channel_id=1, source_target_pairs={{0,1},{1,0},{2,3},{3,2},{4,5},{5,4},{6,7},{7,6},{8,9},{9,8},{10,11... | collective-permute-start | bytes 1572872 | tf_op jit(solution)/shard_map/ppermute | solution.py:548
  103.8 34.5 %collective-permute-start.13 = (bf16[256,2048]{1,0:T(8,128)(2,1)}, bf16[256,2048]{1,0:T(8,128)(2,1)}, u32[]{:S(2)}, u32[]{:S(2)}) collective-permute-start(bf16[256,2048]{1,0:T(8,128)(2,1)} %collective-permute-done.9.refs_5_.refs_7_), channel_id=1, source_target_pairs={{0,1},{1,0},{2,3},{3,2},{4,5},{5,4},{6,7},{7,6},{8,9},{9,8},{10,11... | collective-permute-start | bytes 3145736 | tf_op jit(solution)/shard_map/ppermute | solution.py:548
  103.8 34.4 %collective-permute-start.14 = (bf16[256,2048]{1,0:T(8,128)(2,1)}, bf16[256,2048]{1,0:T(8,128)(2,1)}, u32[]{:S(2)}, u32[]{:S(2)}) collective-permute-start(bf16[256,2048]{1,0:T(8,128)(2,1)} %get-tuple-element.108.refs_5_), channel_id=1, source_target_pairs={{0,2},{1,3},{2,0},{3,1},{4,6},{5,7},{6,4},{7,5},{8,10},{9,11},{10,... | collective-permute-start | bytes 3145736 | tf_op jit(solution)/shard_map/ppermute | solution.py:561
  105.3 34.5 %collective-permute-start.12 = (bf16[512,1024]{1,0:T(8,128)(2,1)}, bf16[512,1024]{1,0:T(8,128)(2,1)}, u32[]{:S(2)}, u32[]{:S(2)}) collective-permute-start(bf16[512,1024]{1,0:T(8,128)(2,1)} %pad_maximum_fusion), channel_id=1, source_target_pairs={{16,2},{17,3},{18,0},{19,1},{20,6},{21,7},{22,4},{23,5},{24,10},{2... | collective-permute-start | bytes 3145736 | tf_op jit(solution)/shard_map/ppermute | solution.py:574
  110.1 29.7 %collective-permute-start.15 = (bf16[256,2048]{1,0:T(8,128)(2,1)}, bf16[256,2048]{1,0:T(8,128)(2,1)}, u32[]{:S(2)}, u32[]{:S(2)}) collective-permute-start(bf16[256,2048]{1,0:T(8,128)(2,1)} %collective-permute-done.10.refs_9_), channel_id=1, source_target_pairs={{0,4},{4,0},{8,12},{12,8},{1,5},{5,1},{9,13},{13,9},{2,6},{6,2},{1... | collective-permute-start | bytes 3145736 | tf_op jit(solution)/shard_map/ppermute | solution.py:566
  118.4 51.7 %collective-permute-start.25 = (f32[256,1024]{1,0:T(8,128)}, f32[256,1024]{1,0:T(8,128)}, u32[]{:S(2)}, u32[]{:S(2)}) collective-permute-start(f32[256,1024]{1,0:T(8,128)} %get-tuple-element.205), channel_id=1, source_target_pairs={{0,16},{16,0},{1,17},{17,1},{2,18},{18,2},{3,19},{19,3},{4,20},{20... | collective-permute-start | bytes 3145736 | tf_op jit(solution)/shard_map/ppermute | solution.py:540
  139.8 24.9 %collective-permute-start.20 = (bf16[256,2048]{1,0:T(8,128)(2,1)}, bf16[256,2048]{1,0:T(8,128)(2,1)}, u32[]{:S(2)}, u32[]{:S(2)}) collective-permute-start(bf16[256,2048]{1,0:T(8,128)(2,1)} %get-tuple-element.120.refs_4_.refs_6_), channel_id=1, source_target_pairs={{0,2},{1,3},{2,0},{3,1},{4,6},{5,7},{6,4},{7,5},{8,10},{9,11},{10,... | collective-permute-start | bytes 3145736 | tf_op jit(solution)/shard_map/ppermute | solution.py:561
  139.8 24.9 %collective-permute-start.21 = (bf16[256,2048]{1,0:T(8,128)(2,1)}, bf16[256,2048]{1,0:T(8,128)(2,1)}, u32[]{:S(2)}, u32[]{:S(2)}) collective-permute-start(bf16[256,2048]{1,0:T(8,128)(2,1)} %collective-permute-done.13.refs_9_.refs_11_), channel_id=1, source_target_pairs={{0,4},{4,0},{8,12},{12,8},{1,5},{5,1},{9,13},{13,9},{2,6},{6,2},{1... | collective-permute-start | bytes 3145736 | tf_op jit(solution)/shard_map/ppermute | solution.py:566
  141.4 23.3 %collective-permute-start.22 = (bf16[256,2048]{1,0:T(8,128)(2,1)}, bf16[256,2048]{1,0:T(8,128)(2,1)}, u32[]{:S(2)}, u32[]{:S(2)}) collective-permute-start(bf16[256,2048]{1,0:T(8,128)(2,1)} %collective-permute-done.14.refs_7_), channel_id=1, source_target_pairs={{0,1},{1,0},{2,3},{3,2},{4,5},{5,4},{6,7},{7,6},{8,9},{9,8},{10,11... | collective-permute-start | bytes 3145736 | tf_op jit(solution)/shard_map/ppermute | solution.py:548
  144.1 19.7 %collective-permute-start.23 = (bf16[2,2,1024]{2,1,0:T(2,128)(2,1)S(1)}, bf16[2,2,1024]{2,1,0:T(2,128)(2,1)S(1)}, u32[]{:S(2)}, u32[]{:S(2)}) collective-permute-start(bf16[2,2,1024]{2,1,0:T(2,128)(2,1)S(1)} %pad_maximum_fusion.13), channel_id=1, source_target_pairs={{0,2},{1,3},{2,0},{3,1},{4,6},{5,7},{6,4},{7,5},{8,10},{9,11},{10,... | collective-permute-start | bytes 24584 | tf_op jit(solution)/shard_map/ppermute | solution.py:561
  164.7 23.6 %collective-permute-start.26 = (bf16[256,2048]{1,0:T(8,128)(2,1)}, bf16[256,2048]{1,0:T(8,128)(2,1)}, u32[]{:S(2)}, u32[]{:S(2)}) collective-permute-start(bf16[256,2048]{1,0:T(8,128)(2,1)} %get-tuple-element.130.refs_6_), channel_id=1, source_target_pairs={{0,2},{1,3},{2,0},{3,1},{4,6},{5,7},{6,4},{7,5},{8,10},{9,11},{10,... | collective-permute-start | bytes 3145736 | tf_op jit(solution)/shard_map/ppermute | solution.py:561
  165.9 22.4 %collective-permute-start.27 = (bf16[256,2048]{1,0:T(8,128)(2,1)}, bf16[256,2048]{1,0:T(8,128)(2,1)}, u32[]{:S(2)}, u32[]{:S(2)}) collective-permute-start(bf16[256,2048]{1,0:T(8,128)(2,1)} %collective-permute-done.22.refs_11_), channel_id=1, source_target_pairs={{0,4},{4,0},{8,12},{12,8},{1,5},{5,1},{9,13},{13,9},{2,6},{6,2},{1... | collective-permute-start | bytes 3145736 | tf_op jit(solution)/shard_map/ppermute | solution.py:566
  166.3 20.2 %collective-permute-start.28 = (bf16[256,1024]{1,0:T(8,128)(2,1)}, bf16[256,1024]{1,0:T(8,128)(2,1)}, u32[]{:S(2)}, u32[]{:S(2)}) collective-permute-start(bf16[256,1024]{1,0:T(8,128)(2,1)} %copy-done.17), channel_id=1, source_target_pairs={{0,1},{1,0},{2,3},{3,2},{4,5},{5,4},{6,7},{7,6},{8,9},{9,8},{10,11... | collective-permute-start | bytes 1572872 | tf_op jit(solution)/shard_map/ppermute | solution.py:548
  169.9 18.4 %collective-permute-start.29 = (bf16[256,1024]{1,0:T(8,128)(2,1)}, bf16[256,1024]{1,0:T(8,128)(2,1)}, u32[]{:S(2)}, u32[]{:S(2)}) collective-permute-start(bf16[256,1024]{1,0:T(8,128)(2,1)} %get-tuple-element.134), channel_id=1, source_target_pairs={{0,1},{1,0},{2,3},{3,2},{4,5},{5,4},{6,7},{7,6},{8,9},{9,8},{10,11... | collective-permute-start | bytes 1572872 | tf_op jit(solution)/shard_map/ppermute | solution.py:548
  197.7 14.3 %collective-permute-start.33 = (bf16[512,512]{0,1:T(8,128)(2,1)S(1)}, bf16[512,512]{0,1:T(8,128)(2,1)S(1)}, u32[]{:S(2)}, u32[]{:S(2)}) collective-permute-start(bf16[512,512]{0,1:T(8,128)(2,1)S(1)} %bitcast.115), channel_id=1, source_target_pairs={{0,18},{1,19},{2,16},{3,17},{16,2},{17,3},{18,0},{19,1},{4,22},{5,... | collective-permute-start | bytes 1572872 | tf_op jit(solution)/shard_map/ppermute | solution.py:557
  291.4 14.3 %collective-permute-start.46 = (bf16[256,1024]{1,0:T(8,128)(2,1)S(1)}, bf16[256,1024]{1,0:T(8,128)(2,1)S(1)}, u32[]{:S(2)}, u32[]{:S(2)}) collective-permute-start(bf16[256,1024]{1,0:T(8,128)(2,1)S(1)} %get-tuple-element.211.high_own), channel_id=1, source_target_pairs={{0,18},{1,19},{2,16},{3,17},{4,22},{5,23},{6,20},{7,21},{8,26},{9,... | collective-permute-start | bytes 1572872 | tf_op jit(solution)/shard_map/ppermute | solution.py:574
  370.8 15.2 %collective-permute-start.54 = (bf16[256,1024]{1,0:T(8,128)(2,1)S(1)}, bf16[256,1024]{1,0:T(8,128)(2,1)S(1)}, u32[]{:S(2)}, u32[]{:S(2)}) collective-permute-start(bf16[256,1024]{1,0:T(8,128)(2,1)S(1)} %fusion.26.low_own), channel_id=1, source_target_pairs={{16,2},{17,3},{18,0},{19,1},{20,6},{21,7},{22,4},{23,5},{24,10},{2... | collective-permute-start | bytes 1572872 | tf_op jit(solution)/shard_map/ppermute | solution.py:574
  (92 other events, 685.8 us)

commit v5 on v4

--- a/solution.py
+++ b/solution.py
@@ -391,7 +391,7 @@
             pltpu.SemaphoreType.DMA((4,)),
             pltpu.SemaphoreType.DMA((2,)),
         ],
-        compiler_params=pltpu.CompilerParams(vmem_limit_bytes=20 << 20),
+        compiler_params=pltpu.CompilerParams(vmem_limit_bytes=58 << 20),
         cost_estimate=small_cost,
         name="feed_forward_chunks",
     )(place, up, down)
@@ -912,10 +912,11 @@
     normed_pair = (layer_0.norm_two(layer_0.middle), layer_0.norm_two(middle_peer))
 
     stages.next()
-    half_odd_1 = half_send(odd[1])
-    own_proj, far_pack = lax.optimization_barrier((proj_own, far_pack, *stages.before))[:2]
+    own_proj, far_pack = lax.optimization_barrier((proj_own, far_pack, layer_0.middle))[:2]
     cotangent = jnp.where(low, far_pack[head_width:], own_row)
     proj_1 = jnp.where(low, far_pack[:head_width], own_proj)
+    stages.before += [*normed_pair, proj_1, cotangent]
+    half_odd_1 = half_send(odd[1])
     projs = (layer_0.out, proj_1)
     if shared:
         corner_odd_1 = [plane_send(value) for value in corner_even_1]
@@ -984,12 +985,11 @@
     summed = tied(message, group.swapped)
     summed = group.sum_planes(summed)
     hidden_width = hidden_part.shape[1]
-    hidden_part = summed[:, :hidden_width]
-    hidden_grad = group.sum_shards(hidden_part)
     kept = summed[:, hidden_width : hidden_width + 2 * head_width]
-    sent = summed[:, hidden_width + 2 * head_width :]
+    came = group.cross(summed[:, hidden_width + 2 * head_width :])
+    hidden_grad = group.sum_shards(summed[:, :hidden_width])
     pad = ((0, prefix_rows - prefix_len), (0, 0))
-    w2_grad, b2_grad = second_grads(kept, group.cross(sent), jnp.pad(hidden_low, pad), heads_local)
+    w2_grad, b2_grad = second_grads(kept, came, jnp.pad(hidden_low, pad), heads_local)
     embed_grad, w1_grad, b1_grad = first_grads(
         hidden_grad, jnp.pad(curve, pad), jnp.pad(prefix_embed, pad), reparam_w1, prefix_len
     )

time: 393 us -> 385 us (0.980)
  other arithmetic: 40.4 us -> 31 us
  waiting for transfers between devices: 160 us -> 165 us
    ppermute x15, waiting for transfers between devices: 97.6 us -> 110 us  [shift(): return lax.ppermute(value, 'tensor', pairs)]
    ppermute x5, waiting for transfers between devices: 18.3 us -> 12.6 us  [half_swap(): return lax.ppermute(value, 'tensor', pairs)]
    unnamed x107 -> x157, local copies, waits for them, and re-layouts: 7.32 us -> 3.1 us
  transfers between devices with their start and end apart: 63 -> 63, of which waited for: 33 -> 35; matrix products, arithmetic and copies ran while one was open for 12% -> 10% of each run, Pallas kernels for 6% -> 6%
where the time goes in v5:
time: 385 us; the launch traced here: 380 us
  waiting for transfers between devices  165 us (43%)
  Pallas kernels  89.5 us (23%)
  starting transfers between devices  64.1 us (17%)
  other arithmetic  31 us (8%)
  matrix products  16.6 us (4%)
  local copies, waits for them, and re-layouts  11.8 us (3%)
    ppermute x15, waiting for transfers between devices, shift(): return lax.ppermute(value, 'tensor', pairs)  110 us
    pallas_call x3, Pallas kernels, feed_forward(): pl.pallas_call(functools.partial(feed_forward_kernel, groups, per, with_o...  39 us
    pallas_call x2, Pallas kernels, attention_backward(): pl.pallas_call(functools.partial(attention_backward_kernel, count, block_...  24.2 us
    ppermute x24, starting transfers between devices, core_swap(): return lax.ppermute(value, 'section', [(0, 1), (1, 0)])  23.6 us
    ppermute x5, waiting for transfers between devices, cross_from(): return lax.ppermute(value, ('section', 'tensor'), pairs)  19.5 us
    pallas_call x2, Pallas kernels, attention_forward(): pl.pallas_call(functools.partial(attention_forward_kernel, count, block_r...  16 us
    ppermute x24, waiting for transfers between devices, core_swap(): return lax.ppermute(value, 'section', [(0, 1), (1, 0)])  15.5 us
    ppermute x15, starting transfers between devices, shift(): return lax.ppermute(value, 'tensor', pairs)  13.2 us
  transfers between devices with their start and end apart: 63, of which 35 were waited for; matrix products, arithmetic and copies ran while one was open for 10% of the time, Pallas kernels for 6%

profile of v5, /device:TPU:1, one launch (start us, length us, event | category | flops | bytes accessed | tf_op | source)
XLA Modules:
  0.0 380.5 jit_solution(4723229015172311056)
XLA Ops:
  2.5 5.1 %feed_forward_chunks.1 = (bf16[2,256,2048]{2,1,0:T(8,128)(2,1)}, bf16[2,256,2048]{2,1,0:T(8,128)(2,1)}) custom-call(s32[2]{0:T(128)} %pad_add_fusion.1.place_ref, bf16[1024,1024]{1,0:T(8,128)(2,1)} %bitcast.122, bf16[1024,1024]{1,0:T(8,128)(2,1)} %bitcast.123), custom_call_target="tpu_custom_call" | custom-call | flops 1 | bytes 1 | tf_op jit(solution)/shard_map/feed_forward_chunks/pallas_call | solution.py:382
  14.5 4.0 %collective-permute-done.1 = bf16[256,1024]{1,0:T(8,128)(2,1)S(1)} collective-permute-done((bf16[256,1024]{1,0:T(8,128)(2,1)S(1)}, bf16[256,1024]{1,0:T(8,128)(2,1)S(1)}, u32[]{:S(2)}, u32[]{:S(2)}) %collective-permute-start.1) | collective-permute-done | bytes 524320 | tf_op jit(solution)/shard_map/ppermute | solution.py:574
  30.3 17.6 %collective-permute-done.4.refs_7_.refs_9_ = bf16[256,2048]{1,0:T(8,128)(2,1)} collective-permute-done((bf16[256,2048]{1,0:T(8,128)(2,1)}, bf16[256,2048]{1,0:T(8,128)(2,1)}, u32[]{:S(2)}, u32[]{:S(2)}) %collective-permute-start.4) | collective-permute-done | bytes 1048608 | tf_op jit(solution)/shard_map/ppermute | solution.py:548
  52.9 8.0 %collective-permute-done.5 = bf16[256,1024]{1,0:T(8,128)(2,1)S(1)} collective-permute-done((bf16[256,1024]{1,0:T(8,128)(2,1)S(1)}, bf16[256,1024]{1,0:T(8,128)(2,1)S(1)}, u32[]{:S(2)}, u32[]{:S(2)}) %collective-permute-start.5) | collective-permute-done | bytes 524320 | tf_op jit(solution)/shard_map/ppermute | solution.py:548
  72.0 8.0 %attention_forward.2 = (bf16[512,256]{1,0:T(8,128)(2,1)S(1)}, bf16[512,256]{1,0:T(8,128)(2,1)S(1)}, f32[8,1024]{1,0:T(8,128)S(1)}) custom-call(s32[4]{0:T(128)S(1)} %pad_add_fusion.2.order_ref, bf16[512,768]{1,0:T(8,128)(2,1)S(1)} %add_convert_fusion.3.refs_0_, bf16[512,768]{1,0:T(8,128)(2,1)S(1)} %add_convert_fusion.2.refs_1_, ...), custom_call_target="tpu_custom_call" | custom-call | flops 1 | bytes 1 | tf_op jit(solution)/shard_map/attention_forward/pallas_call | solution.py:288
  80.0 15.1 %collective-permute-done.8 = bf16[256,1024]{1,0:T(8,128)(2,1)S(1)} collective-permute-done((bf16[256,1024]{1,0:T(8,128)(2,1)S(1)}, bf16[256,1024]{1,0:T(8,128)(2,1)S(1)}, u32[]{:S(2)}, u32[]{:S(2)}) %collective-permute-start.8) | collective-permute-done | bytes 524320 | tf_op jit(solution)/shard_map/ppermute | solution.py:574
  106.2 5.9 %collective-permute-done.16 = bf16[256,1024]{1,0:T(8,128)(2,1)S(1)} collective-permute-done((bf16[256,1024]{1,0:T(8,128)(2,1)S(1)}, bf16[256,1024]{1,0:T(8,128)(2,1)S(1)}, u32[]{:S(2)}, u32[]{:S(2)}) %collective-permute-start.16) | collective-permute-done | bytes 524320 | tf_op jit(solution)/shard_map/ppermute | solution.py:548
  114.2 20.4 %collective-permute-done.19.refs_9_.refs_11_ = bf16[256,2048]{1,0:T(8,128)(2,1)} collective-permute-done((bf16[256,2048]{1,0:T(8,128)(2,1)S(1)}, bf16[256,2048]{1,0:T(8,128)(2,1)}, u32[]{:S(2)}, u32[]{:S(2)}) %collective-permute-start.19) | collective-permute-done | bytes 1048608 | tf_op jit(solution)/shard_map/ppermute | solution.py:548
  146.3 12.6 %collective-permute-done.22.refs_6_.refs_8_ = bf16[256,2048]{1,0:T(8,128)(2,1)} collective-permute-done((bf16[256,2048]{1,0:T(8,128)(2,1)}, bf16[256,2048]{1,0:T(8,128)(2,1)}, u32[]{:S(2)}, u32[]{:S(2)}) %collective-permute-start.22) | collective-permute-done | bytes 1048608 | tf_op jit(solution)/shard_map/ppermute | solution.py:561
  164.4 10.5 %feed_forward.3 = (f32[256,1024]{1,0:T(8,128)}, bf16[256,1024]{1,0:T(8,128)(2,1)}) custom-call(bf16[256,1024]{1,0:T(8,128)(2,1)} %get-tuple-element.128.refs_0_.refs_1_, bf16[256,1024]{1,0:T(8,128)(2,1)} %get-tuple-element.246.refs_1_.refs_0_, f32[4,1,512]{2,1,0:T(1,128)} %reshape_squeeze.7.refs_2_, bf16[256,2048]{1,0:T(8,128)(2,1)} %fusion.29.refs_3_.refs_5_, ...), custom_call_target="tpu_custom_call" | custom-call | flops 1 | bytes 1 | tf_op jit(solution)/shard_map/feed_forward/pallas_call | solution.py:408
  174.9 7.5 %collective-permute-done.29 = bf16[256,1024]{1,0:T(8,128)(2,1)} collective-permute-done((bf16[256,1024]{1,0:T(8,128)(2,1)}, bf16[256,1024]{1,0:T(8,128)(2,1)}, u32[]{:S(2)}, u32[]{:S(2)}) %collective-permute-start.29) | collective-permute-done | bytes 524320 | tf_op jit(solution)/shard_map/ppermute | solution.py:548
  182.4 4.8 %collective-permute-start.30 = (bf16[256,1024]{1,0:T(8,128)(2,1)}, bf16[256,1024]{1,0:T(8,128)(2,1)S(1)}, u32[]{:S(2)}, u32[]{:S(2)}) collective-permute-start(bf16[256,1024]{1,0:T(8,128)(2,1)} %get-tuple-element.135), channel_id=1, source_target_pairs={{0,16},{16,0},{1,17},{17,1},{2,18},{18,2},{3,19},{19,3},{4,20},{20... | collective-permute-start | bytes 1572872 | tf_op jit(solution)/shard_map/ppermute | solution.py:540
  194.1 10.7 %collective-permute-done.31 = bf16[256,1024]{1,0:T(8,128)(2,1)S(1)} collective-permute-done((bf16[256,1024]{1,0:T(8,128)(2,1)S(1)}, bf16[256,1024]{1,0:T(8,128)(2,1)S(1)}, u32[]{:S(2)}, u32[]{:S(2)}) %collective-permute-start.31) | collective-permute-done | bytes 524320 | tf_op jit(solution)/shard_map/ppermute | solution.py:548
  211.1 8.0 %attention_forward.3 = (bf16[512,256]{1,0:T(8,128)(2,1)S(1)}, bf16[512,256]{1,0:T(8,128)(2,1)S(1)}, f32[8,1024]{1,0:T(8,128)S(1)}) custom-call(s32[4]{0:T(128)S(1)} %pad_add_fusion.3.order_ref, bf16[512,768]{1,0:T(8,128)(2,1)S(1)} %add_convert_fusion.1.refs_0_, bf16[512,768]{1,0:T(8,128)(2,1)S(1)} %add_convert_fusion.refs_1_, ...), custom_call_target="tpu_custom_call" | custom-call | flops 1 | bytes 1 | tf_op jit(solution)/shard_map/attention_forward/pallas_call | solution.py:288
  219.4 6.2 %collective-permute-done.35 = bf16[512,256]{1,0:T(8,128)(2,1)S(1)} collective-permute-done((bf16[512,256]{1,0:T(8,128)(2,1)S(1)}, bf16[512,256]{1,0:T(8,128)(2,1)S(1)}, u32[]{:S(2)}, u32[]{:S(2)}) %collective-permute-start.35) | collective-permute-done | bytes 262176 | tf_op jit(solution)/shard_map/ppermute | solution.py:548
  236.3 15.6 %feed_forward.4 = (f32[256,1024]{1,0:T(8,128)}, bf16[256,1024]{1,0:T(8,128)(2,1)}, f32[256,1024]{1,0:T(8,128)}, bf16[256,1024]{1,0:T(8,128)(2,1)}) custom-call(bf16[256,1024]{1,0:T(8,128)(2,1)} %add_convert_fusion.7.refs_0_, bf16[256,1024]{1,0:T(8,128)(2,1)} %collective-permute-done.37.refs_1_, f32[4,1,512]{2,1,0:T(1,128)} %reshape_squeeze.8.refs_2_, ...), custom_call_target="tpu_custom_call" | custom-call | flops 1 | bytes 1 | tf_op jit(solution)/shard_map/feed_forward/pallas_call | solution.py:408
  262.0 6.8 %collective-permute-done.41.refs_3_ = bf16[512,256]{1,0:T(8,128)(2,1)S(1)} collective-permute-done((bf16[512,256]{1,0:T(8,128)(2,1)S(1)}, bf16[512,256]{1,0:T(8,128)(2,1)S(1)}, u32[]{:S(2)}, u32[]{:S(2)}) %collective-permute-start.41) | collective-permute-done | bytes 262176 | tf_op jit(solution)/shard_map/ppermute | solution.py:548
  268.8 12.1 %attention_backward.2 = (bf16[512,768]{1,0:T(8,128)(2,1)S(1)}, bf16[512,768]{1,0:T(8,128)(2,1)S(1)}, f32[2,16,256]{2,1,0:T(8,128)S(1)}) custom-call(s32[4]{0:T(128)S(1)} %pad_add_fusion.3.order_ref, bf16[512,768]{1,0:T(8,128)(2,1)S(1)} %add_convert_fusion.1.refs_0_, bf16[512,768]{1,0:T(8,128)(2,1)S(1)} %copy-done.2, ...), custom_call_target="tpu_custom_call" | custom-call | flops 1 | bytes 1 | tf_op jit(solution)/shard_map/attention_backward/pallas_call | solution.py:316
  286.9 11.8 %collective-permute-done.43 = bf16[256,1024]{1,0:T(8,128)(2,1)S(1)} collective-permute-done((bf16[256,1024]{1,0:T(8,128)(2,1)S(1)}, bf16[256,1024]{1,0:T(8,128)(2,1)S(1)}, u32[]{:S(2)}, u32[]{:S(2)}) %collective-permute-start.43) | collective-permute-done | bytes 524320 | tf_op jit(solution)/shard_map/ppermute | solution.py:548
  303.3 12.9 %feed_forward.5 = (f32[256,1024]{1,0:T(8,128)}, bf16[256,1024]{1,0:T(8,128)(2,1)}) custom-call(bf16[256,1024]{1,0:T(8,128)(2,1)} %get-tuple-element.246.refs_1_.refs_0_, bf16[256,1024]{1,0:T(8,128)(2,1)} %get-tuple-element.128.refs_0_.refs_1_, f32[4,1,512]{2,1,0:T(1,128)} %reshape_squeeze.7.refs_2_, bf16[256,1024]{1,0:T(8,128)(2,1)} %copy-done.29, ...), custom_call_target="tpu_custom_call" | custom-call | flops 1 | bytes 1 | tf_op jit(solution)/shard_map/feed_forward/pallas_call | solution.py:408
  325.3 6.4 %collective-permute-done.50.refs_3_ = bf16[512,256]{1,0:T(8,128)(2,1)S(1)} collective-permute-done((bf16[512,256]{1,0:T(8,128)(2,1)S(1)}, bf16[512,256]{1,0:T(8,128)(2,1)S(1)}, u32[]{:S(2)}, u32[]{:S(2)}) %collective-permute-start.50) | collective-permute-done | bytes 262176 | tf_op jit(solution)/shard_map/ppermute | solution.py:548
  331.7 12.1 %attention_backward.3 = (bf16[512,768]{1,0:T(8,128)(2,1)S(1)}, bf16[512,768]{1,0:T(8,128)(2,1)S(1)}, f32[2,16,256]{2,1,0:T(8,128)S(1)}) custom-call(s32[4]{0:T(128)S(1)} %pad_add_fusion.2.order_ref, bf16[512,768]{1,0:T(8,128)(2,1)S(1)} %add_convert_fusion.3.refs_0_, bf16[512,768]{1,0:T(8,128)(2,1)S(1)} %add_convert_fusion.2.refs_1_, ...), custom_call_target="tpu_custom_call" | custom-call | flops 1 | bytes 1 | tf_op jit(solution)/shard_map/attention_backward/pallas_call | solution.py:316
  353.9 7.1 %collective-permute-done.52 = bf16[256,1024]{1,0:T(8,128)(2,1)S(1)} collective-permute-done((bf16[256,1024]{1,0:T(8,128)(2,1)S(1)}, bf16[256,1024]{1,0:T(8,128)(2,1)S(1)}, u32[]{:S(2)}, u32[]{:S(2)}) %collective-permute-start.52) | collective-permute-done | bytes 524320 | tf_op jit(solution)/shard_map/ppermute | solution.py:548
  369.9 5.2 %collective-permute-done.60 = f32[16,512]{1,0:T(8,128)S(1)} collective-permute-done((f32[16,512]{1,0:T(8,128)S(1)}, f32[16,512]{1,0:T(8,128)S(1)}, u32[]{:S(2)}, u32[]{:S(2)}) %collective-permute-start.60) | collective-permute-done | bytes 32800 | tf_op jit(solution)/shard_map/ppermute | solution.py:590
  (397 shorter events, 143.4 us)
Async XLA Ops:
  21.8 26.1 %collective-permute-start.4 = (bf16[256,2048]{1,0:T(8,128)(2,1)}, bf16[256,2048]{1,0:T(8,128)(2,1)}, u32[]{:S(2)}, u32[]{:S(2)}) collective-permute-start(bf16[256,2048]{1,0:T(8,128)(2,1)} %fusion.29.refs_3_.refs_5_), channel_id=1, source_target_pairs={{0,1},{1,0},{2,3},{3,2},{4,5},{5,4},{6,7},{7,6},{8,9},{9,8},{10,11... | collective-permute-start | bytes 3145736 | tf_op jit(solution)/shard_map/ppermute | solution.py:548
  24.2 28.7 %collective-permute-start.6 = (bf16[2,1024]{1,0:T(2,128)(2,1)S(1)}, bf16[2,1024]{1,0:T(2,128)(2,1)S(1)}, u32[]{:S(2)}, u32[]{:S(2)}) collective-permute-start(bf16[2,1024]{1,0:T(2,128)(2,1)S(1)} %bitcast.151), channel_id=1, source_target_pairs={{0,1},{1,0},{2,3},{3,2},{4,5},{5,4},{6,7},{7,6},{8,9},{9,8},{10,11... | collective-permute-start | bytes 12296 | tf_op jit(solution)/shard_map/ppermute | solution.py:548
  24.5 36.8 %collective-permute-start.2 = (bf16[1024,768]{0,1:T(8,128)(2,1)S(1)}, bf16[1024,768]{0,1:T(8,128)(2,1)}, u32[]{:S(2)}, u32[]{:S(2)}) collective-permute-start(bf16[1024,768]{0,1:T(8,128)(2,1)S(1)} %bitcast.112), channel_id=1, source_target_pairs={{0,18},{1,19},{2,16},{3,17},{16,2},{17,3},{18,0},{19,1},{4,22},{5,... | collective-permute-start | bytes 4718600 | tf_op jit(solution)/shard_map/ppermute | solution.py:557
  64.3 30.9 %collective-permute-start.9 = (bf16[256,2048]{1,0:T(8,128)(2,1)}, bf16[256,2048]{1,0:T(8,128)(2,1)S(1)}, u32[]{:S(2)}, u32[]{:S(2)}) collective-permute-start(bf16[256,2048]{1,0:T(8,128)(2,1)} %fusion.29.refs_3_.refs_5_), channel_id=1, source_target_pairs={{0,2},{1,3},{2,0},{3,1},{4,6},{5,7},{6,4},{7,5},{8,10},{9,11},{10,... | collective-permute-start | bytes 3145736 | tf_op jit(solution)/shard_map/ppermute | solution.py:561
  65.6 29.6 %collective-permute-start.10 = (bf16[256,2048]{1,0:T(8,128)(2,1)S(1)}, bf16[256,2048]{1,0:T(8,128)(2,1)S(1)}, u32[]{:S(2)}, u32[]{:S(2)}) collective-permute-start(bf16[256,2048]{1,0:T(8,128)(2,1)S(1)} %get-tuple-element.121.refs_5_), channel_id=1, source_target_pairs={{0,1},{1,0},{2,3},{3,2},{4,5},{5,4},{6,7},{7,6},{8,9},{9,8},{10,11... | collective-permute-start | bytes 3145736 | tf_op jit(solution)/shard_map/ppermute | solution.py:548
  67.0 28.1 %collective-permute-start.11 = (bf16[256,2048]{1,0:T(8,128)(2,1)}, bf16[256,2048]{1,0:T(8,128)(2,1)S(1)}, u32[]{:S(2)}, u32[]{:S(2)}) collective-permute-start(bf16[256,2048]{1,0:T(8,128)(2,1)} %collective-permute-done.4.refs_7_.refs_9_), channel_id=1, source_target_pairs={{0,4},{4,0},{8,12},{12,8},{1,5},{5,1},{9,13},{13,9},{2,6},{6,2},{1... | collective-permute-start | bytes 3145736 | tf_op jit(solution)/shard_map/ppermute | solution.py:566
  68.4 26.6 %collective-permute-start.8 = (bf16[256,1024]{1,0:T(8,128)(2,1)S(1)}, bf16[256,1024]{1,0:T(8,128)(2,1)S(1)}, u32[]{:S(2)}, u32[]{:S(2)}) collective-permute-start(bf16[256,1024]{1,0:T(8,128)(2,1)S(1)} %bitcast.119), channel_id=1, source_target_pairs={{0,18},{1,19},{2,16},{3,17},{4,22},{5,23},{6,20},{7,21},{8,26},{9,... | collective-permute-start | bytes 1572872 | tf_op jit(solution)/shard_map/ppermute | solution.py:574
  98.1 14.1 %collective-permute-start.16 = (bf16[256,1024]{1,0:T(8,128)(2,1)S(1)}, bf16[256,1024]{1,0:T(8,128)(2,1)S(1)}, u32[]{:S(2)}, u32[]{:S(2)}) collective-permute-start(bf16[256,1024]{1,0:T(8,128)(2,1)S(1)} %add_convert_fusion.11), channel_id=1, source_target_pairs={{0,1},{1,0},{2,3},{3,2},{4,5},{5,4},{6,7},{7,6},{8,9},{9,8},{10,11... | collective-permute-start | bytes 1572872 | tf_op jit(solution)/shard_map/ppermute | solution.py:548
  100.0 34.6 %collective-permute-start.19 = (bf16[256,2048]{1,0:T(8,128)(2,1)S(1)}, bf16[256,2048]{1,0:T(8,128)(2,1)}, u32[]{:S(2)}, u32[]{:S(2)}) collective-permute-start(bf16[256,2048]{1,0:T(8,128)(2,1)S(1)} %collective-permute-done.9.refs_5_.refs_7_), channel_id=1, source_target_pairs={{0,1},{1,0},{2,3},{3,2},{4,5},{5,4},{6,7},{7,6},{8,9},{9,8},{10,11... | collective-permute-start | bytes 3145736 | tf_op jit(solution)/shard_map/ppermute | solution.py:548
  100.1 34.5 %collective-permute-start.20 = (bf16[256,2048]{1,0:T(8,128)(2,1)S(1)}, bf16[256,2048]{1,0:T(8,128)(2,1)}, u32[]{:S(2)}, u32[]{:S(2)}) collective-permute-start(bf16[256,2048]{1,0:T(8,128)(2,1)S(1)} %get-tuple-element.121.refs_5_), channel_id=1, source_target_pairs={{0,2},{1,3},{2,0},{3,1},{4,6},{5,7},{6,4},{7,5},{8,10},{9,11},{10,... | collective-permute-start | bytes 3145736 | tf_op jit(solution)/shard_map/ppermute | solution.py:561
  100.8 34.2 %collective-permute-start.12 = (bf16[512,1024]{1,0:T(8,128)(2,1)S(1)}, bf16[512,1024]{1,0:T(8,128)(2,1)S(1)}, u32[]{:S(2)}, u32[]{:S(2)}) collective-permute-start(bf16[512,1024]{1,0:T(8,128)(2,1)S(1)} %pad_maximum_fusion), channel_id=1, source_target_pairs={{16,2},{17,3},{18,0},{19,1},{20,6},{21,7},{22,4},{23,5},{24,10},{2... | collective-permute-start | bytes 3145736 | tf_op jit(solution)/shard_map/ppermute | solution.py:574
  104.4 30.7 %collective-permute-start.21 = (bf16[256,2048]{1,0:T(8,128)(2,1)S(1)}, bf16[256,2048]{1,0:T(8,128)(2,1)S(1)}, u32[]{:S(2)}, u32[]{:S(2)}) collective-permute-start(bf16[256,2048]{1,0:T(8,128)(2,1)S(1)} %collective-permute-done.10.refs_9_), channel_id=1, source_target_pairs={{0,4},{4,0},{8,12},{12,8},{1,5},{5,1},{9,13},{13,9},{2,6},{6,2},{1... | collective-permute-start | bytes 3145736 | tf_op jit(solution)/shard_map/ppermute | solution.py:566
  112.5 27.8 %collective-permute-start.18 = (f32[256,1024]{1,0:T(8,128)S(1)}, f32[256,1024]{1,0:T(8,128)}, u32[]{:S(2)}, u32[]{:S(2)}) collective-permute-start(f32[256,1024]{1,0:T(8,128)S(1)} %get-tuple-element.205), channel_id=1, source_target_pairs={{0,16},{16,0},{1,17},{17,1},{2,18},{18,2},{3,19},{19,3},{4,20},{20... | collective-permute-start | bytes 3145736 | tf_op jit(solution)/shard_map/ppermute | solution.py:540
  135.8 23.0 %collective-permute-start.22 = (bf16[256,2048]{1,0:T(8,128)(2,1)}, bf16[256,2048]{1,0:T(8,128)(2,1)}, u32[]{:S(2)}, u32[]{:S(2)}) collective-permute-start(bf16[256,2048]{1,0:T(8,128)(2,1)} %get-tuple-element.123.refs_4_.refs_6_), channel_id=1, source_target_pairs={{0,2},{1,3},{2,0},{3,1},{4,6},{5,7},{6,4},{7,5},{8,10},{9,11},{10,... | collective-permute-start | bytes 3145736 | tf_op jit(solution)/shard_map/ppermute | solution.py:561
  136.5 22.6 %collective-permute-start.23 = (bf16[256,2048]{1,0:T(8,128)(2,1)}, bf16[256,2048]{1,0:T(8,128)(2,1)}, u32[]{:S(2)}, u32[]{:S(2)}) collective-permute-start(bf16[256,2048]{1,0:T(8,128)(2,1)} %collective-permute-done.19.refs_9_.refs_11_), channel_id=1, source_target_pairs={{0,4},{4,0},{8,12},{12,8},{1,5},{5,1},{9,13},{13,9},{2,6},{6,2},{1... | collective-permute-start | bytes 3145736 | tf_op jit(solution)/shard_map/ppermute | solution.py:566
  138.0 22.2 %collective-permute-start.24 = (bf16[256,2048]{1,0:T(8,128)(2,1)}, bf16[256,2048]{1,0:T(8,128)(2,1)}, u32[]{:S(2)}, u32[]{:S(2)}) collective-permute-start(bf16[256,2048]{1,0:T(8,128)(2,1)} %collective-permute-done.20.refs_7_), channel_id=1, source_target_pairs={{0,1},{1,0},{2,3},{3,2},{4,5},{5,4},{6,7},{7,6},{8,9},{9,8},{10,11... | collective-permute-start | bytes 3145736 | tf_op jit(solution)/shard_map/ppermute | solution.py:548
  160.2 22.2 %collective-permute-start.26 = (bf16[256,2048]{1,0:T(8,128)(2,1)}, bf16[256,2048]{1,0:T(8,128)(2,1)}, u32[]{:S(2)}, u32[]{:S(2)}) collective-permute-start(bf16[256,2048]{1,0:T(8,128)(2,1)} %get-tuple-element.131.refs_6_), channel_id=1, source_target_pairs={{0,2},{1,3},{2,0},{3,1},{4,6},{5,7},{6,4},{7,5},{8,10},{9,11},{10,... | collective-permute-start | bytes 3145736 | tf_op jit(solution)/shard_map/ppermute | solution.py:561
  161.0 21.4 %collective-permute-start.27 = (bf16[256,2048]{1,0:T(8,128)(2,1)}, bf16[256,2048]{1,0:T(8,128)(2,1)}, u32[]{:S(2)}, u32[]{:S(2)}) collective-permute-start(bf16[256,2048]{1,0:T(8,128)(2,1)} %collective-permute-done.24.refs_11_), channel_id=1, source_target_pairs={{0,4},{4,0},{8,12},{12,8},{1,5},{5,1},{9,13},{13,9},{2,6},{6,2},{1... | collective-permute-start | bytes 3145736 | tf_op jit(solution)/shard_map/ppermute | solution.py:566
  161.5 13.4 %collective-permute-start.28 = (bf16[256,1024]{1,0:T(8,128)(2,1)S(1)}, bf16[256,1024]{1,0:T(8,128)(2,1)}, u32[]{:S(2)}, u32[]{:S(2)}) collective-permute-start(bf16[256,1024]{1,0:T(8,128)(2,1)S(1)} %copy-done.17), channel_id=1, source_target_pairs={{0,1},{1,0},{2,3},{3,2},{4,5},{5,4},{6,7},{7,6},{8,9},{9,8},{10,11... | collective-permute-start | bytes 1572872 | tf_op jit(solution)/shard_map/ppermute | solution.py:548
  162.7 19.7 %collective-permute-start.29 = (bf16[256,1024]{1,0:T(8,128)(2,1)}, bf16[256,1024]{1,0:T(8,128)(2,1)}, u32[]{:S(2)}, u32[]{:S(2)}) collective-permute-start(bf16[256,1024]{1,0:T(8,128)(2,1)} %get-tuple-element.134), channel_id=1, source_target_pairs={{0,1},{1,0},{2,3},{3,2},{4,5},{5,4},{6,7},{7,6},{8,9},{9,8},{10,11... | collective-permute-start | bytes 1572872 | tf_op jit(solution)/shard_map/ppermute | solution.py:548
  192.8 14.4 %collective-permute-start.33 = (bf16[512,512]{0,1:T(8,128)(2,1)S(1)}, bf16[512,512]{0,1:T(8,128)(2,1)S(1)}, u32[]{:S(2)}, u32[]{:S(2)}) collective-permute-start(bf16[512,512]{0,1:T(8,128)(2,1)S(1)} %bitcast.115), channel_id=1, source_target_pairs={{0,18},{1,19},{2,16},{3,17},{16,2},{17,3},{18,0},{19,1},{4,22},{5,... | collective-permute-start | bytes 1572872 | tf_op jit(solution)/shard_map/ppermute | solution.py:557
  285.4 13.4 %collective-permute-start.43 = (bf16[256,1024]{1,0:T(8,128)(2,1)S(1)}, bf16[256,1024]{1,0:T(8,128)(2,1)S(1)}, u32[]{:S(2)}, u32[]{:S(2)}) collective-permute-start(bf16[256,1024]{1,0:T(8,128)(2,1)S(1)} %add_convert_fusion.6), channel_id=1, source_target_pairs={{0,1},{1,0},{2,3},{3,2},{4,5},{5,4},{6,7},{7,6},{8,9},{9,8},{10,11... | collective-permute-start | bytes 1572872 | tf_op jit(solution)/shard_map/ppermute | solution.py:548
  285.6 14.3 %collective-permute-start.46 = (bf16[256,1024]{1,0:T(8,128)(2,1)S(1)}, bf16[256,1024]{1,0:T(8,128)(2,1)S(1)}, u32[]{:S(2)}, u32[]{:S(2)}) collective-permute-start(bf16[256,1024]{1,0:T(8,128)(2,1)S(1)} %get-tuple-element.211.high_own), channel_id=1, source_target_pairs={{0,18},{1,19},{2,16},{3,17},{4,22},{5,23},{6,20},{7,21},{8,26},{9,... | collective-permute-start | bytes 1572872 | tf_op jit(solution)/shard_map/ppermute | solution.py:574
  363.5 15.2 %collective-permute-start.54 = (bf16[256,1024]{1,0:T(8,128)(2,1)S(1)}, bf16[256,1024]{1,0:T(8,128)(2,1)S(1)}, u32[]{:S(2)}, u32[]{:S(2)}) collective-permute-start(bf16[256,1024]{1,0:T(8,128)(2,1)S(1)} %fusion.26.low_own), channel_id=1, source_target_pairs={{16,2},{17,3},{18,0},{19,1},{20,6},{21,7},{22,4},{23,5},{24,10},{2... | collective-permute-start | bytes 1572872 | tf_op jit(solution)/shard_map/ppermute | solution.py:574
  (117 other events, 1168.9 us)

commit v6 on v5

--- a/solution.py
+++ b/solution.py
@@ -773,10 +773,10 @@
     side_bias = small_chip[:, 6, : w_up.shape[2]]
     side_bias = jnp.stack([side_bias] + group.shifts(stages, side_bias), axis=1)
     qkv_far = stages.send(group.cross, qkv_own)
+    proj_far_0 = far(proj_own, 0)
 
     stages.next()
     pairs = layer_pair(pairs_own, stages.send(group.cross, pairs_own))
-    proj_far_0 = far(proj_own, 0)
     half_even_0 = half_send(even[0])
     side_even_1 = group.shifts(stages, even[1])
     if shared:

time: 385 us -> 393 us (1.021)
  starting transfers between devices: 64.1 us -> 70.5 us
    ppermute x5, waiting for transfers between devices: 19.5 us -> 4.97 us  [cross_from(): return lax.ppermute(value, ('section', 'tensor'), pairs)]
    ppermute x5, waiting for transfers between devices: 12.6 us -> 22.4 us  [half_swap(): return lax.ppermute(value, 'tensor', pairs)]
    ppermute x15, waiting for transfers between devices: 110 us -> 102 us  [shift(): return lax.ppermute(value, 'tensor', pairs)]
    ppermute x4, waiting for transfers between devices: 1.58 us -> 8.07 us  [cross(): return lax.ppermute(value, ('section', 'tensor'), pairs)]
    ppermute x4, starting transfers between devices: 1.8 us -> 6.89 us  [cross(): return lax.ppermute(value, ('section', 'tensor'), pairs)]
  transfers between devices with their start and end apart: 63 -> 63, of which waited for: 35 -> 37; matrix products, arithmetic and copies ran while one was open for 10% -> 10% of each run, Pallas kernels for 6% -> 6%
where the time goes in v6:
time: 393 us; the launch traced here: 386 us
  waiting for transfers between devices  162 us (41%)
  Pallas kernels  89.1 us (23%)
  starting transfers between devices  70.5 us (18%)
  other arithmetic  34.6 us (9%)
  matrix products  16.6 us (4%)
  local copies, waits for them, and re-layouts  11.4 us (3%)
    ppermute x15, waiting for transfers between devices, shift(): return lax.ppermute(value, 'tensor', pairs)  102 us
    pallas_call x3, Pallas kernels, feed_forward(): pl.pallas_call(functools.partial(feed_forward_kernel, groups, per, with_o...  38.6 us
    pallas_call x2, Pallas kernels, attention_backward(): pl.pallas_call(functools.partial(attention_backward_kernel, count, block_...  24.2 us
    ppermute x24, starting transfers between devices, core_swap(): return lax.ppermute(value, 'section', [(0, 1), (1, 0)])  24 us
    ppermute x5, waiting for transfers between devices, half_swap(): return lax.ppermute(value, 'tensor', pairs)  22.4 us
    pallas_call x2, Pallas kernels, attention_forward(): pl.pallas_call(functools.partial(attention_forward_kernel, count, block_r...  16 us
    ppermute x24, waiting for transfers between devices, core_swap(): return lax.ppermute(value, 'section', [(0, 1), (1, 0)])  15.6 us
    ppermute x15, starting transfers between devices, shift(): return lax.ppermute(value, 'tensor', pairs)  15.4 us
  transfers between devices with their start and end apart: 63, of which 37 were waited for; matrix products, arithmetic and copies ran while one was open for 10% of the time, Pallas kernels for 6%

profile of v6, /device:TPU:1, one launch (start us, length us, event | category | flops | bytes accessed | tf_op | source)
XLA Modules:
  0.0 386.2 jit_solution(5915234785211472990)
XLA Ops:
  2.5 5.1 %feed_forward_chunks.1 = (bf16[2,256,2048]{2,1,0:T(8,128)(2,1)}, bf16[2,256,2048]{2,1,0:T(8,128)(2,1)}) custom-call(s32[2]{0:T(128)} %pad_add_fusion.1.place_ref, bf16[1024,1024]{1,0:T(8,128)(2,1)} %bitcast.118, bf16[1024,1024]{1,0:T(8,128)(2,1)} %bitcast.119), custom_call_target="tpu_custom_call" | custom-call | flops 1 | bytes 1 | tf_op jit(solution)/shard_map/feed_forward_chunks/pallas_call | solution.py:382
  34.8 13.1 %collective-permute-done.4.refs_7_.refs_9_ = bf16[256,2048]{1,0:T(8,128)(2,1)} collective-permute-done((bf16[256,2048]{1,0:T(8,128)(2,1)}, bf16[256,2048]{1,0:T(8,128)(2,1)}, u32[]{:S(2)}, u32[]{:S(2)}) %collective-permute-start.4) | collective-permute-done | bytes 1048608 | tf_op jit(solution)/shard_map/ppermute | solution.py:548
  52.9 8.0 %collective-permute-done.5 = bf16[256,1024]{1,0:T(8,128)(2,1)S(1)} collective-permute-done((bf16[256,1024]{1,0:T(8,128)(2,1)S(1)}, bf16[256,1024]{1,0:T(8,128)(2,1)S(1)}, u32[]{:S(2)}, u32[]{:S(2)}) %collective-permute-start.5) | collective-permute-done | bytes 524320 | tf_op jit(solution)/shard_map/ppermute | solution.py:548
  61.0 7.8 %collective-permute-done.2 = bf16[1024,768]{0,1:T(8,128)(2,1)} collective-permute-done((bf16[1024,768]{0,1:T(8,128)(2,1)S(1)}, bf16[1024,768]{0,1:T(8,128)(2,1)}, u32[]{:S(2)}, u32[]{:S(2)}) %collective-permute-start.2) | collective-permute-done | bytes 1572896 | tf_op jit(solution)/shard_map/ppermute | solution.py:557
  78.9 8.0 %attention_forward.2 = (bf16[512,256]{1,0:T(8,128)(2,1)S(1)}, bf16[512,256]{1,0:T(8,128)(2,1)S(1)}, f32[8,1024]{1,0:T(8,128)S(1)}) custom-call(s32[4]{0:T(128)S(1)} %pad_add_fusion.2.order_ref, bf16[512,768]{1,0:T(8,128)(2,1)S(1)} %add_convert_fusion.3.refs_0_, bf16[512,768]{1,0:T(8,128)(2,1)S(1)} %add_convert_fusion.2.refs_1_, ...), custom_call_target="tpu_custom_call" | custom-call | flops 1 | bytes 1 | tf_op jit(solution)/shard_map/attention_forward/pallas_call | solution.py:288
  88.0 10.5 %collective-permute-done.9.refs_5_.refs_7_ = bf16[256,2048]{1,0:T(8,128)(2,1)S(1)} collective-permute-done((bf16[256,2048]{1,0:T(8,128)(2,1)}, bf16[256,2048]{1,0:T(8,128)(2,1)S(1)}, u32[]{:S(2)}, u32[]{:S(2)}) %collective-permute-start.9) | collective-permute-done | bytes 1048608 | tf_op jit(solution)/shard_map/ppermute | solution.py:561
  111.5 5.9 %collective-permute-done.16 = bf16[256,1024]{1,0:T(8,128)(2,1)S(1)} collective-permute-done((bf16[256,1024]{1,0:T(8,128)(2,1)S(1)}, bf16[256,1024]{1,0:T(8,128)(2,1)S(1)}, u32[]{:S(2)}, u32[]{:S(2)}) %collective-permute-start.16) | collective-permute-done | bytes 524320 | tf_op jit(solution)/shard_map/ppermute | solution.py:548
  119.6 20.3 %collective-permute-done.19.refs_9_.refs_11_ = bf16[256,2048]{1,0:T(8,128)(2,1)} collective-permute-done((bf16[256,2048]{1,0:T(8,128)(2,1)S(1)}, bf16[256,2048]{1,0:T(8,128)(2,1)}, u32[]{:S(2)}, u32[]{:S(2)}) %collective-permute-start.19) | collective-permute-done | bytes 1048608 | tf_op jit(solution)/shard_map/ppermute | solution.py:548
  151.9 11.9 %collective-permute-done.22.refs_6_.refs_8_ = bf16[256,2048]{1,0:T(8,128)(2,1)} collective-permute-done((bf16[256,2048]{1,0:T(8,128)(2,1)}, bf16[256,2048]{1,0:T(8,128)(2,1)}, u32[]{:S(2)}, u32[]{:S(2)}) %collective-permute-start.22) | collective-permute-done | bytes 1048608 | tf_op jit(solution)/shard_map/ppermute | solution.py:561
  170.2 10.1 %feed_forward.3 = (f32[256,1024]{1,0:T(8,128)}, bf16[256,1024]{1,0:T(8,128)(2,1)}) custom-call(bf16[256,1024]{1,0:T(8,128)(2,1)} %get-tuple-element.128.refs_0_.refs_1_, bf16[256,1024]{1,0:T(8,128)(2,1)} %get-tuple-element.246.refs_1_.refs_0_, f32[4,1,512]{2,1,0:T(1,128)} %reshape_squeeze.7.refs_2_, bf16[256,2048]{1,0:T(8,128)(2,1)} %fusion.29.refs_3_.refs_5_, ...), custom_call_target="tpu_custom_call" | custom-call | flops 1 | bytes 1 | tf_op jit(solution)/shard_map/feed_forward/pallas_call | solution.py:408
  180.3 8.3 %collective-permute-done.29 = bf16[256,1024]{1,0:T(8,128)(2,1)} collective-permute-done((bf16[256,1024]{1,0:T(8,128)(2,1)}, bf16[256,1024]{1,0:T(8,128)(2,1)}, u32[]{:S(2)}, u32[]{:S(2)}) %collective-permute-start.29) | collective-permute-done | bytes 524320 | tf_op jit(solution)/shard_map/ppermute | solution.py:548
  188.6 4.4 %collective-permute-start.30 = (bf16[256,1024]{1,0:T(8,128)(2,1)}, bf16[256,1024]{1,0:T(8,128)(2,1)S(1)}, u32[]{:S(2)}, u32[]{:S(2)}) collective-permute-start(bf16[256,1024]{1,0:T(8,128)(2,1)} %get-tuple-element.135), channel_id=1, source_target_pairs={{0,16},{16,0},{1,17},{17,1},{2,18},{18,2},{3,19},{19,3},{4,20},{20... | collective-permute-start | bytes 1572872 | tf_op jit(solution)/shard_map/ppermute | solution.py:540
  199.3 11.3 %collective-permute-done.31 = bf16[256,1024]{1,0:T(8,128)(2,1)S(1)} collective-permute-done((bf16[256,1024]{1,0:T(8,128)(2,1)S(1)}, bf16[256,1024]{1,0:T(8,128)(2,1)S(1)}, u32[]{:S(2)}, u32[]{:S(2)}) %collective-permute-start.31) | collective-permute-done | bytes 524320 | tf_op jit(solution)/shard_map/ppermute | solution.py:548
  215.9 8.0 %attention_forward.3 = (bf16[512,256]{1,0:T(8,128)(2,1)S(1)}, bf16[512,256]{1,0:T(8,128)(2,1)S(1)}, f32[8,1024]{1,0:T(8,128)S(1)}) custom-call(s32[4]{0:T(128)S(1)} %pad_add_fusion.3.order_ref, bf16[512,768]{1,0:T(8,128)(2,1)S(1)} %add_convert_fusion.1.refs_0_, bf16[512,768]{1,0:T(8,128)(2,1)S(1)} %add_convert_fusion.refs_1_, ...), custom_call_target="tpu_custom_call" | custom-call | flops 1 | bytes 1 | tf_op jit(solution)/shard_map/attention_forward/pallas_call | solution.py:288
  225.2 5.3 %collective-permute-done.35 = bf16[512,256]{1,0:T(8,128)(2,1)S(1)} collective-permute-done((bf16[512,256]{1,0:T(8,128)(2,1)S(1)}, bf16[512,256]{1,0:T(8,128)(2,1)S(1)}, u32[]{:S(2)}, u32[]{:S(2)}) %collective-permute-start.35) | collective-permute-done | bytes 262176 | tf_op jit(solution)/shard_map/ppermute | solution.py:548
  241.2 15.6 %feed_forward.4 = (f32[256,1024]{1,0:T(8,128)}, bf16[256,1024]{1,0:T(8,128)(2,1)}, f32[256,1024]{1,0:T(8,128)}, bf16[256,1024]{1,0:T(8,128)(2,1)}) custom-call(bf16[256,1024]{1,0:T(8,128)(2,1)} %add_convert_fusion.7.refs_0_, bf16[256,1024]{1,0:T(8,128)(2,1)} %collective-permute-done.37.refs_1_, f32[4,1,512]{2,1,0:T(1,128)} %reshape_squeeze.8.refs_2_, ...), custom_call_target="tpu_custom_call" | custom-call | flops 1 | bytes 1 | tf_op jit(solution)/shard_map/feed_forward/pallas_call | solution.py:408
  267.8 5.8 %collective-permute-done.41.refs_3_ = bf16[512,256]{1,0:T(8,128)(2,1)S(1)} collective-permute-done((bf16[512,256]{1,0:T(8,128)(2,1)S(1)}, bf16[512,256]{1,0:T(8,128)(2,1)S(1)}, u32[]{:S(2)}, u32[]{:S(2)}) %collective-permute-start.41) | collective-permute-done | bytes 262176 | tf_op jit(solution)/shard_map/ppermute | solution.py:548
  273.6 12.1 %attention_backward.2 = (bf16[512,768]{1,0:T(8,128)(2,1)S(1)}, bf16[512,768]{1,0:T(8,128)(2,1)S(1)}, f32[2,16,256]{2,1,0:T(8,128)S(1)}) custom-call(s32[4]{0:T(128)S(1)} %pad_add_fusion.3.order_ref, bf16[512,768]{1,0:T(8,128)(2,1)S(1)} %add_convert_fusion.1.refs_0_, bf16[512,768]{1,0:T(8,128)(2,1)S(1)} %copy-done.2, ...), custom_call_target="tpu_custom_call" | custom-call | flops 1 | bytes 1 | tf_op jit(solution)/shard_map/attention_backward/pallas_call | solution.py:316
  292.8 10.9 %collective-permute-done.43 = bf16[256,1024]{1,0:T(8,128)(2,1)S(1)} collective-permute-done((bf16[256,1024]{1,0:T(8,128)(2,1)S(1)}, bf16[256,1024]{1,0:T(8,128)(2,1)S(1)}, u32[]{:S(2)}, u32[]{:S(2)}) %collective-permute-start.43) | collective-permute-done | bytes 524320 | tf_op jit(solution)/shard_map/ppermute | solution.py:548
  308.2 12.9 %feed_forward.5 = (f32[256,1024]{1,0:T(8,128)}, bf16[256,1024]{1,0:T(8,128)(2,1)}) custom-call(bf16[256,1024]{1,0:T(8,128)(2,1)} %get-tuple-element.246.refs_1_.refs_0_, bf16[256,1024]{1,0:T(8,128)(2,1)} %get-tuple-element.128.refs_0_.refs_1_, f32[4,1,512]{2,1,0:T(1,128)} %reshape_squeeze.7.refs_2_, bf16[256,1024]{1,0:T(8,128)(2,1)} %copy-done.28, ...), custom_call_target="tpu_custom_call" | custom-call | flops 1 | bytes 1 | tf_op jit(solution)/shard_map/feed_forward/pallas_call | solution.py:408
  331.1 5.5 %collective-permute-done.50.refs_3_ = bf16[512,256]{1,0:T(8,128)(2,1)S(1)} collective-permute-done((bf16[512,256]{1,0:T(8,128)(2,1)S(1)}, bf16[512,256]{1,0:T(8,128)(2,1)S(1)}, u32[]{:S(2)}, u32[]{:S(2)}) %collective-permute-start.50) | collective-permute-done | bytes 262176 | tf_op jit(solution)/shard_map/ppermute | solution.py:548
  336.6 12.1 %attention_backward.3 = (bf16[512,768]{1,0:T(8,128)(2,1)S(1)}, bf16[512,768]{1,0:T(8,128)(2,1)S(1)}, f32[2,16,256]{2,1,0:T(8,128)S(1)}) custom-call(s32[4]{0:T(128)S(1)} %pad_add_fusion.2.order_ref, bf16[512,768]{1,0:T(8,128)(2,1)S(1)} %add_convert_fusion.3.refs_0_, bf16[512,768]{1,0:T(8,128)(2,1)S(1)} %add_convert_fusion.2.refs_1_, ...), custom_call_target="tpu_custom_call" | custom-call | flops 1 | bytes 1 | tf_op jit(solution)/shard_map/attention_backward/pallas_call | solution.py:316
  359.7 6.2 %collective-permute-done.52 = bf16[256,1024]{1,0:T(8,128)(2,1)S(1)} collective-permute-done((bf16[256,1024]{1,0:T(8,128)(2,1)S(1)}, bf16[256,1024]{1,0:T(8,128)(2,1)S(1)}, u32[]{:S(2)}, u32[]{:S(2)}) %collective-permute-start.52) | collective-permute-done | bytes 524320 | tf_op jit(solution)/shard_map/ppermute | solution.py:548
  376.0 4.8 %collective-permute-done.60 = f32[16,512]{1,0:T(8,128)S(1)} collective-permute-done((f32[16,512]{1,0:T(8,128)S(1)}, f32[16,512]{1,0:T(8,128)S(1)}, u32[]{:S(2)}, u32[]{:S(2)}) %collective-permute-start.60) | collective-permute-done | bytes 32800 | tf_op jit(solution)/shard_map/ppermute | solution.py:590
  (395 shorter events, 160.0 us)
Async XLA Ops:
  21.8 26.1 %collective-permute-start.4 = (bf16[256,2048]{1,0:T(8,128)(2,1)}, bf16[256,2048]{1,0:T(8,128)(2,1)}, u32[]{:S(2)}, u32[]{:S(2)}) collective-permute-start(bf16[256,2048]{1,0:T(8,128)(2,1)} %fusion.29.refs_3_.refs_5_), channel_id=1, source_target_pairs={{0,1},{1,0},{2,3},{3,2},{4,5},{5,4},{6,7},{7,6},{8,9},{9,8},{10,11... | collective-permute-start | bytes 3145736 | tf_op jit(solution)/shard_map/ppermute | solution.py:548
  24.2 28.7 %collective-permute-start.6 = (bf16[2,1024]{1,0:T(2,128)(2,1)S(1)}, bf16[2,1024]{1,0:T(2,128)(2,1)S(1)}, u32[]{:S(2)}, u32[]{:S(2)}) collective-permute-start(bf16[2,1024]{1,0:T(2,128)(2,1)S(1)} %bitcast.147), channel_id=1, source_target_pairs={{0,1},{1,0},{2,3},{3,2},{4,5},{5,4},{6,7},{7,6},{8,9},{9,8},{10,11... | collective-permute-start | bytes 12296 | tf_op jit(solution)/shard_map/ppermute | solution.py:548
  24.3 28.7 %collective-permute-start.7 = (bf16[256,1024]{1,0:T(8,128)(2,1)}, bf16[256,1024]{1,0:T(8,128)(2,1)}, u32[]{:S(2)}, u32[]{:S(2)}) collective-permute-start(bf16[256,1024]{1,0:T(8,128)(2,1)} %bitcast.2), channel_id=1, source_target_pairs={{0,18},{1,19},{2,16},{3,17},{4,22},{5,23},{6,20},{7,21},{8,26},{9,... | collective-permute-start | bytes 1572872 | tf_op jit(solution)/shard_map/ppermute | solution.py:574
  26.0 42.8 %collective-permute-start.2 = (bf16[1024,768]{0,1:T(8,128)(2,1)S(1)}, bf16[1024,768]{0,1:T(8,128)(2,1)}, u32[]{:S(2)}, u32[]{:S(2)}) collective-permute-start(bf16[1024,768]{0,1:T(8,128)(2,1)S(1)} %bitcast.112), channel_id=1, source_target_pairs={{0,18},{1,19},{2,16},{3,17},{16,2},{17,3},{18,0},{19,1},{4,22},{5,... | collective-permute-start | bytes 4718600 | tf_op jit(solution)/shard_map/ppermute | solution.py:557
  73.9 24.6 %collective-permute-start.9 = (bf16[256,2048]{1,0:T(8,128)(2,1)}, bf16[256,2048]{1,0:T(8,128)(2,1)S(1)}, u32[]{:S(2)}, u32[]{:S(2)}) collective-permute-start(bf16[256,2048]{1,0:T(8,128)(2,1)} %fusion.29.refs_3_.refs_5_), channel_id=1, source_target_pairs={{0,2},{1,3},{2,0},{3,1},{4,6},{5,7},{6,4},{7,5},{8,10},{9,11},{10,... | collective-permute-start | bytes 3145736 | tf_op jit(solution)/shard_map/ppermute | solution.py:561
  74.0 24.5 %collective-permute-start.10 = (bf16[256,2048]{1,0:T(8,128)(2,1)S(1)}, bf16[256,2048]{1,0:T(8,128)(2,1)S(1)}, u32[]{:S(2)}, u32[]{:S(2)}) collective-permute-start(bf16[256,2048]{1,0:T(8,128)(2,1)S(1)} %get-tuple-element.121.refs_5_), channel_id=1, source_target_pairs={{0,1},{1,0},{2,3},{3,2},{4,5},{5,4},{6,7},{7,6},{8,9},{9,8},{10,11... | collective-permute-start | bytes 3145736 | tf_op jit(solution)/shard_map/ppermute | solution.py:548
  75.4 23.9 %collective-permute-start.11 = (bf16[256,2048]{1,0:T(8,128)(2,1)}, bf16[256,2048]{1,0:T(8,128)(2,1)S(1)}, u32[]{:S(2)}, u32[]{:S(2)}) collective-permute-start(bf16[256,2048]{1,0:T(8,128)(2,1)} %collective-permute-done.4.refs_7_.refs_9_), channel_id=1, source_target_pairs={{0,4},{4,0},{8,12},{12,8},{1,5},{5,1},{9,13},{13,9},{2,6},{6,2},{1... | collective-permute-start | bytes 3145736 | tf_op jit(solution)/shard_map/ppermute | solution.py:566
  103.9 13.5 %collective-permute-start.16 = (bf16[256,1024]{1,0:T(8,128)(2,1)S(1)}, bf16[256,1024]{1,0:T(8,128)(2,1)S(1)}, u32[]{:S(2)}, u32[]{:S(2)}) collective-permute-start(bf16[256,1024]{1,0:T(8,128)(2,1)S(1)} %add_convert_fusion.11), channel_id=1, source_target_pairs={{0,1},{1,0},{2,3},{3,2},{4,5},{5,4},{6,7},{7,6},{8,9},{9,8},{10,11... | collective-permute-start | bytes 1572872 | tf_op jit(solution)/shard_map/ppermute | solution.py:548
  104.0 35.9 %collective-permute-start.19 = (bf16[256,2048]{1,0:T(8,128)(2,1)S(1)}, bf16[256,2048]{1,0:T(8,128)(2,1)}, u32[]{:S(2)}, u32[]{:S(2)}) collective-permute-start(bf16[256,2048]{1,0:T(8,128)(2,1)S(1)} %collective-permute-done.9.refs_5_.refs_7_), channel_id=1, source_target_pairs={{0,1},{1,0},{2,3},{3,2},{4,5},{5,4},{6,7},{7,6},{8,9},{9,8},{10,11... | collective-permute-start | bytes 3145736 | tf_op jit(solution)/shard_map/ppermute | solution.py:548
  105.4 34.5 %collective-permute-start.20 = (bf16[256,2048]{1,0:T(8,128)(2,1)S(1)}, bf16[256,2048]{1,0:T(8,128)(2,1)}, u32[]{:S(2)}, u32[]{:S(2)}) collective-permute-start(bf16[256,2048]{1,0:T(8,128)(2,1)S(1)} %get-tuple-element.121.refs_5_), channel_id=1, source_target_pairs={{0,2},{1,3},{2,0},{3,1},{4,6},{5,7},{6,4},{7,5},{8,10},{9,11},{10,... | collective-permute-start | bytes 3145736 | tf_op jit(solution)/shard_map/ppermute | solution.py:561
  106.6 34.2 %collective-permute-start.12 = (bf16[512,1024]{1,0:T(8,128)(2,1)S(1)}, bf16[512,1024]{1,0:T(8,128)(2,1)S(1)}, u32[]{:S(2)}, u32[]{:S(2)}) collective-permute-start(bf16[512,1024]{1,0:T(8,128)(2,1)S(1)} %pad_maximum_fusion), channel_id=1, source_target_pairs={{16,2},{17,3},{18,0},{19,1},{20,6},{21,7},{22,4},{23,5},{24,10},{2... | collective-permute-start | bytes 3145736 | tf_op jit(solution)/shard_map/ppermute | solution.py:574
  110.1 30.7 %collective-permute-start.21 = (bf16[256,2048]{1,0:T(8,128)(2,1)S(1)}, bf16[256,2048]{1,0:T(8,128)(2,1)S(1)}, u32[]{:S(2)}, u32[]{:S(2)}) collective-permute-start(bf16[256,2048]{1,0:T(8,128)(2,1)S(1)} %collective-permute-done.10.refs_9_), channel_id=1, source_target_pairs={{0,4},{4,0},{8,12},{12,8},{1,5},{5,1},{9,13},{13,9},{2,6},{6,2},{1... | collective-permute-start | bytes 3145736 | tf_op jit(solution)/shard_map/ppermute | solution.py:566
  117.8 28.3 %collective-permute-start.18 = (f32[256,1024]{1,0:T(8,128)S(1)}, f32[256,1024]{1,0:T(8,128)}, u32[]{:S(2)}, u32[]{:S(2)}) collective-permute-start(f32[256,1024]{1,0:T(8,128)S(1)} %get-tuple-element.205), channel_id=1, source_target_pairs={{0,16},{16,0},{1,17},{17,1},{2,18},{18,2},{3,19},{19,3},{4,20},{20... | collective-permute-start | bytes 3145736 | tf_op jit(solution)/shard_map/ppermute | solution.py:540
  141.2 22.6 %collective-permute-start.22 = (bf16[256,2048]{1,0:T(8,128)(2,1)}, bf16[256,2048]{1,0:T(8,128)(2,1)}, u32[]{:S(2)}, u32[]{:S(2)}) collective-permute-start(bf16[256,2048]{1,0:T(8,128)(2,1)} %get-tuple-element.123.refs_4_.refs_6_), channel_id=1, source_target_pairs={{0,2},{1,3},{2,0},{3,1},{4,6},{5,7},{6,4},{7,5},{8,10},{9,11},{10,... | collective-permute-start | bytes 3145736 | tf_op jit(solution)/shard_map/ppermute | solution.py:561
  142.3 23.1 %collective-permute-start.23 = (bf16[256,2048]{1,0:T(8,128)(2,1)}, bf16[256,2048]{1,0:T(8,128)(2,1)}, u32[]{:S(2)}, u32[]{:S(2)}) collective-permute-start(bf16[256,2048]{1,0:T(8,128)(2,1)} %collective-permute-done.19.refs_9_.refs_11_), channel_id=1, source_target_pairs={{0,4},{4,0},{8,12},{12,8},{1,5},{5,1},{9,13},{13,9},{2,6},{6,2},{1... | collective-permute-start | bytes 3145736 | tf_op jit(solution)/shard_map/ppermute | solution.py:566
  143.6 22.8 %collective-permute-start.24 = (bf16[256,2048]{1,0:T(8,128)(2,1)}, bf16[256,2048]{1,0:T(8,128)(2,1)}, u32[]{:S(2)}, u32[]{:S(2)}) collective-permute-start(bf16[256,2048]{1,0:T(8,128)(2,1)} %collective-permute-done.20.refs_7_), channel_id=1, source_target_pairs={{0,1},{1,0},{2,3},{3,2},{4,5},{5,4},{6,7},{7,6},{8,9},{9,8},{10,11... | collective-permute-start | bytes 3145736 | tf_op jit(solution)/shard_map/ppermute | solution.py:548
  166.4 22.3 %collective-permute-start.26 = (bf16[256,2048]{1,0:T(8,128)(2,1)}, bf16[256,2048]{1,0:T(8,128)(2,1)}, u32[]{:S(2)}, u32[]{:S(2)}) collective-permute-start(bf16[256,2048]{1,0:T(8,128)(2,1)} %get-tuple-element.131.refs_6_), channel_id=1, source_target_pairs={{0,2},{1,3},{2,0},{3,1},{4,6},{5,7},{6,4},{7,5},{8,10},{9,11},{10,... | collective-permute-start | bytes 3145736 | tf_op jit(solution)/shard_map/ppermute | solution.py:561
  166.4 22.3 %collective-permute-start.27 = (bf16[256,2048]{1,0:T(8,128)(2,1)}, bf16[256,2048]{1,0:T(8,128)(2,1)}, u32[]{:S(2)}, u32[]{:S(2)}) collective-permute-start(bf16[256,2048]{1,0:T(8,128)(2,1)} %collective-permute-done.24.refs_11_), channel_id=1, source_target_pairs={{0,4},{4,0},{8,12},{12,8},{1,5},{5,1},{9,13},{13,9},{2,6},{6,2},{1... | collective-permute-start | bytes 3145736 | tf_op jit(solution)/shard_map/ppermute | solution.py:566
  167.6 21.0 %collective-permute-start.29 = (bf16[256,1024]{1,0:T(8,128)(2,1)}, bf16[256,1024]{1,0:T(8,128)(2,1)}, u32[]{:S(2)}, u32[]{:S(2)}) collective-permute-start(bf16[256,1024]{1,0:T(8,128)(2,1)} %get-tuple-element.134), channel_id=1, source_target_pairs={{0,1},{1,0},{2,3},{3,2},{4,5},{5,4},{6,7},{7,6},{8,9},{9,8},{10,11... | collective-permute-start | bytes 1572872 | tf_op jit(solution)/shard_map/ppermute | solution.py:548
  197.4 13.2 %collective-permute-start.31 = (bf16[256,1024]{1,0:T(8,128)(2,1)S(1)}, bf16[256,1024]{1,0:T(8,128)(2,1)S(1)}, u32[]{:S(2)}, u32[]{:S(2)}) collective-permute-start(bf16[256,1024]{1,0:T(8,128)(2,1)S(1)} %fusion.13), channel_id=1, source_target_pairs={{0,1},{1,0},{2,3},{3,2},{4,5},{5,4},{6,7},{7,6},{8,9},{9,8},{10,11... | collective-permute-start | bytes 1572872 | tf_op jit(solution)/shard_map/ppermute | solution.py:548
  197.7 14.4 %collective-permute-start.33 = (bf16[512,512]{0,1:T(8,128)(2,1)S(1)}, bf16[512,512]{0,1:T(8,128)(2,1)S(1)}, u32[]{:S(2)}, u32[]{:S(2)}) collective-permute-start(bf16[512,512]{0,1:T(8,128)(2,1)S(1)} %bitcast.115), channel_id=1, source_target_pairs={{0,18},{1,19},{2,16},{3,17},{16,2},{17,3},{18,0},{19,1},{4,22},{5,... | collective-permute-start | bytes 1572872 | tf_op jit(solution)/shard_map/ppermute | solution.py:557
  290.3 13.4 %collective-permute-start.43 = (bf16[256,1024]{1,0:T(8,128)(2,1)S(1)}, bf16[256,1024]{1,0:T(8,128)(2,1)S(1)}, u32[]{:S(2)}, u32[]{:S(2)}) collective-permute-start(bf16[256,1024]{1,0:T(8,128)(2,1)S(1)} %add_convert_fusion.6), channel_id=1, source_target_pairs={{0,1},{1,0},{2,3},{3,2},{4,5},{5,4},{6,7},{7,6},{8,9},{9,8},{10,11... | collective-permute-start | bytes 1572872 | tf_op jit(solution)/shard_map/ppermute | solution.py:548
  291.5 13.3 %collective-permute-start.46 = (bf16[256,1024]{1,0:T(8,128)(2,1)S(1)}, bf16[256,1024]{1,0:T(8,128)(2,1)S(1)}, u32[]{:S(2)}, u32[]{:S(2)}) collective-permute-start(bf16[256,1024]{1,0:T(8,128)(2,1)S(1)} %get-tuple-element.211.high_own), channel_id=1, source_target_pairs={{0,18},{1,19},{2,16},{3,17},{4,22},{5,23},{6,20},{7,21},{8,26},{9,... | collective-permute-start | bytes 1572872 | tf_op jit(solution)/shard_map/ppermute | solution.py:574
  369.2 15.2 %collective-permute-start.54 = (bf16[256,1024]{1,0:T(8,128)(2,1)S(1)}, bf16[256,1024]{1,0:T(8,128)(2,1)S(1)}, u32[]{:S(2)}, u32[]{:S(2)}) collective-permute-start(bf16[256,1024]{1,0:T(8,128)(2,1)S(1)} %fusion.26.low_own), channel_id=1, source_target_pairs={{16,2},{17,3},{18,0},{19,1},{20,6},{21,7},{22,4},{23,5},{24,10},{2... | collective-permute-start | bytes 1572872 | tf_op jit(solution)/shard_map/ppermute | solution.py:574
  (116 other events, 1208.4 us)
